TPU v7x, 32 devices: a whole 2x2x4 slice. The times are simulated.
32 devices in a mesh: pol: 4 (over y, x), slab: 8 (over z, core).
Axes of the slice: x: 2, y: 2, z: 4, core: 2. Of those that a mesh axis runs over, the one named last changes fastest.
Arguments:
- correlations: bfloat16 [2, 4, 512, 256], P(None, 'pol', 'slab'), may hold values from -6 to 6
- tracks: float32 [3, 512, 256], P(None, 'slab'), may hold values from -1 to 1
- vis_counts: int32 [512], P('slab'), may hold values from 1 to 256
- offsets: int32 [2, 512], replicated, may hold values from 0 to 4064, as said below
- held_counts: int32 [8], replicated, may hold values from 1 to 64, as said below
- pixel_weight: float32 [32, 32], replicated, may hold values from 0.25 to 1
Outputs:
- sky_image: float32 [2, 4, 4096, 4096], P(None, 'pol', 'slab')
Inputs may be any that keep to these rules, and one draw needn't show every extreme that they name: A holder's live slots are its first held_counts ones; one holder holds 64. offsets[0, b] // 512 == b // 64: a subgrid starts in the row slab of its holder.
All inputs are finite; a program needn't handle non-finite values.
Results may differ from a plain program's by a relative error of at most 0.0039.
Values may be sent and summed in bfloat16 or wider, within the bound.
No kernel may reach another device: no remote copies, remote signals or barrier semaphores. Data moves between devices by JAX's collectives and lax.ppermute only.
A program may use at most 128 MiB of HBM per device.

v0:
```python
import math

import jax
import jax.numpy as jnp
import numpy as np
from jax import lax
from jax.sharding import PartitionSpec as P

G = 4096
SUB = 32
VIS = 256
SLOTS = 64


TWO_PI = 2.0 * math.pi
FIELD_VIEW = 0.6
DEPTH_SCALE = 40.0
TRACK_SCALE = 0.375
COEF_REAL = np.array(
    [[0.5, 0.0, 0.0, 0.5], [0.5, 0.0, 0.0, -0.5], [0.0, 0.5, 0.5, 0.0], [0.0, 0.0, 0.0, 0.0]],
    np.float32,
)
COEF_IMAG = np.array(
    [[0.0, 0.0, 0.0, 0.0], [0.0, 0.0, 0.0, 0.0], [0.0, 0.0, 0.0, 0.0], [0.0, -0.5, 0.5, 0.0]],
    np.float32,
)


def partner_2(value, axis, distance):
    return lax.ppermute(value, axis, [(i, i ^ 1 << distance) for i in range(lax.axis_size(axis))])


def passed_along(value, axis, by):
    peers = lax.axis_size(axis)
    pairs = [(i, i + by) for i in range(peers) if 0 <= i + by < peers]
    return lax.ppermute(value, axis, pairs)


def pixel_tables():
    cells = jnp.arange(SUB * SUB, dtype=jnp.int32)
    row_pos = (cells // SUB - SUB // 2).astype(jnp.float32) / SUB
    col_pos = (cells % SUB - SUB // 2).astype(jnp.float32) / SUB
    depth = jnp.sqrt(1.0 - (FIELD_VIEW * col_pos) ** 2 - (FIELD_VIEW * row_pos) ** 2) - 1.0
    return (col_pos, row_pos, depth)


def phasor_table(track_set, tables):
    col_pos, row_pos, depth = tables
    u_cells = track_set[0] * (TRACK_SCALE * SUB)
    v_cells = track_set[1] * (TRACK_SCALE * SUB)
    w_cells = track_set[2] * DEPTH_SCALE
    phase = TWO_PI * (
        u_cells[:, None] * col_pos[None, :]
        + v_cells[:, None] * row_pos[None, :]
        + w_cells[:, None] * depth[None, :]
    )
    return jnp.concatenate([jnp.cos(phase), jnp.sin(phase)], axis=1).astype(jnp.bfloat16)


def subgrid_tables():
    positions = jnp.arange(SUB, dtype=jnp.int32) - SUB // 2
    turn_count = positions[:, None] * positions[None, :] % SUB
    angles = -TWO_PI * turn_count.astype(jnp.float32) / SUB
    return (jnp.cos(angles), jnp.sin(angles))


def dft_table(length):
    positions = jnp.arange(length, dtype=jnp.int32)
    turn_count = positions[:, None] * positions[None, :] % length
    angles = TWO_PI * turn_count.astype(jnp.float32) / length
    return (jnp.cos(angles), jnp.sin(angles))


def twiddle_table(first_len, second_len, length):
    first_pos = jnp.arange(first_len, dtype=jnp.int32)
    second_pos = jnp.arange(second_len, dtype=jnp.int32)
    turn_count = first_pos[:, None] * second_pos[None, :] % length
    angles = TWO_PI * turn_count.astype(jnp.float32) / length
    return (jnp.cos(angles), jnp.sin(angles))


def complex_einsum(pattern, left_pair, right_pair):
    highest = lax.Precision.HIGHEST
    left_re, left_im = left_pair
    right_re, right_im = right_pair
    real_part = jnp.einsum(pattern, left_re, right_re, precision=highest) - jnp.einsum(
        pattern, left_im, right_im, precision=highest
    )
    imag_part = jnp.einsum(pattern, left_re, right_im, precision=highest) + jnp.einsum(
        pattern, left_im, right_re, precision=highest
    )
    return (real_part, imag_part)


def complex_multiply(data_pair, table_pair):
    data_re, data_im = data_pair
    table_re, table_im = table_pair
    return (data_re * table_re - data_im * table_im, data_re * table_im + data_im * table_re)


def subgrid_transform(sub_re, sub_im, dft_pair):
    half_re, half_im = complex_einsum("...ij,cj->...ic", (sub_re, sub_im), dft_pair)
    return complex_einsum("ai,...ic->...ac", dft_pair, (half_re, half_im))


def place_blocks(window, blocks, row_starts, col_starts):
    block_count = blocks.shape[1]
    zero_index = jnp.zeros((), jnp.int32)

    def add_one(slot_index, current_window):
        block = lax.dynamic_index_in_dim(blocks, slot_index, 1, keepdims=False)
        corner = (zero_index, row_starts[slot_index], col_starts[slot_index])
        current = lax.dynamic_slice(current_window, corner, (2, SUB, SUB))
        return lax.dynamic_update_slice(current_window, current + block, corner)

    return lax.fori_loop(0, block_count, add_one, window)


def on_device(correlations, tracks, vis_counts, offsets, held_counts, pixel_weight):
    highest = lax.Precision.HIGHEST
    slab_count = lax.axis_size("slab")
    slab_index = lax.axis_index("slab")
    stokes_index = lax.axis_index("pol")
    pixel_area = SUB * SUB
    rows_local = G // slab_count
    tables = pixel_tables()
    dft_pair = subgrid_tables()
    gathered = lax.all_gather(correlations, "pol", axis=1, tiled=True)
    corr_float = gathered.astype(jnp.float32)
    select = (jnp.arange(4, dtype=jnp.int32) == stokes_index).astype(jnp.float32)
    coef_re = jnp.sum(select[:, None] * jnp.asarray(COEF_REAL), axis=0)
    coef_im = jnp.sum(select[:, None] * jnp.asarray(COEF_IMAG), axis=0)
    stokes_re = jnp.einsum("p,pnv->nv", coef_re, corr_float[0], precision=highest) - jnp.einsum(
        "p,pnv->nv", coef_im, corr_float[1], precision=highest
    )
    stokes_im = jnp.einsum("p,pnv->nv", coef_re, corr_float[1], precision=highest) + jnp.einsum(
        "p,pnv->nv", coef_im, corr_float[0], precision=highest
    )
    visible = (jnp.arange(VIS, dtype=jnp.int32)[None, :] < vis_counts[:, None]).astype(jnp.bfloat16)
    stokes_vis = jnp.stack([stokes_re, stokes_im]).astype(jnp.bfloat16) * visible[None]
    holder_ids = jnp.arange(slab_count, dtype=jnp.int32)
    own_held = jnp.sum(jnp.where(holder_ids == slab_index, held_counts, 0))

    def grid_range(vis_set, track_set, first_slot, stop_slot, capacity):

        def one_slot(slot_index, subgrid_set):
            phasor = phasor_table(
                lax.dynamic_index_in_dim(track_set, slot_index, 1, keepdims=False), tables
            )
            vis_slot = lax.dynamic_index_in_dim(vis_set, slot_index, 1, keepdims=False)
            product = jnp.dot(vis_slot, phasor, preferred_element_type=jnp.float32)
            sub_re = product[0, :pixel_area] - product[1, pixel_area:]
            sub_im = product[0, pixel_area:] + product[1, :pixel_area]
            update = jnp.stack([sub_re, sub_im])[:, None, :]
            return lax.dynamic_update_slice_in_dim(subgrid_set, update, slot_index, 1)

        zero_set = jnp.zeros((2, capacity, pixel_area), jnp.float32)
        return lax.fori_loop(first_slot, stop_slot, one_slot, zero_set)

    half_slots = SLOTS // 2
    swap_bit = slab_count.bit_length() - 2
    partner = jnp.bitwise_xor(slab_index, slab_count // 2)
    partner_held = jnp.sum(jnp.where(holder_ids == partner, held_counts, 0))
    pair_total = own_held + partner_held
    own_give = jnp.maximum(own_held - (pair_total + 1) // 2, 0)
    partner_give = jnp.maximum(partner_held - (pair_total + 1) // 2, 0)
    own_start = jnp.minimum(own_held - own_give, SLOTS - half_slots)
    partner_start = jnp.minimum(partner_held - partner_give, SLOTS - half_slots)
    send_vis = lax.dynamic_slice_in_dim(stokes_vis, own_start, half_slots, 1).astype(jnp.float32)
    send_track = lax.dynamic_slice_in_dim(tracks, own_start, half_slots, 1)
    got_vis, got_track = partner_2((send_vis, send_track), "slab", swap_bit)
    first_slot = partner_held - partner_give - partner_start
    helped = grid_range(
        got_vis.astype(jnp.bfloat16), got_track, first_slot, first_slot + partner_give, half_slots
    )
    returned_set = partner_2(helped, "slab", swap_bit)
    own_part = grid_range(stokes_vis, tracks, 0, own_held - own_give, SLOTS)
    subgrids = own_part + lax.dynamic_update_slice_in_dim(
        jnp.zeros_like(own_part), returned_set, own_start, 1
    )
    weight_flat = pixel_weight.reshape(pixel_area)
    sub_re = (subgrids[0] * weight_flat).reshape(SLOTS, SUB, SUB)
    sub_im = (subgrids[1] * weight_flat).reshape(SLOTS, SUB, SUB)
    uv_re, uv_im = subgrid_transform(sub_re, sub_im, dft_pair)
    uv_blocks = jnp.stack([uv_re, uv_im])
    own_offsets = lax.dynamic_slice_in_dim(offsets, slab_index * SLOTS, SLOTS, 1)
    own_rows = own_offsets[0] - slab_index * rows_local
    own_cols = own_offsets[1]
    window = jnp.zeros((2, rows_local + SUB, G), jnp.float32)
    window = place_blocks(window, uv_blocks, own_rows, own_cols)
    lower_rows = passed_along(window[:, rows_local:], "slab", 1)
    slab_grid = window[:, :rows_local].at[:, :SUB].add(lower_rows)
    small_side = G // 128
    large_side = 128
    table_small = dft_table(small_side)
    table_large = dft_table(large_side)
    twiddle = twiddle_table(small_side, large_side, G)
    plane_re = slab_grid[0].reshape(rows_local, small_side, large_side)
    plane_im = slab_grid[1].reshape(rows_local, small_side, large_side)
    step_re, step_im = complex_einsum("rkc,kx->rxc", (plane_re, plane_im), table_small)
    step_re, step_im = complex_multiply((step_re, step_im), twiddle)
    step_re, step_im = complex_einsum("rxc,cb->bxr", (step_re, step_im), table_large)
    moved_block = lax.all_to_all(
        jnp.stack([step_re, step_im]), "slab", split_axis=1, concat_axis=3, tiled=True
    )
    line_re = moved_block[0].reshape(rows_local, large_side, small_side)
    line_im = moved_block[1].reshape(rows_local, large_side, small_side)
    line_re, line_im = complex_einsum("xab,ay->xby", (line_re, line_im), table_large)
    line_re, line_im = complex_multiply((line_re, line_im), twiddle)
    line_re, line_im = complex_einsum("xby,bz->xzy", (line_re, line_im), table_small)
    norm_scale = 1.0 / (SUB * SUB * math.sqrt(VIS * SLOTS * slab_count / 8.0))
    sky_re = line_re.reshape(rows_local, G) * norm_scale
    sky_im = line_im.reshape(rows_local, G) * norm_scale
    return jnp.stack([sky_re, sky_im])[:, None]


def solution(mesh):
    in_specs = (P(None, "pol", "slab", None), P(None, "slab", None), P("slab"), P(), P(), P())
    out_specs = P(None, "pol", "slab", None)
    return jax.shard_map(
        on_device, mesh=mesh, in_specs=in_specs, out_specs=out_specs, check_vma=False
    )
```

profile of v0, /device:TPU:0, one launch (start us, length us, event | category | flops | bytes accessed | tf_op | source)
XLA Modules:
  0.0 1716.5 jit_solution(8754197887101331359)
XLA Ops:
  4.8 4.1 collective-permute-start.1
  8.9 9.3 all_gather.3
  21.9 5.5 while.41
  22.7 4.4 cosine_convert_fusion.4
  29.1 8.2 collective-permute-start.2
  37.6 4.0 collective-permute-done.2
  42.3 6.2 add.274
  57.8 8.4 broadcast_in_dim.15
  66.2 573.0 %while.40 = (s32[]{:T(128)}, f32[2,544,4096]{2,1,0:T(8,128)}, s32[64]{0:T(128)S(1)}, s32[64]{0:T(128)S(1)}, f32[2,64,32,32]{3,2,0,1:T(8,128)S(1)}, /*index=5*/s32[]{:T(128)}, s32[]{:T(128)}, s32[]{:T(128)}, s32[]{:T(128)}) while((s32[]{:T(128)}, f32[2,544,4096]{2,1,0:T(8,128)}, s32[64]{0:T(128)S(1)}, s32[64]{0:T(128)S(1)}, ...), condition=%wide.region_9.10_spmd, body=%wide.region_8.9_spmd.sunk | while | flops 2056 | bytes 41169 | solution.py:116
  107.8 3.1 dynamic_update_slice.24
  179.6 3.1 dynamic_update_slice.24
  188.5 3.1 dynamic_update_slice.24
  313.4 3.1 dynamic_update_slice.24
  331.3 3.1 dynamic_update_slice.24
  403.0 3.1 dynamic_update_slice.24
  412.0 3.1 dynamic_update_slice.24
  510.6 3.1 dynamic_update_slice.24
  582.3 3.1 dynamic_update_slice.24
  640.5 170.5 %collective-permute-start.3 = (f32[2,32,4096]{2,1,0:T(8,128)S(1)}, f32[2,32,4096]{2,1,0:T(8,128)S(1)}, u32[]{:S(2)}, u32[]{:S(2)}) collective-permute-start(f32[2,32,4096]{2,1,0:T(8,128)S(1)} %slice.121), channel_id=1, source_target_pairs={{0,1},{1,2},{2,3},{3,4},{4,5},{5,6},{6,7},{8,9},{9,10},{10,11},{11... | collective-permute-start | bytes 3145736 | tf_op jit(solution)/shard_map/ppermute | solution.py:36
  811.1 6.7 slice.119
  819.2 6.5 slice_bitcast_fusion
  825.7 5.2 copy.205
  830.9 9.4 fusion.161
  840.3 9.6 fusion.148
  851.9 9.5 fusion.146
  861.4 19.0 %subtract_bitcast_fusion.1 = (f32[512,32,128]{2,1,0:T(8,128)}, f32[512,32,128]{2,1,0:T(8,128)}) fusion(f32[32,128]{1,0:T(8,128)S(1)} %get-tuple-element.353, f32[32,128]{1,0:T(8,128)S(1)} %get-tuple-element.354, f32[32,512,128]{2,0,1:T(8,128)} %fusion.146, f32[32,512,128]{2,0,1:T(8,128)} %fusion.161, f32[32,512,128]{2,0,1:T(8,128)} %fusion.148, ...), kind=kOutput, calls=%fused_computation.98 | convolution fusion | flops 822097920 | bytes 50364416 | tf_op jit(solution)/shard_map/rkc,kx->rxc/dot_general | solution.py:86
  880.3 23.5 %fusion.63 = f32[128,512,32]{1,0,2:T(8,128)S(1)} fusion(f32[512,32,128]{2,1,0:T(8,128)} %get-tuple-element.340), kind=kOutput, calls=%fused_computation.99 | convolution fusion | flops 3221454848 | bytes 16777216 | tf_op jit(solution)/shard_map/rxc,cb->bxr/dot_general | solution.py:89
  903.9 14.1 fusion.65
  918.0 17.2 %subtract_bitcast_fusion = f32[1,128,32,512]{3,1,2,0:T(8,128)} fusion(f32[128,512,32]{1,0,2:T(8,128)} %fusion.65, f32[512,32,128]{2,1,0:T(8,128)S(1)} %bitcast.219), kind=kOutput, calls=%fused_computation.96 | convolution fusion | flops 3223552000 | bytes 25165824 | tf_op jit(solution)/shard_map/rxc,cb->bxr/dot_general | solution.py:86
  935.2 14.2 add_bitcast_fusion
  949.4 7.3 pad_maximum_fusion
  956.8 16.6 copy.160
  973.3 375.1 %all_to_all.15 = f32[2,128,32,512]{3,2,0,1:T(8,128)S(1)} all-to-all(f32[2,128,32,512]{3,2,0,1:T(8,128)S(1)} %copy.160), channel_id=1, replica_groups=mesh['pol'=4,'slab'=8] {'slab'}, dimensions={1} | all-to-all | bytes 33554432 | tf_op jit(solution)/shard_map/all_to_all | solution.py:203
  1348.5 10.4 copy.247
  1358.9 6.9 fusion.295
  1365.8 20.9 %reshape_squeeze.15 = f32[512,128,32]{2,1,0:T(8,128)} reshape(f32[1,16,32,8,512]{4,3,2,1,0:T(8,128)} %get-tuple-element.341) | data formatting | bytes 16777216 | tf_op jit(solution)/shard_map/reshape;squeeze | solution.py:207
  1386.7 57.7 %fusion.112 = f32[512,32,128]{2,1,0:T(8,128)} fusion(f32[512,128,32]{2,1,0:T(8,128)} %reshape_squeeze.15), kind=kOutput, calls=%fused_computation.159 | convolution fusion | flops 3221454848 | bytes 16777216 | tf_op jit(solution)/shard_map/xab,ay->xby/dot_general | solution.py:89
  1444.4 58.0 %fusion.106 = f32[512,32,128]{2,1,0:T(8,128)} fusion(f32[512,128,32]{2,1,0:T(8,128)} %reshape_squeeze.15), kind=kOutput, calls=%fused_computation.151 | convolution fusion | flops 3221454848 | bytes 16777216 | tf_op jit(solution)/shard_map/xab,ay->xby/dot_general | solution.py:86
  1502.4 20.9 %reshape_squeeze.14 = f32[512,128,32]{2,1,0:T(8,128)} reshape(f32[1,16,32,8,512]{4,3,2,1,0:T(8,128)} %get-tuple-element.342) | data formatting | bytes 16777216 | tf_op jit(solution)/shard_map/reshape;squeeze | solution.py:206
  1523.2 57.7 %fusion.114 = f32[512,32,128]{2,1,0:T(8,128)} fusion(f32[512,128,32]{2,1,0:T(8,128)} %reshape_squeeze.14), kind=kOutput, calls=%fused_computation.161 | convolution fusion | flops 3221454848 | bytes 16777216 | tf_op jit(solution)/shard_map/xab,ay->xby/dot_general | solution.py:86
  1580.9 62.4 %multiply_add_fusion = (f32[512,32,128]{2,1,0:T(8,128)}, f32[512,32,128]{2,1,0:T(8,128)}) fusion(f32[32,128]{1,0:T(8,128)S(1)} %get-tuple-element.353, f32[32,128]{1,0:T(8,128)S(1)} %get-tuple-element.354, f32[512,32,128]{2,1,0:T(8,128)} %fusion.112, f32[512,32,128]{2,1,0:T(8,128)} %fusion.114, f32[512,32,128]{2,1,0:T(8,128)} %fusion.106, ...), kind=kOutput, calls=%fused_computation.93 | convolution fusion | flops 3238232064 | bytes 50364416 | tf_op jit(solution)/shard_map/xab,ay->xby/dot_general | solution.py:89
  1643.4 10.9 fusion.143
  1654.3 9.6 fusion.159
  1663.9 11.4 multiply_bitcast_fusion.1
  1675.3 10.4 multiply_bitcast_fusion
  1685.7 9.4 mul.577
  1695.2 9.4 mul.574
  1704.5 11.8 maximum_bitcast_fusion.2
  (323 shorter events, 333.1 us)
Async XLA Ops:
  0.0 27.4 %copy-start = (s32[2,512]{1,0:T(2,128)S(1)}, s32[2,512]{1,0:T(2,128)}, u32[]{:S(2)}) copy-start(s32[2,512]{1,0:T(2,128)} %param.19) | copy-start | bytes 12292
  4.8 23.9 %collective-permute-start.1 = (f32[3,32,256]{2,1,0:T(8,128)S(1)}, f32[3,32,256]{2,1,0:T(8,128)S(1)}, u32[]{:S(2)}, u32[]{:S(2)}) collective-permute-start(f32[3,32,256]{2,1,0:T(8,128)S(1)} %constant_dynamic-slice_fusion.4), channel_id=1, source_target_pairs={{0,4},{1,5},{2,6},{3,7},{4,0},{5,1},{6,2},{7,3},{8,12},{9,13},{10,... | collective-permute-start | bytes 294920 | tf_op jit(solution)/shard_map/ppermute | solution.py:30
  21.2 7.4 collective-permute-start
  29.1 19.5 %copy-start.5 = (f32[32,32]{1,0:T(8,128)S(1)}, f32[32,32]{1,0:T(8,128)}, u32[]{:S(2)}) copy-start(f32[32,32]{1,0:T(8,128)} %param.21) | copy-start | bytes 12292
  29.1 12.5 collective-permute-start.2
  640.5 177.3 %collective-permute-start.3 = (f32[2,32,4096]{2,1,0:T(8,128)S(1)}, f32[2,32,4096]{2,1,0:T(8,128)S(1)}, u32[]{:S(2)}, u32[]{:S(2)}) collective-permute-start(f32[2,32,4096]{2,1,0:T(8,128)S(1)} %slice.121), channel_id=1, source_target_pairs={{0,1},{1,2},{2,3},{3,4},{4,5},{5,6},{6,7},{8,9},{9,10},{10,11},{11... | collective-permute-start | bytes 3145736 | tf_op jit(solution)/shard_map/ppermute | solution.py:36
  830.9 19.1 %slice-start.4 = ((s8[8388608]{0:T(1024)(128)(4,1)}), s8[4194304]{0:T(1024)(128)(4,1)S(1)}, s32[]{:S(2)}) async-start(s8[8388608]{0:T(1024)(128)(4,1)} %bitcast.226), calls=%async_computation.5 | async-start | bytes 8388608
  840.3 9.7 slice-start.5
  851.8 9.5 copy-start.3
  880.3 23.5 %copy-start.4 = (f32[512,32,128]{2,1,0:T(8,128)S(1)}, f32[512,32,128]{2,1,0:T(8,128)}, u32[]{:S(2)}) copy-start(f32[512,32,128]{2,1,0:T(8,128)} %get-tuple-element.340) | copy-start | bytes 25165828
  880.3 37.6 %slice-start.2 = ((s8[8388608]{0:T(1024)(128)(4,1)}), s8[4194304]{0:T(1024)(128)(4,1)S(1)}, s32[]{:S(2)}) async-start(s8[8388608]{0:T(1024)(128)(4,1)} %bitcast.218), calls=%async_computation.3 | async-start | bytes 8388608
  903.9 14.1 slice-start.3
  1643.3 10.9 copy-start.2
  1643.3 20.5 %slice-start = ((s8[8388608]{0:T(1024)(128)(4,1)}), s8[4194304]{0:T(1024)(128)(4,1)S(1)}, s32[]{:S(2)}) async-start(s8[8388608]{0:T(1024)(128)(4,1)} %bitcast.216), calls=%async_computation.1 | async-start | bytes 8388608
  1654.3 9.6 slice-start.1
  1704.5 11.8 copy-start.1
where the time goes:
time: 1750 us; the launch traced here: 1720 us
  local copies, waits for them, and re-layouts  410 us (23%)
  matrix products  404 us (23%)
  blocking collectives  384 us (22%)
  loops' own time  235 us (13%)
  starting transfers between devices  183 us (10%)
  other arithmetic  92.2 us (5%)
    all_to_all x1, blocking collectives, on_device(): lax.all_to_all(jnp.stack([step_re, step_im]), 'slab', split_axis=1, conca...  375 us
    another operation x1, loops' own time, place_blocks(): return lax.fori_loop(0, block_count, add_one, window)  234 us
    dynamic_update_slice x64, local copies, waits for them, and re-layouts, add_one(): return lax.dynamic_update_slice(current_window, current + block, corner)  197 us
    ppermute x1, starting transfers between devices, passed_along(): return lax.ppermute(value, axis, pairs)  170 us
    dot_general x6, matrix products, complex_einsum(): jnp.einsum(pattern, left_re, right_re, precision=highest)  105 us
    dot_general x6, matrix products, complex_einsum(): jnp.einsum(pattern, left_im, right_re, precision=highest)  103 us
    dot_general x6, matrix products, complex_einsum(): jnp.einsum(pattern, left_re, right_im, precision=highest)  98.9 us
    dot_general x6, matrix products, complex_einsum(): jnp.einsum(pattern, left_im, right_im, precision=highest)  94.9 us
  transfers between devices with their start and end apart: 4, of which 1 were waited for; matrix products, arithmetic and copies ran while one was open for 1% of the time, Pallas kernels for 0%

commit v1 on v0

--- a/solution.py
+++ b/solution.py
@@ -1,9 +1,12 @@
+import functools
 import math
 
 import jax
 import jax.numpy as jnp
 import numpy as np
 from jax import lax
+from jax.experimental import pallas as pl
+from jax.experimental.pallas import tpu as pltpu
 from jax.sharding import PartitionSpec as P
 
 G = 4096
@@ -214,9 +217,507 @@
     return jnp.stack([sky_re, sky_im])[:, None]
 
 
+LANES = 128
+GROUP = 8
+
+
+def turn_polynomials():
+    z = np.cos(np.linspace(0.0, np.pi, 4001)) * 0.125 + 0.125
+    r = np.sqrt(z)
+    sine = np.where(r > 0, np.sin(np.pi * r) / np.where(r > 0, r, 1.0), np.pi)
+    fits = []
+    for values in (sine, np.cos(np.pi * r)):
+        fit = np.polynomial.chebyshev.Chebyshev.fit(z, values, 5, domain=[0.0, 0.25])
+        fits.append([float(v) for v in fit.convert(kind=np.polynomial.Polynomial).coef])
+    return fits
+
+
+SINE_COEF, COSINE_COEF = turn_polynomials()
+
+
+def cos_sin_turns(turns):
+    rest = turns - jnp.floor(turns + 0.5)
+    square = rest * rest
+    sine = SINE_COEF[-1]
+    cosine = COSINE_COEF[-1]
+    for coef in SINE_COEF[-2::-1]:
+        sine = sine * square + coef
+    for coef in COSINE_COEF[-2::-1]:
+        cosine = cosine * square + coef
+    sine = sine * rest
+    double = sine + sine
+    return 1.0 - double * sine, double * cosine
+
+
+def times(left, right):
+    return (left[0] * right[0] - left[1] * right[1], left[0] * right[1] + left[1] * right[0])
+
+
+def plus(left, right):
+    return (left[0] + right[0], left[1] + right[1])
+
+
+def minus(left, right):
+    return (left[0] - right[0], left[1] - right[1])
+
+
+def quarter(value, sign):
+    if sign > 0:
+        return (-value[1], value[0])
+    return (value[1], -value[0])
+
+
+def dft_4(values, sign):
+    a, b, c, d = values
+    even_sum, even_diff = plus(a, c), minus(a, c)
+    odd_sum, odd_diff = plus(b, d), quarter(minus(b, d), sign)
+    return [plus(even_sum, odd_sum), plus(even_diff, odd_diff), minus(even_sum, odd_sum), minus(even_diff, odd_diff)]
+
+
+ROOT_HALF = math.sqrt(0.5)
+
+
+def dft_8(values, sign):
+    even = dft_4(values[0::2], sign)
+    odd = dft_4(values[1::2], sign)
+    a, b = odd[1]
+    odd[1] = ((a - b) * ROOT_HALF, (a + b) * ROOT_HALF) if sign > 0 else ((a + b) * ROOT_HALF, (b - a) * ROOT_HALF)
+    odd[2] = quarter(odd[2], sign)
+    a, b = odd[3]
+    odd[3] = ((-a - b) * ROOT_HALF, (a - b) * ROOT_HALF) if sign > 0 else ((b - a) * ROOT_HALF, (-a - b) * ROOT_HALF)
+    return [plus(e, o) for e, o in zip(even, odd)] + [minus(e, o) for e, o in zip(even, odd)]
+
+
+def pixel_rows():
+    row, col = np.divmod(np.arange(SUB * SUB), SUB)
+    l = ((col - SUB // 2) / SUB).astype(np.float32)
+    m = ((row - SUB // 2) / SUB).astype(np.float32)
+    view = np.float32(FIELD_VIEW)
+    n = (np.sqrt(np.float32(1.0) - (view * l) ** 2 - (view * m) ** 2) - np.float32(1.0)).astype(np.float32)
+    return np.stack([l, m, n, row.astype(np.float32)] + [np.zeros_like(l)] * 4).astype(np.float32)
+
+
+def row_twiddles():
+    angle = -2.0 * np.pi * np.arange(8)[:, None] * (np.arange(LANES)[None, :] // SUB) / SUB
+    return np.concatenate([np.cos(angle), np.sin(angle)], axis=0).astype(np.float32)
+
+
+def subgrid_kernel(
+    count_ref, pol_ref, source_ref, start_ref, slots_ref, table_ref, twiddle_ref, weight_ref, *refs
+):
+    out_refs, more_ref, held_ref = refs[:4], refs[4], refs[5]
+    held_ref[...] = jnp.zeros_like(held_ref)
+    pol = pol_ref[0]
+
+    def one_slot(index, carry):
+        values = slots_ref[source_ref[index]]
+        row_start = start_ref[index].astype(jnp.float32)
+
+        def corr(c, p):
+            return values[4 * c + p : 4 * c + p + 1]
+
+        stokes = [
+            0.5 * corr(0, 0) + 0.5 * corr(0, 3),
+            0.5 * corr(0, 0) - 0.5 * corr(0, 3),
+            0.5 * corr(0, 1) + 0.5 * corr(0, 2),
+            0.5 * corr(1, 1) - 0.5 * corr(1, 2),
+            0.5 * corr(1, 0) + 0.5 * corr(1, 3),
+            0.5 * corr(1, 0) - 0.5 * corr(1, 3),
+            0.5 * corr(1, 1) + 0.5 * corr(1, 2),
+            0.5 * corr(0, 2) - 0.5 * corr(0, 1),
+        ]
+        rows = []
+        for part in (stokes[:4], stokes[4:]):
+            for k in range(4):
+                row = part[k]
+                for other in range(1, 4):
+                    row = jnp.where(pol == other, part[k ^ other], row)
+                rows.append(row)
+        vis = jnp.concatenate(rows, axis=0).astype(jnp.bfloat16)
+        track = jnp.transpose(values[8:16])
+        shape = (VIS, LANES)
+        u = jnp.broadcast_to(track[:, 0:1] * (TRACK_SCALE * SUB), shape)
+        v = jnp.broadcast_to(track[:, 1:2] * (TRACK_SCALE * SUB), shape)
+        w = jnp.broadcast_to(track[:, 2:3] * DEPTH_SCALE, shape)
+        placed = []
+        for tile in range(SUB * SUB // LANES):
+            lanes = pl.ds(tile * LANES, LANES)
+            turns = u * table_ref[0:1, lanes] + v * table_ref[1:2, lanes] + w * table_ref[2:3, lanes]
+            cosine, sine = cos_sin_turns(turns)
+            phasor = jnp.concatenate([cosine.astype(jnp.bfloat16), sine.astype(jnp.bfloat16)], axis=1)
+            product = jnp.dot(vis, phasor, preferred_element_type=jnp.float32)
+            real = product[:4, :LANES] - product[4:, LANES:]
+            imag = product[:4, LANES:] + product[4:, :LANES]
+            weight = weight_ref[0:1, lanes]
+            pixel_row = table_ref[3:4, lanes]
+            turn = (row_start * (pixel_row - SUB // 2) + pixel_row * (SUB // 2)) * (1.0 / SUB)
+            turn_re, turn_im = cos_sin_turns(turn)
+            turn_re, turn_im = turn_re * weight, turn_im * weight
+            placed.append(times((real, imag), (turn_re, turn_im)))
+        for rho, value in enumerate(dft_8(placed, -1)):
+            if rho:
+                value = times(value, (twiddle_ref[rho : rho + 1], twiddle_ref[8 + rho : 9 + rho]))
+            held_ref[index, :, pl.ds(2 * rho * LANES, LANES)] = value[0]
+            held_ref[index, :, pl.ds((2 * rho + 1) * LANES, LANES)] = value[1]
+        return carry
+
+    lax.fori_loop(0, count_ref[0], one_slot, 0)
+    for k in range(4):
+        out_refs[k][...] = held_ref[:GROUP, k, :].astype(jnp.bfloat16)
+        more_ref[k] = held_ref[GROUP:, k, :].astype(jnp.bfloat16)
+
+
+def subgrids_of(count, pol, source, start, slots, weight_row):
+    capacity = source.shape[0]
+    smem = pl.BlockSpec(memory_space=pltpu.SMEM)
+    vmem = pl.BlockSpec(memory_space=pltpu.VMEM)
+    return pl.pallas_call(
+        subgrid_kernel,
+        out_shape=[jax.ShapeDtypeStruct((GROUP, 2 * SUB * SUB), jnp.bfloat16)] * 4
+        + [jax.ShapeDtypeStruct((4, capacity - GROUP, 2 * SUB * SUB), jnp.bfloat16)],
+        in_specs=[smem] * 4 + [vmem] * 4,
+        out_specs=[vmem] * 5,
+        scratch_shapes=[pltpu.VMEM((capacity, 4, 2 * SUB * SUB), jnp.float32)],
+        name="subgrids",
+    )(count, pol, source, start, slots, jnp.asarray(pixel_rows()), jnp.asarray(row_twiddles()), weight_row)
+
+
+def image_kernel(pol_step, x_block, slabs, groups_ref, base_ref, row_ref, col_ref, mix_ref, twist_ref, *refs):
+    first_refs, more_ref, sky_ref = refs[:slabs], refs[slabs], refs[slabs + 1]
+    bundle_ref, phase_ref, col_phase_ref, half_ref, moved_ref, sum_ref, stage_ref, out_ref = refs[slabs + 2 : -3]
+    later_ref, sem_ref, later_sem_ref = refs[-3:]
+    x_blocks = sky_ref.shape[1] // x_block
+    groups = groups_ref[0]
+    lane_index = lax.broadcasted_iota(jnp.int32, (LANES, LANES), 1)
+    eighth = SUB // 4
+    out_rows = out_ref.shape[2]
+    out_steps = x_block // out_rows
+    group_chunks = 4 // pol_step
+    depth = 2 * LANES
+
+    def load_phases(group, part):
+        chunk = group * group_chunks + part
+        rows = jnp.transpose(jnp.broadcast_to(row_ref[pl.ds(chunk, 1), :].astype(jnp.float32), (LANES, LANES)))
+        rows = rows.astype(jnp.int32)
+        high = lax.shift_right_logical(rows, 5)
+        low = jnp.bitwise_and(rows, SUB - 1)
+        here = cos_sin_turns(jnp.bitwise_and(high * lane_index, LANES - 1).astype(jnp.float32) * (1.0 / LANES))
+        later = cos_sin_turns(jnp.bitwise_and((high + 1) * lane_index, LANES - 1).astype(jnp.float32) * (1.0 / LANES))
+        re_rows = pl.ds(part * depth, LANES)
+        im_rows = pl.ds(part * depth + LANES, LANES)
+
+        def one_phase(residue, inner):
+            carried = low > residue
+            re = jnp.where(carried, later[0], here[0]).astype(jnp.bfloat16)
+            im = jnp.where(carried, later[1], here[1])
+            phase_ref[residue, re_rows, :LANES] = re
+            phase_ref[residue, re_rows, LANES:] = im.astype(jnp.bfloat16)
+            phase_ref[residue, im_rows, :LANES] = (-im).astype(jnp.bfloat16)
+            phase_ref[residue, im_rows, LANES:] = re
+            return inner
+
+        lax.fori_loop(0, SUB, one_phase, 0)
+
+    def move_rows(group, part, block):
+        chunk = group * group_chunks + part
+        cols = col_ref[pl.ds(chunk, 1), :]
+        x_index = lax.broadcasted_iota(jnp.int32, (x_block, LANES), 0) + (base_ref[0] + block * x_block)
+        turns = jnp.bitwise_and(x_index * cols, G - 1).astype(jnp.float32) * (1.0 / G)
+        turn_re, turn_im = cos_sin_turns(turns)
+        col_phase_ref[0] = turn_re
+        col_phase_ref[1] = turn_im
+        for pair in range(eighth // 2):
+            wide = jnp.concatenate(
+                [
+                    bundle_ref[part, :, pl.ds(4 * pair * LANES, depth)],
+                    bundle_ref[part, :, pl.ds((4 * pair + 2) * LANES, depth)],
+                ],
+                axis=0,
+            )
+            for side in range(2):
+                half_ref[pair, side] = lax.dot_general(
+                    mix_ref[block, side], wide, (((1,), (1,)), ((), ())), preferred_element_type=jnp.float32
+                )
+
+        def one_tile(tile, inner):
+            rows_at = pl.ds(pl.multiple_of(tile * 16, 16), 16)
+            turn = (col_phase_ref[0, rows_at], col_phase_ref[1, rows_at])
+            for low in range(eighth):
+                at = pl.ds(low % 2 * LANES, LANES)
+                for high in range(4):
+                    tile_rows = pl.ds(pl.multiple_of(high * x_block + tile * 16, 16), 16)
+                    value = (half_ref[low // 2, 0, tile_rows, at], half_ref[low // 2, 1, tile_rows, at])
+                    re, im = times(value, turn)
+                    moved_ref[low + 8 * high, rows_at, pl.ds(part * depth, LANES)] = re.astype(jnp.bfloat16)
+                    moved_ref[low + 8 * high, rows_at, pl.ds(part * depth + LANES, LANES)] = im.astype(jnp.bfloat16)
+            return inner
+
+        lax.fori_loop(0, x_block // 16, one_tile, 0)
+
+    def load_group(group):
+        @pl.when(group > 0)
+        def _():
+            copy = pltpu.make_async_copy(more_ref, later_ref, later_sem_ref)
+            copy.start()
+            copy.wait()
+
+        for part in range(group_chunks):
+            polarized = pl.ds(part * pol_step, pol_step)
+            span = pol_step * GROUP
+            for peer in range(slabs):
+                rows_at = pl.ds(peer * span, span)
+
+                @pl.when(group == 0)
+                def _(part=part, polarized=polarized, peer=peer, rows_at=rows_at):
+                    bundle_ref[part, rows_at] = first_refs[peer][polarized].reshape(span, -1)
+
+                @pl.when(group > 0)
+                def _(part=part, polarized=polarized, peer=peer, rows_at=rows_at):
+                    bundle_ref[part, rows_at] = later_ref[peer, polarized].reshape(span, -1)
+
+            load_phases(group, part)
+
+    def copy_out(block, step):
+        x_at = pl.ds(pl.multiple_of(block * x_block + step * out_rows, 8), out_rows)
+        return pltpu.make_async_copy(out_ref.at[step], sky_ref.at[:, x_at], sem_ref.at[step])
+
+    def one_block(block, carry):
+        def one_group(group, inner):
+            @pl.when((block == 0) | (groups > 1))
+            def _():
+                load_group(group)
+
+            for part in range(group_chunks):
+                move_rows(group, part, block)
+
+            @pl.when(group == 0)
+            def _():
+                def one_residue(residue, innermost):
+                    sum_ref[residue] = jnp.dot(
+                        moved_ref[residue], phase_ref[residue], preferred_element_type=jnp.float32
+                    )
+                    return innermost
+
+                lax.fori_loop(0, SUB, one_residue, 0, unroll=4)
+
+            @pl.when(group > 0)
+            def _():
+                def one_residue(residue, innermost):
+                    sum_ref[residue] += jnp.dot(
+                        moved_ref[residue], phase_ref[residue], preferred_element_type=jnp.float32
+                    )
+                    return innermost
+
+                lax.fori_loop(0, SUB, one_residue, 0)
+
+            return inner
+
+        lax.fori_loop(0, groups, one_group, 0)
+
+        def one_step(step, inner):
+            @pl.when(block > 0)
+            def _():
+                copy_out(block - 1, step).wait()
+
+            def one_tile(tile, innermost):
+                rows_at = pl.ds(pl.multiple_of(step * out_rows + tile * 8, 8), 8)
+                for second in range(4):
+                    parts = []
+                    for first in range(8):
+                        residue = 4 * first + second
+                        value = (sum_ref[residue, rows_at, :LANES], sum_ref[residue, rows_at, LANES:])
+                        twist = (twist_ref[2 * residue : 2 * residue + 1], twist_ref[2 * residue + 1 : 2 * residue + 2])
+                        parts.append(times(value, twist))
+                    for first, value in enumerate(dft_8(parts, 1)):
+                        if first * second:
+                            angle = TWO_PI * first * second / SUB
+                            value = times(value, (math.cos(angle), math.sin(angle)))
+                        stage_ref[second, first, 0] = value[0]
+                        stage_ref[second, first, 1] = value[1]
+                to_rows = pl.ds(pl.multiple_of(tile * 8, 8), 8)
+                for first in range(8):
+                    parts = [(stage_ref[second, first, 0], stage_ref[second, first, 1]) for second in range(4)]
+                    for second, value in enumerate(dft_4(parts, 1)):
+                        lanes = pl.ds((first + 8 * second) * LANES, LANES)
+                        out_ref[step, 0, to_rows, lanes] = value[0]
+                        out_ref[step, 1, to_rows, lanes] = value[1]
+                return innermost
+
+            lax.fori_loop(0, out_rows // 8, one_tile, 0)
+            copy_out(block, step).start()
+            return inner
+
+        lax.fori_loop(0, out_steps, one_step, 0)
+        return carry
+
+    lax.fori_loop(0, x_blocks, one_block, 0)
+    for step in range(out_steps):
+        copy_out(x_blocks - 1, step).wait()
+
+
+def twist_table(scale):
+    residue = np.arange(SUB)[:, None]
+    lane = np.arange(LANES)[None, :]
+    angle = 2.0 * np.pi * (residue * lane % G) / G
+    sign = np.where(residue % 2 == 0, scale, -scale)
+    return np.stack([sign * np.cos(angle), sign * np.sin(angle)], axis=1).reshape(2 * SUB, LANES).astype(np.float32)
+
+
+def mix_table(x_base, x_count, x_block):
+    highest = lax.Precision.HIGHEST
+    x_index = x_base + jnp.arange(x_count, dtype=jnp.int32)
+    cell = jnp.arange(SUB, dtype=jnp.int32)
+    line_re, line_im = cos_sin_turns((x_index[:, None] * cell[None, :] % G).astype(jnp.float32) * (1.0 / G))
+    cells, pixels = np.arange(SUB)[:, None], np.arange(LANES)[None, :] % SUB
+    angle = -2.0 * np.pi * ((cells - SUB // 2) * (pixels - SUB // 2) % SUB) / SUB
+    sub_re, sub_im = jnp.asarray(np.cos(angle), jnp.float32), jnp.asarray(np.sin(angle), jnp.float32)
+    core_re = jnp.dot(line_re, sub_re, precision=highest) - jnp.dot(line_im, sub_im, precision=highest)
+    core_im = jnp.dot(line_re, sub_im, precision=highest) + jnp.dot(line_im, sub_re, precision=highest)
+    blocks = x_count // x_block
+    core_re = core_re.reshape(blocks, 1, x_block, LANES)
+    core_im = core_im.reshape(blocks, 1, x_block, LANES)
+    turn = (np.arange(4)[:, None] * (np.arange(LANES)[None, :] // SUB)) % 4
+    turn_re = jnp.asarray(np.array([1.0, 0.0, -1.0, 0.0], np.float32)[turn][None, :, None, :])
+    turn_im = jnp.asarray(np.array([0.0, -1.0, 0.0, 1.0], np.float32)[turn][None, :, None, :])
+    re = (core_re * turn_re - core_im * turn_im).astype(jnp.bfloat16)
+    im = (core_re * turn_im + core_im * turn_re).astype(jnp.bfloat16)
+    table = jnp.stack([jnp.concatenate([re, -im], axis=3), jnp.concatenate([im, re], axis=3)], axis=1)
+    return table.reshape(blocks, 2, 4 * x_block, 2 * LANES)
+
+
+def image_of(groups, x_base, first, more, rows, cols, mix, x_count, x_block, scale, pol_step):
+    out_rows = min(x_block, 64)
+    parts = 4 // pol_step
+    slabs = len(first)
+    smem = pl.BlockSpec(memory_space=pltpu.SMEM)
+    vmem = pl.BlockSpec(memory_space=pltpu.VMEM)
+    hbm = pl.BlockSpec(memory_space=pl.ANY)
+    return pl.pallas_call(
+        functools.partial(image_kernel, pol_step, x_block, slabs),
+        out_shape=jax.ShapeDtypeStruct((2, x_count, G), jnp.float32),
+        in_specs=[smem, smem] + [vmem] * (4 + slabs) + [hbm],
+        out_specs=hbm,
+        scratch_shapes=[
+            pltpu.VMEM((parts, LANES, 2 * SUB * SUB), jnp.bfloat16),
+            pltpu.VMEM((SUB, parts * 2 * LANES, 2 * LANES), jnp.bfloat16),
+            pltpu.VMEM((2, x_block, LANES), jnp.float32),
+            pltpu.VMEM((4, 2, 4 * x_block, 2 * LANES), jnp.float32),
+            pltpu.VMEM((SUB, x_block, parts * 2 * LANES), jnp.bfloat16),
+            pltpu.VMEM((SUB, x_block, 2 * LANES), jnp.float32),
+            pltpu.VMEM((4, 8, 2, 8, LANES), jnp.float32),
+            pltpu.VMEM((x_block // out_rows, 2, out_rows, G), jnp.float32),
+            pltpu.VMEM(more.shape, more.dtype),
+            pltpu.SemaphoreType.DMA((x_block // out_rows,)),
+            pltpu.SemaphoreType.DMA,
+        ],
+        compiler_params=pltpu.CompilerParams(vmem_limit_bytes=60 * 1024 * 1024),
+        name="image",
+    )(groups, x_base, rows, cols, mix, jnp.asarray(twist_table(scale)), *first, more)
+
+
+def exchanged(value, axis, distance):
+    peers = lax.axis_size(axis)
+    return lax.ppermute(value, axis, [(i, i ^ distance) for i in range(peers)])
+
+
+def gathered(pieces):
+    slabs = lax.axis_size("slab")
+    value = jnp.stack([pieces[0]] + [exchanged(piece, "pol", k) for k, piece in enumerate(pieces) if k])
+    values = []
+    for k in range(0, slabs, 2):
+        moved = exchanged(value, "slab", k) if k else value
+        values += [moved, exchanged(moved, "slab", 1)]
+    return values
+
+
+def in_image_domain(correlations, tracks, vis_counts, offsets, held_counts, pixel_weight):
+    pols, slabs = lax.axis_size("pol"), lax.axis_size("slab")
+    pol, slab = lax.axis_index("pol"), lax.axis_index("slab")
+    devices = pols * slabs
+    waves = SLOTS // devices
+    capacity = SLOTS * slabs // devices
+    x_count = G // slabs
+    own_device = pol * slabs + slab
+    held = held_counts.astype(jnp.int32)
+    holders = jnp.arange(slabs, dtype=jnp.int32)
+    before = jnp.sum(jnp.where(holders[None, :] < holders[:, None], held[None, :], 0), axis=1)
+    total = jnp.sum(held)
+    own_before = jnp.sum(jnp.where(holders == slab, before, 0))
+
+    slot = jnp.arange(SLOTS, dtype=jnp.int32)
+    order = jnp.where(slot[None, :] < held[:, None], before[:, None] + slot[None, :], -1).reshape(-1)
+    device_at, seat_at = order % devices, order // devices
+    pol_step = LANES // (GROUP * slabs)
+    lane_order = (device_at % slabs) ^ slab
+    pol_order = (device_at // slabs) ^ pol
+    place = (seat_at // GROUP) * (pols // pol_step) + pol_order // pol_step
+    place = place * LANES + lane_order * (pol_step * GROUP) + pol_order % pol_step * GROUP + seat_at % GROUP
+    place = jnp.where(order >= 0, place, -1)
+    chunk_count = capacity // GROUP * (pols // pol_step)
+    spots = jnp.arange(chunk_count * LANES, dtype=jnp.int32)
+    chosen = spots[:, None] == place[None, :]
+    rows = jnp.sum(jnp.where(chosen, offsets[0][None, :], 0), axis=1).reshape(chunk_count, LANES)
+    cols = jnp.sum(jnp.where(chosen, offsets[1][None, :], 0), axis=1).reshape(chunk_count, LANES)
+    seats = jnp.arange(capacity, dtype=jnp.int32)
+    mine = (seats[:, None] * devices + own_device) == order[None, :]
+    wave_at = jnp.broadcast_to(holders[:, None] * waves + slot[None, :] // devices, (slabs, SLOTS)).reshape(-1)
+    source = jnp.sum(jnp.where(mine, wave_at[None, :], 0), axis=1)
+    start = jnp.sum(jnp.where(mine, jnp.bitwise_and(offsets[0], SUB - 1)[None, :], 0), axis=1)
+    count = jnp.maximum((total - own_device + devices - 1) // devices, 0).reshape(1)
+
+    visible = jnp.arange(VIS, dtype=jnp.int32)[None, :] < vis_counts[:, None]
+    corr = jnp.where(visible[None], correlations[:, 0].astype(jnp.float32), 0.0)
+    shift = (devices - own_before % devices) % devices
+
+    def sent(value):
+        lead = value.shape[0]
+        value = value.reshape(lead, waves, devices, VIS)
+        value = lax.dynamic_slice_in_dim(jnp.concatenate([value, value], axis=2), shift, devices, 2)
+        return jnp.transpose(value, (2, 1, 0, 3)).reshape(devices, waves * lead * VIS)
+
+    track_piece = waves * 3 * VIS // pols
+    track_part = lax.dynamic_slice_in_dim(sent(tracks), pol * track_piece, track_piece, 1)
+    packed = jnp.concatenate([sent(corr), track_part], axis=1)
+    got = lax.all_to_all(packed, ("pol", "slab"), 0, 0, tiled=True).reshape(pols, slabs, -1)
+    corr_size = waves * 2 * VIS
+    got_corr = jnp.transpose(got[:, :, :corr_size].reshape(pols, slabs, waves, 2, VIS), (1, 2, 3, 0, 4))
+    got_track = jnp.transpose(got[:, :, corr_size:], (1, 0, 2)).reshape(slabs, waves, 3, VIS)
+    slots = jnp.concatenate(
+        [
+            got_corr.reshape(slabs, waves, 2 * pols, VIS),
+            got_track,
+            jnp.zeros((slabs, waves, 16 - 2 * pols - 3, VIS), jnp.float32),
+        ],
+        axis=2,
+    ).reshape(slabs * waves, 16, VIS)
+    weight_row = pixel_weight.reshape(1, SUB * SUB)
+    *subgrids, extra = subgrids_of(count, pol.reshape(1), source, start, slots, weight_row)
+    first = gathered(subgrids)
+    many = total > devices * GROUP
+    more = lax.cond(
+        many,
+        lambda: jnp.stack(gathered([extra[k] for k in range(pols)])),
+        lambda: jnp.zeros((slabs,) + extra.shape, extra.dtype),
+    )
+    groups = jnp.where(many, capacity // GROUP, 1).reshape(1)
+    norm_scale = 1.0 / (SUB * SUB * math.sqrt(VIS * SLOTS * slabs / 8.0))
+    x_base = (slab * x_count).reshape(1)
+    x_block = min(x_count, 256)
+    mix_base, _ = lax.optimization_barrier((x_base, subgrids[0]))
+    mix = mix_table(mix_base[0], x_count, x_block)
+    sky = image_of(groups, x_base, first, more, rows, cols, mix, x_count, x_block, norm_scale, pol_step)
+    return sky[:, None]
+
+
+def fits_image_domain(mesh):
+    pols, slabs = mesh.shape["pol"], mesh.shape["slab"]
+    devices = pols * slabs
+    whole = slabs & (slabs - 1) == 0 and slabs * GROUP <= LANES and SLOTS * slabs == 2 * GROUP * devices
+    return whole and pols == 4 and SLOTS % devices == 0 and pols % (LANES // (GROUP * slabs)) == 0
+
+
 def solution(mesh):
     in_specs = (P(None, "pol", "slab", None), P(None, "slab", None), P("slab"), P(), P(), P())
     out_specs = P(None, "pol", "slab", None)
-    return jax.shard_map(
-        on_device, mesh=mesh, in_specs=in_specs, out_specs=out_specs, check_vma=False
-    )
+    body = in_image_domain if fits_image_domain(mesh) else on_device
+    return jax.shard_map(body, mesh=mesh, in_specs=in_specs, out_specs=out_specs, check_vma=False)

time: 1750 us -> 91 us (0.05); the launches traced: 1720 us -> 89.7 us
  local copies, waits for them, and re-layouts: 410 us -> 6.89 us
  matrix products: 404 us -> 2.58 us
  blocking collectives: 384 us -> 0 us
  loops' own time: 235 us -> 0.01 us
  starting transfers between devices: 183 us -> 15.9 us
  other arithmetic: 92.2 us -> 10.1 us
  Pallas kernels: 0 us -> 40.1 us
    dot_general x29 -> x4, matrix products: 404 us -> 2.58 us  [the longest x1 0.65 us: mix_table(): jnp.dot(line_im, sub_im, precision=highest)]
    all_to_all x1 -> x0, blocking collectives: 375 us -> none  [on_device(): lax.all_to_all(jnp.stack([step_re, step_im]), 'slab', split_axis=1, conca...]
    another operation x3 -> x1, loops' own time: 235 us -> 0.01 us  [in_image_domain(): lax.cond(many, lambda: jnp.stack(gathered([extra[k] for k in range(pols)]...]
    dynamic_update_slice x64 -> x0, local copies, waits for them, and re-layouts: 197 us -> none  [add_one(): return lax.dynamic_update_slice(current_window, current + block, corner)]
    ppermute x4 -> x10, starting transfers between devices: 183 us -> 8.54 us  [exchanged(): return lax.ppermute(value, axis, [(i, i ^ distance) for i in range(peers)])]
    dynamic_slice x130 -> x1, local copies, waits for them, and re-layouts: 79.9 us -> 0.01 us  [in_image_domain(): lax.dynamic_slice_in_dim(sent(tracks), pol * track_piece, track_piece, 1)]
    add x64 -> x3, other arithmetic: 63 us -> 0.08 us  [the longest x1 0.07 us: in_image_domain(): holders[:, None] * waves + slot[None, :] // devices]
    another operation x4 -> x1, local copies, waits for them, and re-layouts: 58.4 us -> 1.1 us  [the longest x1 20.9 us: on_device(): line_im = moved_block[1].reshape(rows_local, large_side, small_side)]
  transfers between devices with their start and end apart: 4 -> 11, of which waited for: 1 -> 3; matrix products, arithmetic and copies ran while one was open for 1% -> 13% of each run, Pallas kernels for 0% -> 0%
where the time goes in v1:
time: 91 us; the launch traced here: 89.7 us
  Pallas kernels  40.1 us (44%)
  starting transfers between devices  15.9 us (17%)
  waiting for transfers between devices  10.4 us (11%)
  other arithmetic  10.1 us (11%)
  local copies, waits for them, and re-layouts  6.89 us (8%)
  between operations  3.74 us (4%)
  matrix products  2.58 us (3%)
    pallas_call x1, Pallas kernels, image_of(): pl.pallas_call(functools.partial(image_kernel, pol_step, x_block, slabs),...  29.2 us
    pallas_call x1, Pallas kernels, subgrids_of(): pl.pallas_call(subgrid_kernel, out_shape=[jax.ShapeDtypeStruct((GROUP, 2...  10.9 us
    ppermute x10, waiting for transfers between devices, exchanged(): return lax.ppermute(value, axis, [(i, i ^ distance) for i in range(peers)])  8.98 us
    ppermute x10, starting transfers between devices, exchanged(): return lax.ppermute(value, axis, [(i, i ^ distance) for i in range(peers)])  8.54 us
    all_to_all x1, starting transfers between devices, in_image_domain(): lax.all_to_all(packed, ('pol', 'slab'), 0, 0, tiled=True)  7.33 us
  transfers between devices with their start and end apart: 11, of which 3 were waited for; matrix products, arithmetic and copies ran while one was open for 13% of the time, Pallas kernels for 0%

profile of v1, /device:TPU:0, one launch (start us, length us, event | category | flops | bytes accessed | tf_op | source)
XLA Modules:
  0.0 89.7 jit_solution(8707241005623020121)
XLA Ops:
  0.0 0.8 select_reduce_fusion.2
  0.8 0.6 fusion.49
  3.4 0.7 lt.109
  4.1 0.1 copy.39
  4.2 0.1 iota_compare_fusion.1
  4.3 0.9 convert.1
  5.2 0.1 copy_select_fusion
  5.3 0.2 fusion.7
  5.5 0.1 reshape.394
  5.7 1.1 %copy.41 = f32[3,2,32,256]{3,0,1,2:T(4,128)S(1)} copy(f32[3,2,32,256]{3,2,1,0:T(8,128)} %bitcast.104) | data formatting | bytes 393216 | tf_op jit(solution)/shard_map/reshape | solution.py:674
  6.7 0.2 fusion.5
  7.0 0.1 reshape.396
  7.2 0.9 copy.43
  8.0 7.3 %all-to-all-start = ((f32[32,1,1408]{2,1,0:T(1,128)}), f32[32,1,1408]{2,1,0:T(1,128)S(1)}, u32[]{:S(2)}, u32[]{:S(2)}) async-start(f32[32,1,1408]{2,1,0:T(1,128)} %copy.43), calls=%async_computation | async-start | bytes 360448 | tf_op jit(solution)/shard_map/all_to_all | solution.py:681
  15.3 1.3 %reduce_sum.63 = s32[]{:T(128)} reduce(s32[8]{0:T(128)} %param.19, s32[]{:T(128)} %constant.166.clone.1), dimensions={0}, to_apply=%region_0.1 | reduce | flops 7 | bytes 40 | tf_op jit(solution)/shard_map/reduce_sum | solution.py:644
  17.2 0.7 add_select_fusion.1
  18.5 0.1 broadcast_add_fusion
  18.6 0.1 add.273
  18.7 0.1 select_n.159
  18.8 1.4 %reshape.399.weight_ref = f32[1,1024]{1,0:T(1,128)} reshape(f32[32,32]{1,0:T(8,128)} %param.20) | data formatting | bytes 8192 | tf_op jit(solution)/shard_map/reshape | solution.py:693
  20.2 0.8 broadcast_and_fusion
  20.9 0.1 pad.14.clone
  21.0 0.7 fusion.23
  21.7 1.0 %select_reduce_fusion = (s32[512]{0:T(512)}, s32[512]{0:T(512)}) fusion(s32[512]{0:T(512)S(1)} %bitcast.118, s32[512]{0:T(512)S(1)} %fusion.44, s32[512]{0:T(512)S(1)} %bitcast.119), kind=kLoop, calls=%fused_computation.23 | loop fusion | flops 1309696 | bytes 10240 | tf_op jit(solution)/shard_map/reduce_sum | solution.py:660
  22.7 1.4 %all-to-all-done = f32[32,1,1408]{2,1,0:T(1,128)S(1)} async-done(((f32[32,1,1408]{2,1,0:T(1,128)}), f32[32,1,1408]{2,1,0:T(1,128)S(1)}, u32[]{:S(2)}, u32[]{:S(2)}) %all-to-all-start) | async-done | bytes 180256 | tf_op jit(solution)/shard_map/all_to_all | solution.py:681
  24.1 0.1 copy.52
  24.3 0.8 maximum_maximum_fusion.1.slots_ref
  25.1 10.9 %subgrids.1 = (bf16[8,2048]{1,0:T(8,128)(2,1)}, bf16[8,2048]{1,0:T(8,128)(2,1)}, bf16[8,2048]{1,0:T(8,128)(2,1)}, bf16[8,2048]{1,0:T(8,128)(2,1)}, bf16[4,8,2048]{2,1,0:T(8,128)(2,1)S(1)}) custom-call(s32[1]{0:T(128)} %bitcast.20.count_ref, s32[1]{0:T(128)} %bitcast.21.pol_ref, s32[16]{0:T(128)} %get-tuple-element.22.source_ref, ...), custom_call_target="tpu_custom_call" | custom-call | tf_op jit(solution)/shard_map/subgrids/pallas_call | solution.py:374
  36.0 1.0 %collective-permute-start.10 = (bf16[8,2048]{1,0:T(8,128)(2,1)}, bf16[8,2048]{1,0:T(8,128)(2,1)S(1)}, u32[]{:S(2)}, u32[]{:S(2)}) collective-permute-start(bf16[8,2048]{1,0:T(8,128)(2,1)} %get-tuple-element.17), channel_id=1, source_target_pairs={{0,8},{8,0},{16,24},{24,16},{1,9},{9,1},{17,25},{25,17},{2,10},{10... | collective-permute-start | bytes 98312 | tf_op jit(solution)/shard_map/ppermute | solution.py:620
  37.1 1.1 %conditional.1 = (bf16[8,4,8,2048]{3,2,1,0:T(8,128)(2,1)}) conditional(s32[]{:T(128)} %convert_element_type.38, () %tuple.13, bf16[4,8,2048]{2,1,0:T(8,128)(2,1)S(1)} %get-tuple-element.20), branch_computations={%region_7.8_spmd, %region_8.9_spmd} | conditional | flops 720895 | bytes 6685080 | solution.py:697
  37.1 1.1 %broadcast.407 = bf16[8,4,8,2048]{3,2,1,0:T(8,128)(2,1)} broadcast(bf16[]{:T(256)} %constant.165.clone), dimensions={} | broadcast | bytes 1048578 | tf_op jit(solution)/shard_map/broadcast.6
  38.2 2.4 %collective-permute-start.12 = (bf16[8,2048]{1,0:T(8,128)(2,1)}, bf16[8,2048]{1,0:T(8,128)(2,1)S(1)}, u32[]{:S(2)}, u32[]{:S(2)}) collective-permute-start(bf16[8,2048]{1,0:T(8,128)(2,1)} %get-tuple-element.19), channel_id=1, source_target_pairs={{0,24},{8,16},{16,8},{24,0},{1,25},{9,17},{17,9},{25,1},{2,26},{10... | collective-permute-start | bytes 98312 | tf_op jit(solution)/shard_map/ppermute | solution.py:620
  40.6 0.6 fusion.18
  41.3 0.6 fusion.20
  41.9 0.7 convolution_add_fusion
  42.6 0.7 convolution_subtract_fusion
  43.5 0.1 mul.264
  43.5 0.2 fusion.104
  43.8 2.3 %collective-permute-start.18 = (bf16[4,8,2048]{2,1,0:T(8,128)(2,1)S(1)}, bf16[4,8,2048]{2,1,0:T(8,128)(2,1)S(1)}, u32[]{:S(2)}, u32[]{:S(2)}) collective-permute-start(bf16[4,8,2048]{2,1,0:T(8,128)(2,1)S(1)} %pad_maximum_fusion.1.refs_0_), channel_id=1, source_target_pairs={{0,6},{1,7},{2,4},{3,5},{4,2},{5,3},{6,0},{7,1},{8,14},{9,15},{10,... | collective-permute-start | bytes 393224 | tf_op jit(solution)/shard_map/ppermute | solution.py:620
  46.2 2.1 %collective-permute-start.14 = (bf16[4,8,2048]{2,1,0:T(8,128)(2,1)S(1)}, bf16[4,8,2048]{2,1,0:T(8,128)(2,1)S(1)}, u32[]{:S(2)}, u32[]{:S(2)}) collective-permute-start(bf16[4,8,2048]{2,1,0:T(8,128)(2,1)S(1)} %pad_maximum_fusion.1.refs_0_), channel_id=1, source_target_pairs={{0,2},{1,3},{2,0},{3,1},{4,6},{5,7},{6,4},{7,5},{8,10},{9,11},{10,... | collective-permute-start | bytes 393224 | tf_op jit(solution)/shard_map/ppermute | solution.py:620
  48.3 0.1 fusion.1
  48.4 0.1 collective-permute-start.13
  48.5 3.6 %collective-permute-done.18.refs_6_ = bf16[4,8,2048]{2,1,0:T(8,128)(2,1)S(1)} collective-permute-done((bf16[4,8,2048]{2,1,0:T(8,128)(2,1)S(1)}, bf16[4,8,2048]{2,1,0:T(8,128)(2,1)S(1)}, u32[]{:S(2)}, u32[]{:S(2)}) %collective-permute-start.18) | collective-permute-done | bytes 131104 | tf_op jit(solution)/shard_map/ppermute | solution.py:620
  52.1 5.4 %collective-permute-done.16.refs_4_ = bf16[4,8,2048]{2,1,0:T(8,128)(2,1)S(1)} collective-permute-done((bf16[4,8,2048]{2,1,0:T(8,128)(2,1)S(1)}, bf16[4,8,2048]{2,1,0:T(8,128)(2,1)S(1)}, u32[]{:S(2)}, u32[]{:S(2)}) %collective-permute-start.16) | collective-permute-done | bytes 131104 | tf_op jit(solution)/shard_map/ppermute | solution.py:620
  57.5 0.5 collective-permute-start.15
  58.0 1.5 %maximum_maximum_fusion.mix_ref = bf16[2,2,1024,256]{3,2,1,0:T(8,128)(2,1)} fusion(bf16[2,1,1024,128]{3,2,1,0:T(8,128)(2,1)S(1)} %fusion.1, bf16[2,1,1024,128]{3,2,1,0:T(8,128)(2,1)S(1)} %get-tuple-element.26, bf16[2,1,1024,128]{3,2,1,0:T(8,128)(2,1)S(1)} %get-tuple-element.25), kind=kLoop, calls=%fused_computation.12 | loop fusion | flops 8388608 | bytes 3670016 | tf_op jit(solution)/shard_map/stack | solution.py:584
  59.6 0.5 copy-done.4
  60.3 29.2 %image.1 = f32[2,512,4096]{2,1,0:T(8,128)} custom-call(s32[1]{0:T(128)} %bitcast.14.groups_ref, s32[1]{0:T(128)} %bitcast.15.base_ref, s32[4,128]{1,0:T(4,128)} %bitcast.117, s32[4,128]{1,0:T(4,128)} %bitcast.116, bf16[2,2,1024,256]{3,2,1,0:T(8,128)(2,1)} %maximum_maximum_fusion.mix_ref, f32[64,128]{1,0:T(8,128)} %constant.208.clone.twist_ref, ...), custom_call_target="tpu_custom_call" | custom-call | tf_op jit(solution)/shard_map/image/pallas_call | solution.py:595
  (55 shorter events, 0.6 us)
Async XLA Ops:
  6.7 33.9 %copy-start.11 = (f32[32,128]{1,0:T(8,128)S(1)}, f32[32,128]{1,0:T(8,128)}, u32[]{:S(2)}) copy-start(f32[32,128]{1,0:T(8,128)} %constant.205.clone) | copy-start | bytes 49156
  7.0 34.3 %copy-start.12 = (f32[32,128]{1,0:T(8,128)S(1)}, f32[32,128]{1,0:T(8,128)}, u32[]{:S(2)}) copy-start(f32[32,128]{1,0:T(8,128)} %constant.204.clone) | copy-start | bytes 49156
  8.0 16.0 %all-to-all-start = ((f32[32,1,1408]{2,1,0:T(1,128)}), f32[32,1,1408]{2,1,0:T(1,128)S(1)}, u32[]{:S(2)}, u32[]{:S(2)}) async-start(f32[32,1,1408]{2,1,0:T(1,128)} %copy.43), calls=%async_computation | async-start | bytes 360448 | tf_op jit(solution)/shard_map/all_to_all | solution.py:681
  22.7 20.6 %copy-start.10 = (f32[4,128]{1,0:T(4,128)S(1)}, f32[4,128]{1,0:T(4,128)}, u32[]{:S(2)}) copy-start(f32[4,128]{1,0:T(4,128)} %constant.210) | copy-start | bytes 6148
  24.1 19.3 %copy-start.9 = (f32[4,128]{1,0:T(4,128)S(1)}, f32[4,128]{1,0:T(4,128)}, u32[]{:S(2)}) copy-start(f32[4,128]{1,0:T(4,128)} %constant.211) | copy-start | bytes 6148
  36.0 7.7 %collective-permute-start.10 = (bf16[8,2048]{1,0:T(8,128)(2,1)}, bf16[8,2048]{1,0:T(8,128)(2,1)S(1)}, u32[]{:S(2)}, u32[]{:S(2)}) collective-permute-start(bf16[8,2048]{1,0:T(8,128)(2,1)} %get-tuple-element.17), channel_id=1, source_target_pairs={{0,8},{8,0},{16,24},{24,16},{1,9},{9,1},{17,25},{25,17},{2,10},{10... | collective-permute-start | bytes 98312 | tf_op jit(solution)/shard_map/ppermute | solution.py:620
  38.2 5.6 %collective-permute-start.11 = (bf16[8,2048]{1,0:T(8,128)(2,1)}, bf16[8,2048]{1,0:T(8,128)(2,1)S(1)}, u32[]{:S(2)}, u32[]{:S(2)}) collective-permute-start(bf16[8,2048]{1,0:T(8,128)(2,1)} %get-tuple-element.18), channel_id=1, source_target_pairs={{0,16},{8,24},{16,0},{24,8},{1,17},{9,25},{17,1},{25,9},{2,18},{10... | collective-permute-start | bytes 98312 | tf_op jit(solution)/shard_map/ppermute | solution.py:620
  38.2 5.6 %collective-permute-start.12 = (bf16[8,2048]{1,0:T(8,128)(2,1)}, bf16[8,2048]{1,0:T(8,128)(2,1)S(1)}, u32[]{:S(2)}, u32[]{:S(2)}) collective-permute-start(bf16[8,2048]{1,0:T(8,128)(2,1)} %get-tuple-element.19), channel_id=1, source_target_pairs={{0,24},{8,16},{16,8},{24,0},{1,25},{9,17},{17,9},{25,1},{2,26},{10... | collective-permute-start | bytes 98312 | tf_op jit(solution)/shard_map/ppermute | solution.py:620
  42.6 1.2 %copy-start.8 = (bf16[8,2048]{1,0:T(8,128)(2,1)S(1)}, bf16[8,2048]{1,0:T(8,128)(2,1)}, u32[]{:S(2)}) copy-start(bf16[8,2048]{1,0:T(8,128)(2,1)} %get-tuple-element.15) | copy-start | bytes 98308
  43.8 15.8 %copy-start = (bf16[4,8,2048]{2,1,0:T(8,128)(2,1)}, bf16[4,8,2048]{2,1,0:T(8,128)(2,1)S(1)}, u32[]{:S(2)}) copy-start(bf16[4,8,2048]{2,1,0:T(8,128)(2,1)S(1)} %pad_maximum_fusion.1.refs_0_) | copy-start | bytes 393220
  43.8 8.3 %collective-permute-start.18 = (bf16[4,8,2048]{2,1,0:T(8,128)(2,1)S(1)}, bf16[4,8,2048]{2,1,0:T(8,128)(2,1)S(1)}, u32[]{:S(2)}, u32[]{:S(2)}) collective-permute-start(bf16[4,8,2048]{2,1,0:T(8,128)(2,1)S(1)} %pad_maximum_fusion.1.refs_0_), channel_id=1, source_target_pairs={{0,6},{1,7},{2,4},{3,5},{4,2},{5,3},{6,0},{7,1},{8,14},{9,15},{10,... | collective-permute-start | bytes 393224 | tf_op jit(solution)/shard_map/ppermute | solution.py:620
  46.2 11.3 %collective-permute-start.16 = (bf16[4,8,2048]{2,1,0:T(8,128)(2,1)S(1)}, bf16[4,8,2048]{2,1,0:T(8,128)(2,1)S(1)}, u32[]{:S(2)}, u32[]{:S(2)}) collective-permute-start(bf16[4,8,2048]{2,1,0:T(8,128)(2,1)S(1)} %pad_maximum_fusion.1.refs_0_), channel_id=1, source_target_pairs={{0,4},{1,5},{2,6},{3,7},{4,0},{5,1},{6,2},{7,3},{8,12},{9,13},{10,... | collective-permute-start | bytes 393224 | tf_op jit(solution)/shard_map/ppermute | solution.py:620
  46.2 11.3 %collective-permute-start.14 = (bf16[4,8,2048]{2,1,0:T(8,128)(2,1)S(1)}, bf16[4,8,2048]{2,1,0:T(8,128)(2,1)S(1)}, u32[]{:S(2)}, u32[]{:S(2)}) collective-permute-start(bf16[4,8,2048]{2,1,0:T(8,128)(2,1)S(1)} %pad_maximum_fusion.1.refs_0_), channel_id=1, source_target_pairs={{0,2},{1,3},{2,0},{3,1},{4,6},{5,7},{6,4},{7,5},{8,10},{9,11},{10,... | collective-permute-start | bytes 393224 | tf_op jit(solution)/shard_map/ppermute | solution.py:620
  48.4 11.1 %collective-permute-start.13 = (bf16[4,8,2048]{2,1,0:T(8,128)(2,1)S(1)}, bf16[4,8,2048]{2,1,0:T(8,128)(2,1)S(1)}, u32[]{:S(2)}, u32[]{:S(2)}) collective-permute-start(bf16[4,8,2048]{2,1,0:T(8,128)(2,1)S(1)} %pad_maximum_fusion.1.refs_0_), channel_id=1, source_target_pairs={{0,1},{1,0},{2,3},{3,2},{4,5},{5,4},{6,7},{7,6},{8,9},{9,8},{10,11... | collective-permute-start | bytes 393224 | tf_op jit(solution)/shard_map/ppermute | solution.py:620
  52.1 7.5 %copy-start.1 = (bf16[4,8,2048]{2,1,0:T(8,128)(2,1)}, bf16[4,8,2048]{2,1,0:T(8,128)(2,1)S(1)}, u32[]{:S(2)}) copy-start(bf16[4,8,2048]{2,1,0:T(8,128)(2,1)S(1)} %collective-permute-done.18.refs_6_) | copy-start | bytes 393220
  52.1 7.4 %collective-permute-start.19 = (bf16[4,8,2048]{2,1,0:T(8,128)(2,1)S(1)}, bf16[4,8,2048]{2,1,0:T(8,128)(2,1)S(1)}, u32[]{:S(2)}, u32[]{:S(2)}) collective-permute-start(bf16[4,8,2048]{2,1,0:T(8,128)(2,1)S(1)} %collective-permute-done.18.refs_6_), channel_id=1, source_target_pairs={{0,1},{1,0},{2,3},{3,2},{4,5},{5,4},{6,7},{7,6},{8,9},{9,8},{10,11... | collective-permute-start | bytes 393224 | tf_op jit(solution)/shard_map/ppermute | solution.py:620
  57.5 2.1 %copy-start.2 = (bf16[4,8,2048]{2,1,0:T(8,128)(2,1)}, bf16[4,8,2048]{2,1,0:T(8,128)(2,1)S(1)}, u32[]{:S(2)}) copy-start(bf16[4,8,2048]{2,1,0:T(8,128)(2,1)S(1)} %collective-permute-done.16.refs_4_) | copy-start | bytes 393220
  57.5 2.1 %collective-permute-start.17 = (bf16[4,8,2048]{2,1,0:T(8,128)(2,1)S(1)}, bf16[4,8,2048]{2,1,0:T(8,128)(2,1)S(1)}, u32[]{:S(2)}, u32[]{:S(2)}) collective-permute-start(bf16[4,8,2048]{2,1,0:T(8,128)(2,1)S(1)} %collective-permute-done.16.refs_4_), channel_id=1, source_target_pairs={{0,1},{1,0},{2,3},{3,2},{4,5},{5,4},{6,7},{7,6},{8,9},{9,8},{10,11... | collective-permute-start | bytes 393224 | tf_op jit(solution)/shard_map/ppermute | solution.py:620
  57.5 2.1 %copy-start.3 = (bf16[4,8,2048]{2,1,0:T(8,128)(2,1)}, bf16[4,8,2048]{2,1,0:T(8,128)(2,1)S(1)}, u32[]{:S(2)}) copy-start(bf16[4,8,2048]{2,1,0:T(8,128)(2,1)S(1)} %collective-permute-done.14.refs_2_) | copy-start | bytes 393220
  57.5 2.1 %collective-permute-start.15 = (bf16[4,8,2048]{2,1,0:T(8,128)(2,1)S(1)}, bf16[4,8,2048]{2,1,0:T(8,128)(2,1)S(1)}, u32[]{:S(2)}, u32[]{:S(2)}) collective-permute-start(bf16[4,8,2048]{2,1,0:T(8,128)(2,1)S(1)} %collective-permute-done.14.refs_2_), channel_id=1, source_target_pairs={{0,1},{1,0},{2,3},{3,2},{4,5},{5,4},{6,7},{7,6},{8,9},{9,8},{10,11... | collective-permute-start | bytes 393224 | tf_op jit(solution)/shard_map/ppermute | solution.py:620
  59.5 0.6 copy-start.4
  59.5 0.7 copy-start.5
  59.6 0.7 copy-start.6
  59.6 0.7 copy-start.7

commit v2 on v1

--- a/solution.py
+++ b/solution.py
@@ -227,7 +227,7 @@
     sine = np.where(r > 0, np.sin(np.pi * r) / np.where(r > 0, r, 1.0), np.pi)
     fits = []
     for values in (sine, np.cos(np.pi * r)):
-        fit = np.polynomial.chebyshev.Chebyshev.fit(z, values, 5, domain=[0.0, 0.25])
+        fit = np.polynomial.chebyshev.Chebyshev.fit(z, values, 4, domain=[0.0, 0.25])
         fits.append([float(v) for v in fit.convert(kind=np.polynomial.Polynomial).coef])
     return fits
 
@@ -297,44 +297,113 @@
     return np.stack([l, m, n, row.astype(np.float32)] + [np.zeros_like(l)] * 4).astype(np.float32)
 
 
+HALVES = VIS // LANES
+WAVES = 2
+TRACK_ROWS = WAVES * 3 * HALVES
+
+
+def pack_kernel(held_ref, place_ref, counts_ref, corr_ref, track_ref, out_ref):
+    devices = out_ref.shape[0]
+    slab, pol = place_ref[0], place_ref[1]
+
+    def count_before(holder, total):
+        return total + jnp.where(holder < slab, held_ref[holder], 0)
+
+    shift = jnp.bitwise_and(lax.fori_loop(0, held_ref.shape[0], count_before, 0), devices - 1)
+    counts = jnp.transpose(jnp.broadcast_to(counts_ref[...].astype(jnp.float32), (LANES, counts_ref.shape[1])))
+    lane = lax.broadcasted_iota(jnp.int32, (devices, LANES), 1).astype(jnp.float32)
+    rows = []
+    for wave in range(WAVES):
+        at = pl.ds(wave * devices, devices)
+        for c in range(2):
+            for half in range(HALVES):
+                value = corr_ref[c, at, pl.ds(half * LANES, LANES)].astype(jnp.float32)
+                limit = counts[wave * devices : (wave + 1) * devices] - float(half * LANES)
+                rows.append(jnp.where(lane < limit, value, 0.0))
+    piece = TRACK_ROWS // 4
+    for row in range(piece):
+        value = None
+        for sender in range(4):
+            wave, axis, half = np.unravel_index(sender * piece + row, (WAVES, 3, HALVES))
+            part = track_ref[int(axis), pl.ds(int(wave) * devices, devices), pl.ds(int(half) * LANES, LANES)]
+            value = part if value is None else jnp.where(pol == sender, part, value)
+        rows.append(value)
+    for row, value in enumerate(rows):
+        out_ref[:, row, :] = pltpu.roll(value, shift, 0)
+    for row in range(len(rows), out_ref.shape[1]):
+        out_ref[:, row, :] = jnp.zeros((devices, LANES), jnp.float32)
+
+
+def packed(held, place, counts, corr, tracks, devices):
+    smem = pl.BlockSpec(memory_space=pltpu.SMEM)
+    vmem = pl.BlockSpec(memory_space=pltpu.VMEM)
+    return pl.pallas_call(
+        pack_kernel,
+        out_shape=jax.ShapeDtypeStruct((devices, 16, LANES), jnp.float32),
+        in_specs=[smem, smem, vmem, vmem, vmem],
+        out_specs=vmem,
+        name="packed",
+    )(held, place, counts, corr, tracks)
+
+
 def row_twiddles():
     angle = -2.0 * np.pi * np.arange(8)[:, None] * (np.arange(LANES)[None, :] // SUB) / SUB
     return np.concatenate([np.cos(angle), np.sin(angle)], axis=0).astype(np.float32)
 
 
-def subgrid_kernel(
-    count_ref, pol_ref, source_ref, start_ref, slots_ref, table_ref, twiddle_ref, weight_ref, *refs
-):
-    out_refs, more_ref, held_ref = refs[:4], refs[4], refs[5]
+def subgrid_kernel(held_counts_ref, place_ref, offsets_ref, slots_ref, table_ref, twiddle_ref, weight_ref, *refs):
+    piece_refs, more_ref, held_ref = refs[:4], refs[4], refs[5]
     held_ref[...] = jnp.zeros_like(held_ref)
-    pol = pol_ref[0]
+    slab, pol = place_ref[0], place_ref[1]
+    slabs = slots_ref.shape[0] // 4
+    devices = slots_ref.shape[0]
+    own = pol * slabs + slab
+    total = lax.fori_loop(0, slabs, lambda holder, value: value + held_counts_ref[holder], 0)
+    count = lax.shift_right_logical(total - own + (devices - 1), devices.bit_length() - 1)
+
+    def locate(index):
+        wanted = index * devices + own
+
+        def look(holder, found):
+            before, at_holder, at_slot = found
+            after = before + held_counts_ref[holder]
+            inside = (wanted >= before) & (wanted < after)
+            return after, jnp.where(inside, holder, at_holder), jnp.where(inside, wanted - before, at_slot)
+
+        _, at_holder, at_slot = lax.fori_loop(0, slabs, look, (0, 0, 0))
+        return at_holder, at_slot
 
     def one_slot(index, carry):
-        values = slots_ref[source_ref[index]]
-        row_start = start_ref[index].astype(jnp.float32)
-
-        def corr(c, p):
-            return values[4 * c + p : 4 * c + p + 1]
-
-        stokes = [
-            0.5 * corr(0, 0) + 0.5 * corr(0, 3),
-            0.5 * corr(0, 0) - 0.5 * corr(0, 3),
-            0.5 * corr(0, 1) + 0.5 * corr(0, 2),
-            0.5 * corr(1, 1) - 0.5 * corr(1, 2),
-            0.5 * corr(1, 0) + 0.5 * corr(1, 3),
-            0.5 * corr(1, 0) - 0.5 * corr(1, 3),
-            0.5 * corr(1, 1) + 0.5 * corr(1, 2),
-            0.5 * corr(0, 2) - 0.5 * corr(0, 1),
+        holder, slot = locate(index)
+        early = slot < devices
+        row_start = jnp.bitwise_and(offsets_ref[0, holder * SLOTS + slot], SUB - 1).astype(jnp.float32)
+        tiles = [slots_ref[p * slabs + holder] for p in range(4)]
+        xx, xy, yx, yy = [0.5 * jnp.where(early, tile[0:4], tile[4:8]) for tile in tiles]
+        turned = xy - yx
+        parameters = [xx + yy, xx - yy, xy + yx, jnp.concatenate([turned[2:4], -turned[0:2]], axis=0)]
+        chosen = []
+        for k in range(4):
+            value = parameters[k]
+            for other in range(1, 4):
+                value = jnp.where(pol == other, parameters[k ^ other], value)
+            chosen.append(value)
+        halves = [
+            jnp.concatenate([chosen[k][2 * c + half : 2 * c + half + 1] for c in range(2) for k in range(4)], axis=0)
+            for half in range(2)
         ]
-        rows = []
-        for part in (stokes[:4], stokes[4:]):
-            for k in range(4):
-                row = part[k]
-                for other in range(1, 4):
-                    row = jnp.where(pol == other, part[k ^ other], row)
-                rows.append(row)
-        vis = jnp.concatenate(rows, axis=0).astype(jnp.bfloat16)
-        track = jnp.transpose(values[8:16])
+        vis = jnp.concatenate(halves, axis=1).astype(jnp.bfloat16)
+
+        def track_half(axis, half):
+            found = []
+            for wave in range(WAVES):
+                sender, row = divmod((wave * 3 + axis) * HALVES + half, TRACK_ROWS // 4)
+                found.append(tiles[sender][8 + row : 9 + row])
+            return jnp.where(early, found[0], found[1])
+
+        track = jnp.concatenate(
+            [jnp.concatenate([track_half(axis, half) for half in range(2)], axis=1) for axis in (0, 1, 2, 2, 2, 2, 2, 2)], axis=0
+        )
+        track = jnp.transpose(track)
         shape = (VIS, LANES)
         u = jnp.broadcast_to(track[:, 0:1] * (TRACK_SCALE * SUB), shape)
         v = jnp.broadcast_to(track[:, 1:2] * (TRACK_SCALE * SUB), shape)
@@ -361,30 +430,29 @@
             held_ref[index, :, pl.ds((2 * rho + 1) * LANES, LANES)] = value[1]
         return carry
 
-    lax.fori_loop(0, count_ref[0], one_slot, 0)
+    lax.fori_loop(0, count, one_slot, 0)
     for k in range(4):
-        out_refs[k][...] = held_ref[:GROUP, k, :].astype(jnp.bfloat16)
+        piece_refs[k][...] = held_ref[:GROUP, k, :].astype(jnp.bfloat16)
         more_ref[k] = held_ref[GROUP:, k, :].astype(jnp.bfloat16)
 
 
-def subgrids_of(count, pol, source, start, slots, weight_row):
-    capacity = source.shape[0]
+def subgrids_of(held, place, offsets, slots, weight_row, capacity):
     smem = pl.BlockSpec(memory_space=pltpu.SMEM)
     vmem = pl.BlockSpec(memory_space=pltpu.VMEM)
     return pl.pallas_call(
         subgrid_kernel,
         out_shape=[jax.ShapeDtypeStruct((GROUP, 2 * SUB * SUB), jnp.bfloat16)] * 4
         + [jax.ShapeDtypeStruct((4, capacity - GROUP, 2 * SUB * SUB), jnp.bfloat16)],
-        in_specs=[smem] * 4 + [vmem] * 4,
+        in_specs=[smem] * 3 + [vmem] * 4,
         out_specs=[vmem] * 5,
         scratch_shapes=[pltpu.VMEM((capacity, 4, 2 * SUB * SUB), jnp.float32)],
         name="subgrids",
-    )(count, pol, source, start, slots, jnp.asarray(pixel_rows()), jnp.asarray(row_twiddles()), weight_row)
+    )(held, place, offsets, slots, jnp.asarray(pixel_rows()), jnp.asarray(row_twiddles()), weight_row)
 
 
 def image_kernel(pol_step, x_block, slabs, groups_ref, base_ref, row_ref, col_ref, mix_ref, twist_ref, *refs):
     first_refs, more_ref, sky_ref = refs[:slabs], refs[slabs], refs[slabs + 1]
-    bundle_ref, phase_ref, col_phase_ref, half_ref, moved_ref, sum_ref, stage_ref, out_ref = refs[slabs + 2 : -3]
+    bundle_ref, phase_ref, col_phase_ref, *half_refs, moved_ref, sum_ref, stage_ref, out_ref = refs[slabs + 2 : -3]
     later_ref, sem_ref, later_sem_ref = refs[-3:]
     x_blocks = sky_ref.shape[1] // x_block
     groups = groups_ref[0]
@@ -426,7 +494,10 @@
         turn_re, turn_im = cos_sin_turns(turns)
         col_phase_ref[0] = turn_re
         col_phase_ref[1] = turn_im
-        for pair in range(eighth // 2):
+        re_lanes = pl.ds(pl.multiple_of(part * depth, LANES), LANES)
+        im_lanes = pl.ds(pl.multiple_of(part * depth + LANES, LANES), LANES)
+
+        def mix_pair(pair, half_ref):
             wide = jnp.concatenate(
                 [
                     bundle_ref[part, :, pl.ds(4 * pair * LANES, depth)],
@@ -435,24 +506,29 @@
                 axis=0,
             )
             for side in range(2):
-                half_ref[pair, side] = lax.dot_general(
+                half_ref[side] = lax.dot_general(
                     mix_ref[block, side], wide, (((1,), (1,)), ((), ())), preferred_element_type=jnp.float32
                 )
 
-        def one_tile(tile, inner):
-            rows_at = pl.ds(pl.multiple_of(tile * 16, 16), 16)
-            turn = (col_phase_ref[0, rows_at], col_phase_ref[1, rows_at])
-            for low in range(eighth):
-                at = pl.ds(low % 2 * LANES, LANES)
-                for high in range(4):
-                    tile_rows = pl.ds(pl.multiple_of(high * x_block + tile * 16, 16), 16)
-                    value = (half_ref[low // 2, 0, tile_rows, at], half_ref[low // 2, 1, tile_rows, at])
-                    re, im = times(value, turn)
-                    moved_ref[low + 8 * high, rows_at, pl.ds(part * depth, LANES)] = re.astype(jnp.bfloat16)
-                    moved_ref[low + 8 * high, rows_at, pl.ds(part * depth + LANES, LANES)] = im.astype(jnp.bfloat16)
-            return inner
-
-        lax.fori_loop(0, x_block // 16, one_tile, 0)
+        def turn_pair(pair, half_ref):
+            for tile in range(x_block // 16):
+                rows_at = pl.ds(tile * 16, 16)
+                turn = (col_phase_ref[0, rows_at], col_phase_ref[1, rows_at])
+                for low in range(2):
+                    at = pl.ds(low * LANES, LANES)
+                    for high in range(4):
+                        tile_rows = pl.ds(high * x_block + tile * 16, 16)
+                        re, im = times((half_ref[0, tile_rows, at], half_ref[1, tile_rows, at]), turn)
+                        residue = 2 * pair + low + 8 * high
+                        moved_ref[residue, rows_at, re_lanes] = re.astype(jnp.bfloat16)
+                        moved_ref[residue, rows_at, im_lanes] = im.astype(jnp.bfloat16)
+
+        halves = half_refs
+        mix_pair(0, halves[0])
+        for pair in range(1, eighth // 2):
+            mix_pair(pair, halves[pair % 2])
+            turn_pair(pair - 1, halves[(pair - 1) % 2])
+        turn_pair(eighth // 2 - 1, halves[(eighth // 2 - 1) % 2])
 
     def load_group(group):
         @pl.when(group > 0)
@@ -487,8 +563,11 @@
             def _():
                 load_group(group)
 
-            for part in range(group_chunks):
+            def one_part(part, innermost):
                 move_rows(group, part, block)
+                return innermost
+
+            lax.fori_loop(0, group_chunks, one_part, 0)
 
             @pl.when(group == 0)
             def _():
@@ -563,26 +642,46 @@
     return np.stack([sign * np.cos(angle), sign * np.sin(angle)], axis=1).reshape(2 * SUB, LANES).astype(np.float32)
 
 
+def mix_kernel(base_ref, sub_ref, turn_ref, mix_ref):
+    x_block = mix_ref.shape[2] // 4
+    highest = lax.Precision.HIGHEST
+    cell = lax.broadcasted_iota(jnp.int32, (x_block, LANES), 1)
+
+    def one_block(block, carry):
+        x_index = lax.broadcasted_iota(jnp.int32, (x_block, LANES), 0) + (base_ref[0] + block * x_block)
+        line_re, line_im = cos_sin_turns(jnp.bitwise_and(x_index * cell, G - 1).astype(jnp.float32) * (1.0 / G))
+        by_re = jnp.dot(line_re, sub_ref[...], precision=highest, preferred_element_type=jnp.float32)
+        by_im = jnp.dot(line_im, sub_ref[...], precision=highest, preferred_element_type=jnp.float32)
+        core = (by_re[:, :LANES] - by_im[:, LANES:], by_re[:, LANES:] + by_im[:, :LANES])
+        for rho in range(4):
+            re, im = times(core, (turn_ref[rho : rho + 1], turn_ref[4 + rho : 5 + rho]))
+            rows_at = pl.ds(rho * x_block, x_block)
+            mix_ref[block, 0, rows_at, :LANES] = re.astype(jnp.bfloat16)
+            mix_ref[block, 0, rows_at, LANES:] = (-im).astype(jnp.bfloat16)
+            mix_ref[block, 1, rows_at, :LANES] = im.astype(jnp.bfloat16)
+            mix_ref[block, 1, rows_at, LANES:] = re.astype(jnp.bfloat16)
+        return carry
+
+    lax.fori_loop(0, mix_ref.shape[0], one_block, 0)
+
+
 def mix_table(x_base, x_count, x_block):
-    highest = lax.Precision.HIGHEST
-    x_index = x_base + jnp.arange(x_count, dtype=jnp.int32)
-    cell = jnp.arange(SUB, dtype=jnp.int32)
-    line_re, line_im = cos_sin_turns((x_index[:, None] * cell[None, :] % G).astype(jnp.float32) * (1.0 / G))
-    cells, pixels = np.arange(SUB)[:, None], np.arange(LANES)[None, :] % SUB
+    cells, pixels = np.arange(LANES)[:, None], np.arange(LANES)[None, :] % SUB
     angle = -2.0 * np.pi * ((cells - SUB // 2) * (pixels - SUB // 2) % SUB) / SUB
-    sub_re, sub_im = jnp.asarray(np.cos(angle), jnp.float32), jnp.asarray(np.sin(angle), jnp.float32)
-    core_re = jnp.dot(line_re, sub_re, precision=highest) - jnp.dot(line_im, sub_im, precision=highest)
-    core_im = jnp.dot(line_re, sub_im, precision=highest) + jnp.dot(line_im, sub_re, precision=highest)
-    blocks = x_count // x_block
-    core_re = core_re.reshape(blocks, 1, x_block, LANES)
-    core_im = core_im.reshape(blocks, 1, x_block, LANES)
+    used = cells < SUB
+    sub = np.concatenate([np.where(used, np.cos(angle), 0.0), np.where(used, np.sin(angle), 0.0)], axis=1)
     turn = (np.arange(4)[:, None] * (np.arange(LANES)[None, :] // SUB)) % 4
-    turn_re = jnp.asarray(np.array([1.0, 0.0, -1.0, 0.0], np.float32)[turn][None, :, None, :])
-    turn_im = jnp.asarray(np.array([0.0, -1.0, 0.0, 1.0], np.float32)[turn][None, :, None, :])
-    re = (core_re * turn_re - core_im * turn_im).astype(jnp.bfloat16)
-    im = (core_re * turn_im + core_im * turn_re).astype(jnp.bfloat16)
-    table = jnp.stack([jnp.concatenate([re, -im], axis=3), jnp.concatenate([im, re], axis=3)], axis=1)
-    return table.reshape(blocks, 2, 4 * x_block, 2 * LANES)
+    turns = np.concatenate([np.array([1.0, 0.0, -1.0, 0.0])[turn], np.array([0.0, -1.0, 0.0, 1.0])[turn]])
+    smem = pl.BlockSpec(memory_space=pltpu.SMEM)
+    vmem = pl.BlockSpec(memory_space=pltpu.VMEM)
+    return pl.pallas_call(
+        mix_kernel,
+        out_shape=jax.ShapeDtypeStruct((x_count // x_block, 2, 4 * x_block, 2 * LANES), jnp.bfloat16),
+        in_specs=[smem, vmem, vmem],
+        out_specs=vmem,
+        cost_estimate=pl.CostEstimate(flops=1 << 30, bytes_accessed=1 << 22, transcendentals=0),
+        name="mix",
+    )(x_base, jnp.asarray(sub, jnp.float32), jnp.asarray(turns, jnp.float32))
 
 
 def image_of(groups, x_base, first, more, rows, cols, mix, x_count, x_block, scale, pol_step):
@@ -601,7 +700,8 @@
             pltpu.VMEM((parts, LANES, 2 * SUB * SUB), jnp.bfloat16),
             pltpu.VMEM((SUB, parts * 2 * LANES, 2 * LANES), jnp.bfloat16),
             pltpu.VMEM((2, x_block, LANES), jnp.float32),
-            pltpu.VMEM((4, 2, 4 * x_block, 2 * LANES), jnp.float32),
+            pltpu.VMEM((2, 4 * x_block, 2 * LANES), jnp.float32),
+            pltpu.VMEM((2, 4 * x_block, 2 * LANES), jnp.float32),
             pltpu.VMEM((SUB, x_block, parts * 2 * LANES), jnp.bfloat16),
             pltpu.VMEM((SUB, x_block, 2 * LANES), jnp.float32),
             pltpu.VMEM((4, 8, 2, 8, LANES), jnp.float32),
@@ -620,29 +720,34 @@
     return lax.ppermute(value, axis, [(i, i ^ distance) for i in range(peers)])
 
 
-def gathered(pieces):
+def gathered(pieces, beside=None):
     slabs = lax.axis_size("slab")
     value = jnp.stack([pieces[0]] + [exchanged(piece, "pol", k) for k, piece in enumerate(pieces) if k])
+    planes = [value] + [exchanged(value, "slab", k) for k in range(2, slabs, 2)]
+    made = None
+    if beside is not None:
+        made = beside(value)
+        planes[-1], made = lax.optimization_barrier((planes[-1], made))
     values = []
-    for k in range(0, slabs, 2):
-        moved = exchanged(value, "slab", k) if k else value
-        values += [moved, exchanged(moved, "slab", 1)]
-    return values
+    for plane in planes:
+        values += [plane, exchanged(plane, "slab", 1)]
+    return values, made
 
 
 def in_image_domain(correlations, tracks, vis_counts, offsets, held_counts, pixel_weight):
     pols, slabs = lax.axis_size("pol"), lax.axis_size("slab")
     pol, slab = lax.axis_index("pol"), lax.axis_index("slab")
     devices = pols * slabs
-    waves = SLOTS // devices
     capacity = SLOTS * slabs // devices
     x_count = G // slabs
-    own_device = pol * slabs + slab
     held = held_counts.astype(jnp.int32)
     holders = jnp.arange(slabs, dtype=jnp.int32)
+    where_at = jnp.stack([slab, pol]).astype(jnp.int32)
+    sent = packed(held, where_at, vis_counts.reshape(1, SLOTS), correlations[:, 0], tracks, devices)
+    slots = lax.all_to_all(sent, ("pol", "slab"), 0, 0, tiled=True)
+    held, _ = lax.optimization_barrier((held, sent))
     before = jnp.sum(jnp.where(holders[None, :] < holders[:, None], held[None, :], 0), axis=1)
     total = jnp.sum(held)
-    own_before = jnp.sum(jnp.where(holders == slab, before, 0))
 
     slot = jnp.arange(SLOTS, dtype=jnp.int32)
     order = jnp.where(slot[None, :] < held[:, None], before[:, None] + slot[None, :], -1).reshape(-1)
@@ -658,53 +763,25 @@
     chosen = spots[:, None] == place[None, :]
     rows = jnp.sum(jnp.where(chosen, offsets[0][None, :], 0), axis=1).reshape(chunk_count, LANES)
     cols = jnp.sum(jnp.where(chosen, offsets[1][None, :], 0), axis=1).reshape(chunk_count, LANES)
-    seats = jnp.arange(capacity, dtype=jnp.int32)
-    mine = (seats[:, None] * devices + own_device) == order[None, :]
-    wave_at = jnp.broadcast_to(holders[:, None] * waves + slot[None, :] // devices, (slabs, SLOTS)).reshape(-1)
-    source = jnp.sum(jnp.where(mine, wave_at[None, :], 0), axis=1)
-    start = jnp.sum(jnp.where(mine, jnp.bitwise_and(offsets[0], SUB - 1)[None, :], 0), axis=1)
-    count = jnp.maximum((total - own_device + devices - 1) // devices, 0).reshape(1)
-
-    visible = jnp.arange(VIS, dtype=jnp.int32)[None, :] < vis_counts[:, None]
-    corr = jnp.where(visible[None], correlations[:, 0].astype(jnp.float32), 0.0)
-    shift = (devices - own_before % devices) % devices
-
-    def sent(value):
-        lead = value.shape[0]
-        value = value.reshape(lead, waves, devices, VIS)
-        value = lax.dynamic_slice_in_dim(jnp.concatenate([value, value], axis=2), shift, devices, 2)
-        return jnp.transpose(value, (2, 1, 0, 3)).reshape(devices, waves * lead * VIS)
-
-    track_piece = waves * 3 * VIS // pols
-    track_part = lax.dynamic_slice_in_dim(sent(tracks), pol * track_piece, track_piece, 1)
-    packed = jnp.concatenate([sent(corr), track_part], axis=1)
-    got = lax.all_to_all(packed, ("pol", "slab"), 0, 0, tiled=True).reshape(pols, slabs, -1)
-    corr_size = waves * 2 * VIS
-    got_corr = jnp.transpose(got[:, :, :corr_size].reshape(pols, slabs, waves, 2, VIS), (1, 2, 3, 0, 4))
-    got_track = jnp.transpose(got[:, :, corr_size:], (1, 0, 2)).reshape(slabs, waves, 3, VIS)
-    slots = jnp.concatenate(
-        [
-            got_corr.reshape(slabs, waves, 2 * pols, VIS),
-            got_track,
-            jnp.zeros((slabs, waves, 16 - 2 * pols - 3, VIS), jnp.float32),
-        ],
-        axis=2,
-    ).reshape(slabs * waves, 16, VIS)
+    slots, rows, cols = lax.optimization_barrier((slots, rows, cols))
     weight_row = pixel_weight.reshape(1, SUB * SUB)
-    *subgrids, extra = subgrids_of(count, pol.reshape(1), source, start, slots, weight_row)
-    first = gathered(subgrids)
+    *pieces, extra = subgrids_of(held, where_at, offsets.astype(jnp.int32), slots, weight_row, capacity)
+    norm_scale = 1.0 / (SUB * SUB * math.sqrt(VIS * SLOTS * slabs / 8.0))
+    x_base = (slab * x_count).reshape(1)
+    x_block = min(x_count, 256)
+
+    def mixed(after):
+        base, _ = lax.optimization_barrier((x_base, after))
+        return mix_table(base, x_count, x_block)
+
+    first, mix = gathered(pieces, mixed)
     many = total > devices * GROUP
     more = lax.cond(
         many,
-        lambda: jnp.stack(gathered([extra[k] for k in range(pols)])),
+        lambda: jnp.stack(gathered([extra[k] for k in range(pols)])[0]),
         lambda: jnp.zeros((slabs,) + extra.shape, extra.dtype),
     )
     groups = jnp.where(many, capacity // GROUP, 1).reshape(1)
-    norm_scale = 1.0 / (SUB * SUB * math.sqrt(VIS * SLOTS * slabs / 8.0))
-    x_base = (slab * x_count).reshape(1)
-    x_block = min(x_count, 256)
-    mix_base, _ = lax.optimization_barrier((x_base, subgrids[0]))
-    mix = mix_table(mix_base[0], x_count, x_block)
     sky = image_of(groups, x_base, first, more, rows, cols, mix, x_count, x_block, norm_scale, pol_step)
     return sky[:, None]
 
@@ -713,7 +790,7 @@
     pols, slabs = mesh.shape["pol"], mesh.shape["slab"]
     devices = pols * slabs
     whole = slabs & (slabs - 1) == 0 and slabs * GROUP <= LANES and SLOTS * slabs == 2 * GROUP * devices
-    return whole and pols == 4 and SLOTS % devices == 0 and pols % (LANES // (GROUP * slabs)) == 0
+    return whole and pols == 4 and SLOTS == WAVES * devices and pols % (LANES // (GROUP * slabs)) == 0
 
 
 def solution(mesh):

time: 91 us -> 79.9 us (0.88)
  other arithmetic: 10.1 us -> 5.19 us
  between operations: 3.74 us -> 0.74 us
  matrix products: 2.58 us -> 0 us
  local copies, waits for them, and re-layouts: 6.89 us -> 4.69 us
  Pallas kernels: 40.1 us -> 42.1 us
    pallas_call x0 -> x2, Pallas kernels: none -> 5.97 us  [the longest x1 3.97 us: mix_table(): pl.pallas_call(mix_kernel, out_shape=jax.ShapeDtypeStruct((x_count // x_b...]
    all_to_all x1, waiting for transfers between devices: 1.37 us -> 5.3 us  [in_image_domain(): slots = lax.all_to_all(sent, ('pol', 'slab'), 0, 0, tiled=True)]
    ppermute x10, waiting for transfers between devices: 8.98 us -> 5.5 us  [exchanged(): return lax.ppermute(value, axis, [(i, i ^ distance) for i in range(peers)])]
    dot_general x4 -> x0, matrix products: 2.58 us -> none  [the longest x1 0.65 us: mix_table(): jnp.dot(line_im, sub_im, precision=highest)]
    pallas_call x1, Pallas kernels: 29.2 us -> 26.9 us  [image_of(): pl.pallas_call(functools.partial(image_kernel, pol_step, x_block, slabs),...]
    pallas_call x1, Pallas kernels: 10.9 us -> 9.24 us  [subgrids_of(): pl.pallas_call(subgrid_kernel, out_shape=[jax.ShapeDtypeStruct((GROUP, 2...]
    reshape x4 -> x0, local copies, waits for them, and re-layouts: 1.4 us -> none  [the longest x1 1.07 us: sent(): value = value.reshape(lead, waves, devices, VIS)]
    reduce_sum x2 -> x0, other arithmetic: 1.3 us -> none  [the longest x1 0.67 us: in_image_domain(): jnp.sum(jnp.where(mine, jnp.bitwise_and(offsets[0], SUB - 1)[None, :], 0)...]
  transfers between devices with their start and end apart: 11 -> 11, of which waited for: 3 -> 6; matrix products, arithmetic and copies ran while one was open for 13% -> 9% of each run, Pallas kernels for 0% -> 5%
where the time goes in v2:
time: 79.9 us; the launch traced here: 79.4 us
  Pallas kernels  42.1 us (53%)
  starting transfers between devices  15.8 us (20%)
  waiting for transfers between devices  10.8 us (14%)
  other arithmetic  5.19 us (6%)
  local copies, waits for them, and re-layouts  4.69 us (6%)
    pallas_call x1, Pallas kernels, image_of(): pl.pallas_call(functools.partial(image_kernel, pol_step, x_block, slabs),...  26.9 us
    pallas_call x1, Pallas kernels, subgrids_of(): pl.pallas_call(subgrid_kernel, out_shape=[jax.ShapeDtypeStruct((GROUP, 2...  9.24 us
    ppermute x10, starting transfers between devices, exchanged(): return lax.ppermute(value, axis, [(i, i ^ distance) for i in range(peers)])  8.52 us
    all_to_all x1, starting transfers between devices, in_image_domain(): slots = lax.all_to_all(sent, ('pol', 'slab'), 0, 0, tiled=True)  7.33 us
    ppermute x10, waiting for transfers between devices, exchanged(): return lax.ppermute(value, axis, [(i, i ^ distance) for i in range(peers)])  5.5 us
    all_to_all x1, waiting for transfers between devices, in_image_domain(): slots = lax.all_to_all(sent, ('pol', 'slab'), 0, 0, tiled=True)  5.3 us
    pallas_call x1, Pallas kernels, mix_table(): pl.pallas_call(mix_kernel, out_shape=jax.ShapeDtypeStruct((x_count // x_b...  3.97 us
    pallas_call x1, Pallas kernels, packed(): pl.pallas_call(pack_kernel, out_shape=jax.ShapeDtypeStruct((devices, 16,...  2 us
  transfers between devices with their start and end apart: 11, of which 6 were waited for; matrix products, arithmetic and copies ran while one was open for 9% of the time, Pallas kernels for 5%

profile of v2, /device:TPU:0, one launch (start us, length us, event | category | flops | bytes accessed | tf_op | source)
XLA Modules:
  0.0 79.4 jit_solution(11686459020464335494)
XLA Ops:
  0.0 0.7 pad_add_fusion.place_ref
  0.7 2.0 %packed.1 = f32[32,16,128]{2,1,0:T(8,128)} custom-call(s32[8]{0:T(128)} %held_counts_ref, s32[2]{0:T(128)} %pad_add_fusion.place_ref, s32[1,64]{1,0:T(1,128)} %bitcast.57, bf16[2,64,256]{2,1,0:T(8,128)(2,1)} %bitcast.48, f32[3,64,256]{2,1,0:T(8,128)} %track_ref.1), custom_call_target="tpu_custom_call" | custom-call | tf_op jit(solution)/shard_map/packed/pallas_call | solution.py:340
  2.7 7.3 %all-to-all-start = ((f32[32,16,128]{2,1,0:T(8,128)}), f32[32,16,128]{2,1,0:T(8,128)S(1)}, u32[]{:S(2)}, u32[]{:S(2)}) async-start(f32[32,16,128]{2,1,0:T(8,128)} %packed.1), calls=%async_computation | async-start | bytes 524288 | tf_op jit(solution)/shard_map/all_to_all | solution.py:747
  10.0 1.4 %reshape.170.weight_ref = f32[1,1024]{1,0:T(1,128)} reshape(f32[32,32]{1,0:T(8,128)} %param.18) | data formatting | bytes 8192 | tf_op jit(solution)/shard_map/reshape | solution.py:767
  11.4 0.8 select_reduce_fusion.2
  12.1 0.7 add_select_fusion
  12.9 0.1 select_n.103
  13.0 0.8 fusion.20
  13.8 0.9 %select_reduce_fusion = (s32[512]{0:T(512)}, s32[512]{0:T(512)}) fusion(s32[512]{0:T(512)S(1)} %bitcast.56, s32[512]{0:T(512)S(1)} %fusion.18, s32[512]{0:T(512)S(1)} %bitcast.55), kind=kLoop, calls=%fused_computation.12 | loop fusion | flops 1309696 | bytes 10240 | tf_op jit(solution)/shard_map/reduce_sum | solution.py:765
  14.7 5.3 %all-to-all-done.slots_ref = f32[32,16,128]{2,1,0:T(8,128)S(1)} async-done(((f32[32,16,128]{2,1,0:T(8,128)}), f32[32,16,128]{2,1,0:T(8,128)S(1)}, u32[]{:S(2)}, u32[]{:S(2)}) %all-to-all-start) | async-done | bytes 262176 | tf_op jit(solution)/shard_map/all_to_all | solution.py:747
  20.0 0.7 copy-done
  20.7 9.2 %subgrids.1 = (bf16[8,2048]{1,0:T(8,128)(2,1)}, bf16[8,2048]{1,0:T(8,128)(2,1)}, bf16[8,2048]{1,0:T(8,128)(2,1)}, bf16[8,2048]{1,0:T(8,128)(2,1)}, bf16[4,8,2048]{2,1,0:T(8,128)(2,1)S(1)}) custom-call(s32[8]{0:T(128)} %held_counts_ref, s32[2]{0:T(128)} %pad_add_fusion.place_ref, s32[2,512]{1,0:T(2,128)} %offsets_ref.1, f32[32,16,128]{2,1,0:T(8,128)} %copy-done, ...), custom_call_target="tpu_custom_call" | custom-call | tf_op jit(solution)/shard_map/subgrids/pallas_call | solution.py:442
  29.9 0.9 %collective-permute-start.10 = (bf16[8,2048]{1,0:T(8,128)(2,1)}, bf16[8,2048]{1,0:T(8,128)(2,1)S(1)}, u32[]{:S(2)}, u32[]{:S(2)}) collective-permute-start(bf16[8,2048]{1,0:T(8,128)(2,1)} %get-tuple-element.26), channel_id=1, source_target_pairs={{0,8},{8,0},{16,24},{24,16},{1,9},{9,1},{17,25},{25,17},{2,10},{10... | collective-permute-start | bytes 98312 | tf_op jit(solution)/shard_map/ppermute | solution.py:720
  30.8 0.0 collective-permute-start.11
  30.8 2.6 %collective-permute-start.12 = (bf16[8,2048]{1,0:T(8,128)(2,1)}, bf16[8,2048]{1,0:T(8,128)(2,1)S(1)}, u32[]{:S(2)}, u32[]{:S(2)}) collective-permute-start(bf16[8,2048]{1,0:T(8,128)(2,1)} %get-tuple-element.28), channel_id=1, source_target_pairs={{0,24},{8,16},{16,8},{24,0},{1,25},{9,17},{17,9},{25,1},{2,26},{10... | collective-permute-start | bytes 98312 | tf_op jit(solution)/shard_map/ppermute | solution.py:720
  33.4 1.3 %reduce_sum.36 = s32[]{:T(128)} reduce(s32[8]{0:T(128)} %held_counts_ref, s32[]{:T(128)} %constant.98.clone.1), dimensions={0}, to_apply=%region_0.1 | reduce | flops 7 | bytes 40 | tf_op jit(solution)/shard_map/reduce_sum | solution.py:750
  35.4 0.0 collective-permute-done.10
  35.4 0.0 collective-permute-done.11
  35.4 0.4 collective-permute-done.12
  35.8 0.8 pad_maximum_fusion.1.refs_0_
  36.6 0.0 copy-start.1
  36.6 1.4 %collective-permute-start.13 = (bf16[4,8,2048]{2,1,0:T(8,128)(2,1)S(1)}, bf16[4,8,2048]{2,1,0:T(8,128)(2,1)S(1)}, u32[]{:S(2)}, u32[]{:S(2)}) collective-permute-start(bf16[4,8,2048]{2,1,0:T(8,128)(2,1)S(1)} %pad_maximum_fusion.1.refs_0_), channel_id=1, source_target_pairs={{0,6},{1,7},{2,4},{3,5},{4,2},{5,3},{6,0},{7,1},{8,14},{9,15},{10,... | collective-permute-start | bytes 393224 | tf_op jit(solution)/shard_map/ppermute | solution.py:720
  38.0 1.1 %conditional.1 = (bf16[8,4,8,2048]{3,2,1,0:T(8,128)(2,1)}) conditional(s32[]{:T(128)} %convert_element_type.3, () %tuple.19, bf16[4,8,2048]{2,1,0:T(8,128)(2,1)S(1)} %get-tuple-element.32), branch_computations={%region_4.5_spmd, %region_5.6_spmd} | conditional | flops 720895 | bytes 6685080 | solution.py:779
  38.0 1.1 %broadcast.257 = bf16[8,4,8,2048]{3,2,1,0:T(8,128)(2,1)} broadcast(bf16[]{:T(256)} %constant.95.clone), dimensions={} | broadcast | bytes 1048578 | tf_op jit(solution)/shard_map/broadcast.3
  39.1 0.6 collective-permute-start.17
  39.7 2.5 %collective-permute-start.15 = (bf16[4,8,2048]{2,1,0:T(8,128)(2,1)S(1)}, bf16[4,8,2048]{2,1,0:T(8,128)(2,1)S(1)}, u32[]{:S(2)}, u32[]{:S(2)}) collective-permute-start(bf16[4,8,2048]{2,1,0:T(8,128)(2,1)S(1)} %pad_maximum_fusion.1.refs_0_), channel_id=1, source_target_pairs={{0,2},{1,3},{2,0},{3,1},{4,6},{5,7},{6,4},{7,5},{8,10},{9,11},{10,... | collective-permute-start | bytes 393224 | tf_op jit(solution)/shard_map/ppermute | solution.py:720
  42.2 0.0 collective-permute-start.14
  42.2 4.0 %mix.1.mix_ref = bf16[2,2,1024,256]{3,2,1,0:T(8,128)(2,1)} custom-call(s32[1]{0:T(128)} %bitcast.19.base_ref, f32[128,256]{1,0:T(8,128)} %constant.114.clone.sub_ref, f32[8,128]{1,0:T(8,128)} %constant.115.clone.turn_ref), custom_call_target="tpu_custom_call" | custom-call | flops 1073741824 | bytes 4194304 | tf_op jit(solution)/shard_map/mix/pallas_call | solution.py:677
  46.2 0.0 collective-permute-done.13.refs_6_
  46.2 3.8 %collective-permute-done.17.refs_4_ = bf16[4,8,2048]{2,1,0:T(8,128)(2,1)S(1)} collective-permute-done((bf16[4,8,2048]{2,1,0:T(8,128)(2,1)S(1)}, bf16[4,8,2048]{2,1,0:T(8,128)(2,1)S(1)}, u32[]{:S(2)}, u32[]{:S(2)}) %collective-permute-start.17) | collective-permute-done | bytes 131104 | tf_op jit(solution)/shard_map/ppermute | solution.py:720
  50.0 0.0 collective-permute-start.18
  50.0 0.0 collective-permute-done.15.refs_2_
  50.0 0.0 copy-start.4
  50.0 0.5 collective-permute-start.16
  50.5 0.1 collective-permute-start.19
  50.6 0.0 collective-permute-done.14.refs_1_
  50.6 0.7 collective-permute-done.18.refs_5_
  51.3 0.2 collective-permute-done.16.refs_3_
  51.5 0.3 collective-permute-done.19.refs_7_
  51.8 0.0 copy-done.1
  51.8 0.0 copy-done.2
  51.8 0.0 copy-done.3
  51.8 0.0 copy-done.4
  51.8 0.0 copy-done.5
  51.9 0.1 copy-done.6
  52.0 0.2 copy-done.7
  52.1 0.3 copy-done.8
  52.5 26.9 %image.1 = f32[2,512,4096]{2,1,0:T(8,128)} custom-call(s32[1]{0:T(128)} %bitcast.18.groups_ref, s32[1]{0:T(128)} %bitcast.19.base_ref, s32[4,128]{1,0:T(4,128)} %bitcast.54, s32[4,128]{1,0:T(4,128)} %bitcast.53, bf16[2,2,1024,256]{3,2,1,0:T(8,128)(2,1)} %mix.1.mix_ref, f32[64,128]{1,0:T(8,128)} %constant.116.clone.twist_ref, bf16[4,8,2048]{2,1,0:T(8,128)(2,1)} %copy-done.1, ...), custom_call_target="tpu_custom_call" | custom-call | tf_op jit(solution)/shard_map/image/pallas_call | solution.py:694
  (8 shorter events, 0.0 us)
Async XLA Ops:
  2.7 17.3 %all-to-all-start = ((f32[32,16,128]{2,1,0:T(8,128)}), f32[32,16,128]{2,1,0:T(8,128)S(1)}, u32[]{:S(2)}, u32[]{:S(2)}) async-start(f32[32,16,128]{2,1,0:T(8,128)} %packed.1), calls=%async_computation | async-start | bytes 524288 | tf_op jit(solution)/shard_map/all_to_all | solution.py:747
  20.0 0.7 copy-start
  29.9 5.4 %collective-permute-start.10 = (bf16[8,2048]{1,0:T(8,128)(2,1)}, bf16[8,2048]{1,0:T(8,128)(2,1)S(1)}, u32[]{:S(2)}, u32[]{:S(2)}) collective-permute-start(bf16[8,2048]{1,0:T(8,128)(2,1)} %get-tuple-element.26), channel_id=1, source_target_pairs={{0,8},{8,0},{16,24},{24,16},{1,9},{9,1},{17,25},{25,17},{2,10},{10... | collective-permute-start | bytes 98312 | tf_op jit(solution)/shard_map/ppermute | solution.py:720
  30.8 4.6 %collective-permute-start.11 = (bf16[8,2048]{1,0:T(8,128)(2,1)}, bf16[8,2048]{1,0:T(8,128)(2,1)S(1)}, u32[]{:S(2)}, u32[]{:S(2)}) collective-permute-start(bf16[8,2048]{1,0:T(8,128)(2,1)} %get-tuple-element.27), channel_id=1, source_target_pairs={{0,16},{8,24},{16,0},{24,8},{1,17},{9,25},{17,1},{25,9},{2,18},{10... | collective-permute-start | bytes 98312 | tf_op jit(solution)/shard_map/ppermute | solution.py:720
  30.8 5.0 %collective-permute-start.12 = (bf16[8,2048]{1,0:T(8,128)(2,1)}, bf16[8,2048]{1,0:T(8,128)(2,1)S(1)}, u32[]{:S(2)}, u32[]{:S(2)}) collective-permute-start(bf16[8,2048]{1,0:T(8,128)(2,1)} %get-tuple-element.28), channel_id=1, source_target_pairs={{0,24},{8,16},{16,8},{24,0},{1,25},{9,17},{17,9},{25,1},{2,26},{10... | collective-permute-start | bytes 98312 | tf_op jit(solution)/shard_map/ppermute | solution.py:720
  36.6 15.2 %copy-start.1 = (bf16[4,8,2048]{2,1,0:T(8,128)(2,1)}, bf16[4,8,2048]{2,1,0:T(8,128)(2,1)S(1)}, u32[]{:S(2)}) copy-start(bf16[4,8,2048]{2,1,0:T(8,128)(2,1)S(1)} %pad_maximum_fusion.1.refs_0_) | copy-start | bytes 393220
  36.6 9.5 %collective-permute-start.13 = (bf16[4,8,2048]{2,1,0:T(8,128)(2,1)S(1)}, bf16[4,8,2048]{2,1,0:T(8,128)(2,1)S(1)}, u32[]{:S(2)}, u32[]{:S(2)}) collective-permute-start(bf16[4,8,2048]{2,1,0:T(8,128)(2,1)S(1)} %pad_maximum_fusion.1.refs_0_), channel_id=1, source_target_pairs={{0,6},{1,7},{2,4},{3,5},{4,2},{5,3},{6,0},{7,1},{8,14},{9,15},{10,... | collective-permute-start | bytes 393224 | tf_op jit(solution)/shard_map/ppermute | solution.py:720
  39.1 10.9 %collective-permute-start.17 = (bf16[4,8,2048]{2,1,0:T(8,128)(2,1)S(1)}, bf16[4,8,2048]{2,1,0:T(8,128)(2,1)S(1)}, u32[]{:S(2)}, u32[]{:S(2)}) collective-permute-start(bf16[4,8,2048]{2,1,0:T(8,128)(2,1)S(1)} %pad_maximum_fusion.1.refs_0_), channel_id=1, source_target_pairs={{0,4},{1,5},{2,6},{3,7},{4,0},{5,1},{6,2},{7,3},{8,12},{9,13},{10,... | collective-permute-start | bytes 393224 | tf_op jit(solution)/shard_map/ppermute | solution.py:720
  39.7 10.3 %collective-permute-start.15 = (bf16[4,8,2048]{2,1,0:T(8,128)(2,1)S(1)}, bf16[4,8,2048]{2,1,0:T(8,128)(2,1)S(1)}, u32[]{:S(2)}, u32[]{:S(2)}) collective-permute-start(bf16[4,8,2048]{2,1,0:T(8,128)(2,1)S(1)} %pad_maximum_fusion.1.refs_0_), channel_id=1, source_target_pairs={{0,2},{1,3},{2,0},{3,1},{4,6},{5,7},{6,4},{7,5},{8,10},{9,11},{10,... | collective-permute-start | bytes 393224 | tf_op jit(solution)/shard_map/ppermute | solution.py:720
  42.2 8.4 %collective-permute-start.14 = (bf16[4,8,2048]{2,1,0:T(8,128)(2,1)S(1)}, bf16[4,8,2048]{2,1,0:T(8,128)(2,1)S(1)}, u32[]{:S(2)}, u32[]{:S(2)}) collective-permute-start(bf16[4,8,2048]{2,1,0:T(8,128)(2,1)S(1)} %pad_maximum_fusion.1.refs_0_), channel_id=1, source_target_pairs={{0,1},{1,0},{2,3},{3,2},{4,5},{5,4},{6,7},{7,6},{8,9},{9,8},{10,11... | collective-permute-start | bytes 393224 | tf_op jit(solution)/shard_map/ppermute | solution.py:720
  46.2 5.7 %copy-start.2 = (bf16[4,8,2048]{2,1,0:T(8,128)(2,1)}, bf16[4,8,2048]{2,1,0:T(8,128)(2,1)S(1)}, u32[]{:S(2)}) copy-start(bf16[4,8,2048]{2,1,0:T(8,128)(2,1)S(1)} %collective-permute-done.13.refs_6_) | copy-start | bytes 393220
  50.0 1.9 %copy-start.3 = (bf16[4,8,2048]{2,1,0:T(8,128)(2,1)}, bf16[4,8,2048]{2,1,0:T(8,128)(2,1)S(1)}, u32[]{:S(2)}) copy-start(bf16[4,8,2048]{2,1,0:T(8,128)(2,1)S(1)} %collective-permute-done.17.refs_4_) | copy-start | bytes 393220
  50.0 1.3 %collective-permute-start.18 = (bf16[4,8,2048]{2,1,0:T(8,128)(2,1)S(1)}, bf16[4,8,2048]{2,1,0:T(8,128)(2,1)S(1)}, u32[]{:S(2)}, u32[]{:S(2)}) collective-permute-start(bf16[4,8,2048]{2,1,0:T(8,128)(2,1)S(1)} %collective-permute-done.17.refs_4_), channel_id=1, source_target_pairs={{0,1},{1,0},{2,3},{3,2},{4,5},{5,4},{6,7},{7,6},{8,9},{9,8},{10,11... | collective-permute-start | bytes 393224 | tf_op jit(solution)/shard_map/ppermute | solution.py:720
  50.0 1.9 %copy-start.4 = (bf16[4,8,2048]{2,1,0:T(8,128)(2,1)}, bf16[4,8,2048]{2,1,0:T(8,128)(2,1)S(1)}, u32[]{:S(2)}) copy-start(bf16[4,8,2048]{2,1,0:T(8,128)(2,1)S(1)} %collective-permute-done.15.refs_2_) | copy-start | bytes 393220
  50.0 1.5 %collective-permute-start.16 = (bf16[4,8,2048]{2,1,0:T(8,128)(2,1)S(1)}, bf16[4,8,2048]{2,1,0:T(8,128)(2,1)S(1)}, u32[]{:S(2)}, u32[]{:S(2)}) collective-permute-start(bf16[4,8,2048]{2,1,0:T(8,128)(2,1)S(1)} %collective-permute-done.15.refs_2_), channel_id=1, source_target_pairs={{0,1},{1,0},{2,3},{3,2},{4,5},{5,4},{6,7},{7,6},{8,9},{9,8},{10,11... | collective-permute-start | bytes 393224 | tf_op jit(solution)/shard_map/ppermute | solution.py:720
  50.5 1.3 %collective-permute-start.19 = (bf16[4,8,2048]{2,1,0:T(8,128)(2,1)S(1)}, bf16[4,8,2048]{2,1,0:T(8,128)(2,1)S(1)}, u32[]{:S(2)}, u32[]{:S(2)}) collective-permute-start(bf16[4,8,2048]{2,1,0:T(8,128)(2,1)S(1)} %collective-permute-done.13.refs_6_), channel_id=1, source_target_pairs={{0,1},{1,0},{2,3},{3,2},{4,5},{5,4},{6,7},{7,6},{8,9},{9,8},{10,11... | collective-permute-start | bytes 393224 | tf_op jit(solution)/shard_map/ppermute | solution.py:720
  50.6 1.3 %copy-start.5 = (bf16[4,8,2048]{2,1,0:T(8,128)(2,1)}, bf16[4,8,2048]{2,1,0:T(8,128)(2,1)S(1)}, u32[]{:S(2)}) copy-start(bf16[4,8,2048]{2,1,0:T(8,128)(2,1)S(1)} %collective-permute-done.14.refs_1_) | copy-start | bytes 393220
  51.3 0.7 copy-start.6
  51.5 0.6 copy-start.7
  51.8 0.7 copy-start.8

commit v3 on v2

--- a/solution.py
+++ b/solution.py
@@ -476,8 +476,9 @@
 
         def one_phase(residue, inner):
             carried = low > residue
-            re = jnp.where(carried, later[0], here[0]).astype(jnp.bfloat16)
-            im = jnp.where(carried, later[1], here[1])
+            twist = (twist_ref[pl.ds(2 * residue, 1)], twist_ref[pl.ds(2 * residue + 1, 1)])
+            re, im = times((jnp.where(carried, later[0], here[0]), jnp.where(carried, later[1], here[1])), twist)
+            re = re.astype(jnp.bfloat16)
             phase_ref[residue, re_rows, :LANES] = re
             phase_ref[residue, re_rows, LANES:] = im.astype(jnp.bfloat16)
             phase_ref[residue, im_rows, :LANES] = (-im).astype(jnp.bfloat16)
@@ -577,7 +578,7 @@
                     )
                     return innermost
 
-                lax.fori_loop(0, SUB, one_residue, 0, unroll=4)
+                lax.fori_loop(0, SUB, one_residue, 0, unroll=16)
 
             @pl.when(group > 0)
             def _():
@@ -604,9 +605,7 @@
                     parts = []
                     for first in range(8):
                         residue = 4 * first + second
-                        value = (sum_ref[residue, rows_at, :LANES], sum_ref[residue, rows_at, LANES:])
-                        twist = (twist_ref[2 * residue : 2 * residue + 1], twist_ref[2 * residue + 1 : 2 * residue + 2])
-                        parts.append(times(value, twist))
+                        parts.append((sum_ref[residue, rows_at, :LANES], sum_ref[residue, rows_at, LANES:]))
                     for first, value in enumerate(dft_8(parts, 1)):
                         if first * second:
                             angle = TWO_PI * first * second / SUB
@@ -710,7 +709,7 @@
             pltpu.SemaphoreType.DMA((x_block // out_rows,)),
             pltpu.SemaphoreType.DMA,
         ],
-        compiler_params=pltpu.CompilerParams(vmem_limit_bytes=60 * 1024 * 1024),
+        compiler_params=pltpu.CompilerParams(vmem_limit_bytes=46 * 1024 * 1024),
         name="image",
     )(groups, x_base, rows, cols, mix, jnp.asarray(twist_table(scale)), *first, more)
 

time: 79.9 us -> 77.1 us (0.965); the launches traced: 79.4 us -> 75.6 us
  Pallas kernels: 42.1 us -> 36.7 us
  local copies, waits for them, and re-layouts: 4.69 us -> 6.39 us
    pallas_call x1, Pallas kernels: 26.9 us -> 22.9 us  [image_of(): pl.pallas_call(functools.partial(image_kernel, pol_step, x_block, slabs),...]
    unnamed x18 -> x6, local copies, waits for them, and re-layouts: 1.35 us -> 3.05 us
    pallas_call x1, Pallas kernels: 9.24 us -> 7.8 us  [subgrids_of(): pl.pallas_call(subgrid_kernel, out_shape=[jax.ShapeDtypeStruct((GROUP, 2...]
where the time goes in v3:
time: 77.1 us; the launch traced here: 75.6 us
  Pallas kernels  36.7 us (48%)
  starting transfers between devices  15.8 us (20%)
  waiting for transfers between devices  11.5 us (15%)
  local copies, waits for them, and re-layouts  6.39 us (8%)
  other arithmetic  4.6 us (6%)
    pallas_call x1, Pallas kernels, image_of(): pl.pallas_call(functools.partial(image_kernel, pol_step, x_block, slabs),...  22.9 us
    ppermute x10, starting transfers between devices, exchanged(): return lax.ppermute(value, axis, [(i, i ^ distance) for i in range(peers)])  8.46 us
    pallas_call x1, Pallas kernels, subgrids_of(): pl.pallas_call(subgrid_kernel, out_shape=[jax.ShapeDtypeStruct((GROUP, 2...  7.8 us
    all_to_all x1, starting transfers between devices, in_image_domain(): slots = lax.all_to_all(sent, ('pol', 'slab'), 0, 0, tiled=True)  7.33 us
    all_to_all x1, waiting for transfers between devices, in_image_domain(): slots = lax.all_to_all(sent, ('pol', 'slab'), 0, 0, tiled=True)  5.87 us
    ppermute x10, waiting for transfers between devices, exchanged(): return lax.ppermute(value, axis, [(i, i ^ distance) for i in range(peers)])  5.62 us
    pallas_call x1, Pallas kernels, mix_table(): pl.pallas_call(mix_kernel, out_shape=jax.ShapeDtypeStruct((x_count // x_b...  3.95 us
    unnamed x6, local copies, waits for them, and re-layouts  3.05 us
  transfers between devices with their start and end apart: 11, of which 6 were waited for; matrix products, arithmetic and copies ran while one was open for 9% of the time, Pallas kernels for 5%

profile of v3, /device:TPU:0, one launch (start us, length us, event | category | flops | bytes accessed | tf_op | source)
XLA Modules:
  0.0 75.6 jit_solution(1343394631104596928)
XLA Ops:
  0.0 0.6 pad_add_fusion.place_ref
  0.6 2.0 %packed.1 = f32[32,16,128]{2,1,0:T(8,128)} custom-call(s32[8]{0:T(128)} %held_counts_ref, s32[2]{0:T(128)} %pad_add_fusion.place_ref, s32[1,64]{1,0:T(1,128)} %bitcast.57, bf16[2,64,256]{2,1,0:T(8,128)(2,1)} %bitcast.50, f32[3,64,256]{2,1,0:T(8,128)} %track_ref.1), custom_call_target="tpu_custom_call" | custom-call | tf_op jit(solution)/shard_map/packed/pallas_call | solution.py:340
  2.7 7.3 %all-to-all-start = ((f32[32,16,128]{2,1,0:T(8,128)}), f32[32,16,128]{2,1,0:T(8,128)S(1)}, u32[]{:S(2)}, u32[]{:S(2)}) async-start(f32[32,16,128]{2,1,0:T(8,128)} %packed.1), calls=%async_computation | async-start | bytes 524288 | tf_op jit(solution)/shard_map/all_to_all | solution.py:746
  10.0 1.4 %reshape.170.weight_ref = f32[1,1024]{1,0:T(1,128)} reshape(f32[32,32]{1,0:T(8,128)} %param.18) | data formatting | bytes 8192 | tf_op jit(solution)/shard_map/reshape | solution.py:766
  11.4 0.8 %select_reduce_fusion.2 = s32[8]{0:T(128)S(1)} fusion(s32[8]{0:T(128)} %held_counts_ref), kind=kLoop, calls=%fused_computation.17 | loop fusion | flops 184 | bytes 64 | tf_op jit(solution)/shard_map/reduce_sum | solution.py:748
  12.1 0.7 add_select_fusion
  12.9 0.1 select_n.103
  13.0 0.8 %fusion.20 = (s32[1,512]{1,0:T(1,128)S(1)}, s32[1,512]{1,0:T(1,128)S(1)}) fusion(s32[2,512]{1,0:T(2,128)} %offsets_ref.1), kind=kLoop, calls=%fused_computation.65 | loop fusion | bytes 8192 | tf_op jit(solution)/shard_map/slice | solution.py:763
  13.8 0.4 select_reduce_fusion
  14.1 5.9 %all-to-all-done.slots_ref = f32[32,16,128]{2,1,0:T(8,128)S(1)} async-done(((f32[32,16,128]{2,1,0:T(8,128)}), f32[32,16,128]{2,1,0:T(8,128)S(1)}, u32[]{:S(2)}, u32[]{:S(2)}) %all-to-all-start) | async-done | bytes 262176 | tf_op jit(solution)/shard_map/all_to_all | solution.py:746
  20.0 0.0 copy-start.2
  20.0 0.7 copy-done.2
  20.7 7.8 %subgrids.1 = (bf16[8,2048]{1,0:T(8,128)(2,1)}, bf16[8,2048]{1,0:T(8,128)(2,1)}, bf16[8,2048]{1,0:T(8,128)(2,1)}, bf16[8,2048]{1,0:T(8,128)(2,1)}, bf16[4,8,2048]{2,1,0:T(8,128)(2,1)S(1)}) custom-call(s32[8]{0:T(128)} %held_counts_ref, s32[2]{0:T(128)} %pad_add_fusion.place_ref, s32[2,512]{1,0:T(2,128)} %offsets_ref.1, f32[32,16,128]{2,1,0:T(8,128)} %copy-done.2, ...), custom_call_target="tpu_custom_call" | custom-call | tf_op jit(solution)/shard_map/subgrids/pallas_call | solution.py:442
  28.5 0.9 %collective-permute-start.10 = (bf16[8,2048]{1,0:T(8,128)(2,1)}, bf16[8,2048]{1,0:T(8,128)(2,1)S(1)}, u32[]{:S(2)}, u32[]{:S(2)}) collective-permute-start(bf16[8,2048]{1,0:T(8,128)(2,1)} %get-tuple-element.26), channel_id=1, source_target_pairs={{0,8},{8,0},{16,24},{24,16},{1,9},{9,1},{17,25},{25,17},{2,10},{10... | collective-permute-start | bytes 98312 | tf_op jit(solution)/shard_map/ppermute | solution.py:719
  29.3 0.0 collective-permute-start.11
  29.4 2.6 %collective-permute-start.12 = (bf16[8,2048]{1,0:T(8,128)(2,1)}, bf16[8,2048]{1,0:T(8,128)(2,1)S(1)}, u32[]{:S(2)}, u32[]{:S(2)}) collective-permute-start(bf16[8,2048]{1,0:T(8,128)(2,1)} %get-tuple-element.28), channel_id=1, source_target_pairs={{0,24},{8,16},{16,8},{24,0},{1,25},{9,17},{17,9},{25,1},{2,26},{10... | collective-permute-start | bytes 98312 | tf_op jit(solution)/shard_map/ppermute | solution.py:719
  32.0 1.3 %reduce_sum.36 = s32[]{:T(128)} reduce(s32[8]{0:T(128)} %held_counts_ref, s32[]{:T(128)} %constant.98.clone.1), dimensions={0}, to_apply=%region_0.1 | reduce | flops 7 | bytes 40 | tf_op jit(solution)/shard_map/reduce_sum | solution.py:749
  33.9 0.0 collective-permute-done.10
  33.9 0.0 collective-permute-done.11
  33.9 0.5 collective-permute-done.12
  34.4 0.8 %pad_maximum_fusion.1.refs_0_ = bf16[4,8,2048]{2,1,0:T(8,128)(2,1)S(1)} fusion(bf16[1,8,2048]{2,1,0:T(8,128)(2,1)S(1)} %bitcast.54, bf16[1,8,2048]{2,1,0:T(8,128)(2,1)S(1)} %bitcast.53, bf16[1,8,2048]{2,1,0:T(8,128)(2,1)S(1)} %bitcast.52, bf16[1,8,2048]{2,1,0:T(8,128)(2,1)} %bitcast.51), kind=kLoop, calls=%fused_computation.15 | loop fusion | flops 196608 | bytes 262144 | tf_op jit(solution)/shard_map/stack | solution.py:724
  35.2 1.3 %collective-permute-start.13 = (bf16[4,8,2048]{2,1,0:T(8,128)(2,1)S(1)}, bf16[4,8,2048]{2,1,0:T(8,128)(2,1)S(1)}, u32[]{:S(2)}, u32[]{:S(2)}) collective-permute-start(bf16[4,8,2048]{2,1,0:T(8,128)(2,1)S(1)} %pad_maximum_fusion.1.refs_0_), channel_id=1, source_target_pairs={{0,6},{1,7},{2,4},{3,5},{4,2},{5,3},{6,0},{7,1},{8,14},{9,15},{10,... | collective-permute-start | bytes 393224 | tf_op jit(solution)/shard_map/ppermute | solution.py:719
  36.5 1.1 %conditional.1 = (bf16[8,4,8,2048]{3,2,1,0:T(8,128)(2,1)}) conditional(s32[]{:T(128)} %convert_element_type.3, () %tuple.19, bf16[4,8,2048]{2,1,0:T(8,128)(2,1)S(1)} %get-tuple-element.32), branch_computations={%region_4.5_spmd, %region_5.6_spmd} | conditional | flops 720895 | bytes 6685080 | solution.py:778
  36.5 1.1 %broadcast.257 = bf16[8,4,8,2048]{3,2,1,0:T(8,128)(2,1)} broadcast(bf16[]{:T(256)} %constant.95.clone), dimensions={} | broadcast | bytes 1048578 | tf_op jit(solution)/shard_map/broadcast.3
  37.6 0.6 collective-permute-start.17
  38.2 2.5 %collective-permute-start.15 = (bf16[4,8,2048]{2,1,0:T(8,128)(2,1)S(1)}, bf16[4,8,2048]{2,1,0:T(8,128)(2,1)S(1)}, u32[]{:S(2)}, u32[]{:S(2)}) collective-permute-start(bf16[4,8,2048]{2,1,0:T(8,128)(2,1)S(1)} %pad_maximum_fusion.1.refs_0_), channel_id=1, source_target_pairs={{0,2},{1,3},{2,0},{3,1},{4,6},{5,7},{6,4},{7,5},{8,10},{9,11},{10,... | collective-permute-start | bytes 393224 | tf_op jit(solution)/shard_map/ppermute | solution.py:719
  40.7 0.0 collective-permute-start.14
  40.8 3.9 %mix.1.mix_ref = bf16[2,2,1024,256]{3,2,1,0:T(8,128)(2,1)} custom-call(s32[1]{0:T(128)} %bitcast.19.base_ref, f32[128,256]{1,0:T(8,128)} %constant.114.clone.sub_ref, f32[8,128]{1,0:T(8,128)} %constant.115.clone.turn_ref), custom_call_target="tpu_custom_call" | custom-call | flops 1073741824 | bytes 4194304 | tf_op jit(solution)/shard_map/mix/pallas_call | solution.py:676
  44.7 0.0 collective-permute-done.13.refs_6_
  44.7 3.8 %collective-permute-done.17.refs_4_ = bf16[4,8,2048]{2,1,0:T(8,128)(2,1)S(1)} collective-permute-done((bf16[4,8,2048]{2,1,0:T(8,128)(2,1)S(1)}, bf16[4,8,2048]{2,1,0:T(8,128)(2,1)S(1)}, u32[]{:S(2)}, u32[]{:S(2)}) %collective-permute-start.17) | collective-permute-done | bytes 131104 | tf_op jit(solution)/shard_map/ppermute | solution.py:719
  48.5 0.0 collective-permute-start.18
  48.5 0.0 collective-permute-done.15.refs_2_
  48.5 0.5 collective-permute-start.16
  49.0 0.0 collective-permute-start.19
  49.0 0.0 collective-permute-done.14.refs_1_
  49.0 0.8 %collective-permute-done.18.refs_5_ = bf16[4,8,2048]{2,1,0:T(8,128)(2,1)S(1)} collective-permute-done((bf16[4,8,2048]{2,1,0:T(8,128)(2,1)S(1)}, bf16[4,8,2048]{2,1,0:T(8,128)(2,1)S(1)}, u32[]{:S(2)}, u32[]{:S(2)}) %collective-permute-start.18) | collective-permute-done | bytes 131104 | tf_op jit(solution)/shard_map/ppermute | solution.py:719
  49.8 0.2 collective-permute-done.16.refs_3_
  50.0 0.3 collective-permute-done.19.refs_7_
  50.4 0.0 copy-start
  50.4 1.6 %copy-done = bf16[2,2,1024,256]{3,2,1,0:T(8,128)(2,1)S(1)} copy-done((bf16[2,2,1024,256]{3,2,1,0:T(8,128)(2,1)S(1)}, bf16[2,2,1024,256]{3,2,1,0:T(8,128)(2,1)}, u32[]{:S(2)}) %copy-start) | copy-done | bytes 2097176
  52.0 0.0 copy-start.1
  52.0 0.8 copy-done.1
  52.7 22.9 %image.1 = f32[2,512,4096]{2,1,0:T(8,128)} custom-call(s32[1]{0:T(128)} %bitcast.18.groups_ref, s32[1]{0:T(128)} %bitcast.19.base_ref, s32[4,128]{1,0:T(4,128)S(1)} %bitcast.43, s32[4,128]{1,0:T(4,128)S(1)} %bitcast.42, bf16[2,2,1024,256]{3,2,1,0:T(8,128)(2,1)S(1)} %copy-done, f32[64,128]{1,0:T(8,128)S(1)} %copy-done.1, ...), custom_call_target="tpu_custom_call" | custom-call | tf_op jit(solution)/shard_map/image/pallas_call | solution.py:693
  (1 shorter events, 0.0 us)
Async XLA Ops:
  2.7 17.3 %all-to-all-start = ((f32[32,16,128]{2,1,0:T(8,128)}), f32[32,16,128]{2,1,0:T(8,128)S(1)}, u32[]{:S(2)}, u32[]{:S(2)}) async-start(f32[32,16,128]{2,1,0:T(8,128)} %packed.1), calls=%async_computation | async-start | bytes 524288 | tf_op jit(solution)/shard_map/all_to_all | solution.py:746
  20.0 0.7 copy-start.2
  28.5 5.4 %collective-permute-start.10 = (bf16[8,2048]{1,0:T(8,128)(2,1)}, bf16[8,2048]{1,0:T(8,128)(2,1)S(1)}, u32[]{:S(2)}, u32[]{:S(2)}) collective-permute-start(bf16[8,2048]{1,0:T(8,128)(2,1)} %get-tuple-element.26), channel_id=1, source_target_pairs={{0,8},{8,0},{16,24},{24,16},{1,9},{9,1},{17,25},{25,17},{2,10},{10... | collective-permute-start | bytes 98312 | tf_op jit(solution)/shard_map/ppermute | solution.py:719
  29.3 4.6 %collective-permute-start.11 = (bf16[8,2048]{1,0:T(8,128)(2,1)}, bf16[8,2048]{1,0:T(8,128)(2,1)S(1)}, u32[]{:S(2)}, u32[]{:S(2)}) collective-permute-start(bf16[8,2048]{1,0:T(8,128)(2,1)} %get-tuple-element.27), channel_id=1, source_target_pairs={{0,16},{8,24},{16,0},{24,8},{1,17},{9,25},{17,1},{25,9},{2,18},{10... | collective-permute-start | bytes 98312 | tf_op jit(solution)/shard_map/ppermute | solution.py:719
  29.4 5.0 %collective-permute-start.12 = (bf16[8,2048]{1,0:T(8,128)(2,1)}, bf16[8,2048]{1,0:T(8,128)(2,1)S(1)}, u32[]{:S(2)}, u32[]{:S(2)}) collective-permute-start(bf16[8,2048]{1,0:T(8,128)(2,1)} %get-tuple-element.28), channel_id=1, source_target_pairs={{0,24},{8,16},{16,8},{24,0},{1,25},{9,17},{17,9},{25,1},{2,26},{10... | collective-permute-start | bytes 98312 | tf_op jit(solution)/shard_map/ppermute | solution.py:719
  35.2 9.5 %collective-permute-start.13 = (bf16[4,8,2048]{2,1,0:T(8,128)(2,1)S(1)}, bf16[4,8,2048]{2,1,0:T(8,128)(2,1)S(1)}, u32[]{:S(2)}, u32[]{:S(2)}) collective-permute-start(bf16[4,8,2048]{2,1,0:T(8,128)(2,1)S(1)} %pad_maximum_fusion.1.refs_0_), channel_id=1, source_target_pairs={{0,6},{1,7},{2,4},{3,5},{4,2},{5,3},{6,0},{7,1},{8,14},{9,15},{10,... | collective-permute-start | bytes 393224 | tf_op jit(solution)/shard_map/ppermute | solution.py:719
  37.6 10.9 %collective-permute-start.17 = (bf16[4,8,2048]{2,1,0:T(8,128)(2,1)S(1)}, bf16[4,8,2048]{2,1,0:T(8,128)(2,1)S(1)}, u32[]{:S(2)}, u32[]{:S(2)}) collective-permute-start(bf16[4,8,2048]{2,1,0:T(8,128)(2,1)S(1)} %pad_maximum_fusion.1.refs_0_), channel_id=1, source_target_pairs={{0,4},{1,5},{2,6},{3,7},{4,0},{5,1},{6,2},{7,3},{8,12},{9,13},{10,... | collective-permute-start | bytes 393224 | tf_op jit(solution)/shard_map/ppermute | solution.py:719
  38.2 10.3 %collective-permute-start.15 = (bf16[4,8,2048]{2,1,0:T(8,128)(2,1)S(1)}, bf16[4,8,2048]{2,1,0:T(8,128)(2,1)S(1)}, u32[]{:S(2)}, u32[]{:S(2)}) collective-permute-start(bf16[4,8,2048]{2,1,0:T(8,128)(2,1)S(1)} %pad_maximum_fusion.1.refs_0_), channel_id=1, source_target_pairs={{0,2},{1,3},{2,0},{3,1},{4,6},{5,7},{6,4},{7,5},{8,10},{9,11},{10,... | collective-permute-start | bytes 393224 | tf_op jit(solution)/shard_map/ppermute | solution.py:719
  40.7 8.3 %collective-permute-start.14 = (bf16[4,8,2048]{2,1,0:T(8,128)(2,1)S(1)}, bf16[4,8,2048]{2,1,0:T(8,128)(2,1)S(1)}, u32[]{:S(2)}, u32[]{:S(2)}) collective-permute-start(bf16[4,8,2048]{2,1,0:T(8,128)(2,1)S(1)} %pad_maximum_fusion.1.refs_0_), channel_id=1, source_target_pairs={{0,1},{1,0},{2,3},{3,2},{4,5},{5,4},{6,7},{7,6},{8,9},{9,8},{10,11... | collective-permute-start | bytes 393224 | tf_op jit(solution)/shard_map/ppermute | solution.py:719
  48.5 1.3 %collective-permute-start.18 = (bf16[4,8,2048]{2,1,0:T(8,128)(2,1)S(1)}, bf16[4,8,2048]{2,1,0:T(8,128)(2,1)S(1)}, u32[]{:S(2)}, u32[]{:S(2)}) collective-permute-start(bf16[4,8,2048]{2,1,0:T(8,128)(2,1)S(1)} %collective-permute-done.17.refs_4_), channel_id=1, source_target_pairs={{0,1},{1,0},{2,3},{3,2},{4,5},{5,4},{6,7},{7,6},{8,9},{9,8},{10,11... | collective-permute-start | bytes 393224 | tf_op jit(solution)/shard_map/ppermute | solution.py:719
  48.5 1.5 %collective-permute-start.16 = (bf16[4,8,2048]{2,1,0:T(8,128)(2,1)S(1)}, bf16[4,8,2048]{2,1,0:T(8,128)(2,1)S(1)}, u32[]{:S(2)}, u32[]{:S(2)}) collective-permute-start(bf16[4,8,2048]{2,1,0:T(8,128)(2,1)S(1)} %collective-permute-done.15.refs_2_), channel_id=1, source_target_pairs={{0,1},{1,0},{2,3},{3,2},{4,5},{5,4},{6,7},{7,6},{8,9},{9,8},{10,11... | collective-permute-start | bytes 393224 | tf_op jit(solution)/shard_map/ppermute | solution.py:719
  49.0 1.3 %collective-permute-start.19 = (bf16[4,8,2048]{2,1,0:T(8,128)(2,1)S(1)}, bf16[4,8,2048]{2,1,0:T(8,128)(2,1)S(1)}, u32[]{:S(2)}, u32[]{:S(2)}) collective-permute-start(bf16[4,8,2048]{2,1,0:T(8,128)(2,1)S(1)} %collective-permute-done.13.refs_6_), channel_id=1, source_target_pairs={{0,1},{1,0},{2,3},{3,2},{4,5},{5,4},{6,7},{7,6},{8,9},{9,8},{10,11... | collective-permute-start | bytes 393224 | tf_op jit(solution)/shard_map/ppermute | solution.py:719
  50.4 1.6 %copy-start = (bf16[2,2,1024,256]{3,2,1,0:T(8,128)(2,1)S(1)}, bf16[2,2,1024,256]{3,2,1,0:T(8,128)(2,1)}, u32[]{:S(2)}) copy-start(bf16[2,2,1024,256]{3,2,1,0:T(8,128)(2,1)} %mix.1.mix_ref) | copy-start | bytes 6291460
  52.0 0.8 %copy-start.1 = (f32[64,128]{1,0:T(8,128)S(1)}, f32[64,128]{1,0:T(8,128)}, u32[]{:S(2)}) copy-start(f32[64,128]{1,0:T(8,128)} %constant.116.clone.twist_ref) | copy-start | bytes 98308

commit v4 on v3

--- a/solution.py
+++ b/solution.py
@@ -342,6 +342,7 @@
         out_shape=jax.ShapeDtypeStruct((devices, 16, LANES), jnp.float32),
         in_specs=[smem, smem, vmem, vmem, vmem],
         out_specs=vmem,
+        compiler_params=pltpu.CompilerParams(vmem_limit_bytes=8 * 1024 * 1024),
         name="packed",
     )(held, place, counts, corr, tracks)
 
@@ -446,6 +447,7 @@
         in_specs=[smem] * 3 + [vmem] * 4,
         out_specs=[vmem] * 5,
         scratch_shapes=[pltpu.VMEM((capacity, 4, 2 * SUB * SUB), jnp.float32)],
+        compiler_params=pltpu.CompilerParams(vmem_limit_bytes=16 * 1024 * 1024),
         name="subgrids",
     )(held, place, offsets, slots, jnp.asarray(pixel_rows()), jnp.asarray(row_twiddles()), weight_row)
 
@@ -679,6 +681,7 @@
         in_specs=[smem, vmem, vmem],
         out_specs=vmem,
         cost_estimate=pl.CostEstimate(flops=1 << 30, bytes_accessed=1 << 22, transcendentals=0),
+        compiler_params=pltpu.CompilerParams(vmem_limit_bytes=16 * 1024 * 1024),
         name="mix",
     )(x_base, jnp.asarray(sub, jnp.float32), jnp.asarray(turns, jnp.float32))
 
@@ -769,17 +772,20 @@
     x_base = (slab * x_count).reshape(1)
     x_block = min(x_count, 256)
 
-    def mixed(after):
+    many = total > devices * GROUP
+
+    def besides(after):
         base, _ = lax.optimization_barrier((x_base, after))
-        return mix_table(base, x_count, x_block)
-
-    first, mix = gathered(pieces, mixed)
-    many = total > devices * GROUP
-    more = lax.cond(
-        many,
-        lambda: jnp.stack(gathered([extra[k] for k in range(pols)])[0]),
-        lambda: jnp.zeros((slabs,) + extra.shape, extra.dtype),
-    )
+        mix = mix_table(base, x_count, x_block)
+        more_needed, _ = lax.optimization_barrier((many, mix))
+        more = lax.cond(
+            more_needed,
+            lambda: jnp.stack(gathered([extra[k] for k in range(pols)])[0]),
+            lambda: jnp.zeros((slabs,) + extra.shape, extra.dtype),
+        )
+        return mix, more
+
+    first, (mix, more) = gathered(pieces, besides)
     groups = jnp.where(many, capacity // GROUP, 1).reshape(1)
     sky = image_of(groups, x_base, first, more, rows, cols, mix, x_count, x_block, norm_scale, pol_step)
     return sky[:, None]

time: 77.1 us -> 79 us (1.025); the launches traced: 75.6 us -> 80.1 us
  local copies, waits for them, and re-layouts: 6.39 us -> 11 us
  waiting for transfers between devices: 11.5 us -> 13.7 us
  other arithmetic: 4.6 us -> 2.61 us
    unnamed x6 -> x22, local copies, waits for them, and re-layouts: 3.05 us -> 8.22 us
    pallas_call x1, Pallas kernels: 3.95 us -> 1.72 us  [mix_table(): pl.pallas_call(mix_kernel, out_shape=jax.ShapeDtypeStruct((x_count // x_b...]
    pallas_call x1, Pallas kernels: 7.8 us -> 9.99 us  [subgrids_of(): pl.pallas_call(subgrid_kernel, out_shape=[jax.ShapeDtypeStruct((GROUP, 2...]
    ppermute x10, waiting for transfers between devices: 5.62 us -> 7.23 us  [exchanged(): return lax.ppermute(value, axis, [(i, i ^ distance) for i in range(peers)])]
  transfers between devices with their start and end apart: 11 -> 11, of which waited for: 6 -> 7; matrix products, arithmetic and copies ran while one was open for 9% -> 7% of each run, Pallas kernels for 5% -> 2%
where the time goes in v4:
time: 79 us; the launch traced here: 80.1 us
  Pallas kernels  36.2 us (46%)
  starting transfers between devices  15.8 us (20%)
  waiting for transfers between devices  13.7 us (17%)
  local copies, waits for them, and re-layouts  11 us (14%)
  other arithmetic  2.61 us (3%)
    pallas_call x1, Pallas kernels, image_of(): pl.pallas_call(functools.partial(image_kernel, pol_step, x_block, slabs),...  22.9 us
    pallas_call x1, Pallas kernels, subgrids_of(): pl.pallas_call(subgrid_kernel, out_shape=[jax.ShapeDtypeStruct((GROUP, 2...  9.99 us
    ppermute x10, starting transfers between devices, exchanged(): return lax.ppermute(value, axis, [(i, i ^ distance) for i in range(peers)])  8.52 us
    unnamed x22, local copies, waits for them, and re-layouts  8.22 us
    all_to_all x1, starting transfers between devices, in_image_domain(): slots = lax.all_to_all(sent, ('pol', 'slab'), 0, 0, tiled=True)  7.33 us
    ppermute x10, waiting for transfers between devices, exchanged(): return lax.ppermute(value, axis, [(i, i ^ distance) for i in range(peers)])  7.23 us
    all_to_all x1, waiting for transfers between devices, in_image_domain(): slots = lax.all_to_all(sent, ('pol', 'slab'), 0, 0, tiled=True)  6.46 us
    pallas_call x1, Pallas kernels, mix_table(): pl.pallas_call(mix_kernel, out_shape=jax.ShapeDtypeStruct((x_count // x_b...  1.72 us
  transfers between devices with their start and end apart: 11, of which 7 were waited for; matrix products, arithmetic and copies ran while one was open for 7% of the time, Pallas kernels for 2%

profile of v4, /device:TPU:0, one launch (start us, length us, event | category | flops | bytes accessed | tf_op | source)
XLA Modules:
  0.0 80.1 jit_solution(949489592972777189)
XLA Ops:
  0.0 0.1 pad_add_fusion.place_ref
  0.1 0.0 copy-start
  0.1 0.9 %copy-done = f32[3,64,256]{2,1,0:T(8,128)S(1)} copy-done((f32[3,64,256]{2,1,0:T(8,128)S(1)}, f32[3,64,256]{2,1,0:T(8,128)}, u32[]{:S(2)}) %copy-start) | copy-done | bytes 196632
  1.0 0.8 %copy-done.1 = bf16[2,1,64,256]{3,2,1,0:T(8,128)(2,1)S(1)} copy-done((bf16[2,1,64,256]{3,2,1,0:T(8,128)(2,1)S(1)}, bf16[2,1,64,256]{3,2,1,0:T(8,128)(2,1)}, u32[]{:S(2)}) %copy-start.1) | copy-done | bytes 65560
  1.8 0.7 copy-done.6
  2.5 0.7 copy-done.8
  3.2 1.6 %packed.1 = f32[32,16,128]{2,1,0:T(8,128)} custom-call(s32[8]{0:T(128)S(1)} %copy-done.6, s32[2]{0:T(128)S(1)} %pad_add_fusion.place_ref, s32[1,64]{1,0:T(1,128)S(1)} %bitcast.46, bf16[2,64,256]{2,1,0:T(8,128)(2,1)S(1)} %bitcast.42, f32[3,64,256]{2,1,0:T(8,128)S(1)} %copy-done), custom_call_target="tpu_custom_call" | custom-call | tf_op jit(solution)/shard_map/packed/pallas_call | solution.py:340
  4.7 7.3 %all-to-all-start = ((f32[32,16,128]{2,1,0:T(8,128)}), f32[32,16,128]{2,1,0:T(8,128)S(1)}, u32[]{:S(2)}, u32[]{:S(2)}) async-start(f32[32,16,128]{2,1,0:T(8,128)} %packed.1), calls=%async_computation | async-start | bytes 524288 | tf_op jit(solution)/shard_map/all_to_all | solution.py:749
  12.0 0.8 reshape.170.weight_ref
  12.8 0.8 select_reduce_fusion.2
  13.6 0.7 add_select_fusion
  14.3 0.1 select_n.103
  14.5 0.8 fusion.20
  15.2 0.4 select_reduce_fusion
  15.6 6.5 %all-to-all-done.slots_ref = f32[32,16,128]{2,1,0:T(8,128)S(1)} async-done(((f32[32,16,128]{2,1,0:T(8,128)}), f32[32,16,128]{2,1,0:T(8,128)S(1)}, u32[]{:S(2)}, u32[]{:S(2)}) %all-to-all-start) | async-done | bytes 262176 | tf_op jit(solution)/shard_map/all_to_all | solution.py:749
  22.0 0.8 copy-done.3
  22.8 0.7 copy-done.4
  23.5 0.7 copy-done.5
  24.2 0.7 copy-done.7
  24.8 10.0 %subgrids.1 = (bf16[8,2048]{1,0:T(8,128)(2,1)S(1)}, bf16[8,2048]{1,0:T(8,128)(2,1)S(1)}, bf16[8,2048]{1,0:T(8,128)(2,1)S(1)}, bf16[8,2048]{1,0:T(8,128)(2,1)S(1)}, bf16[4,8,2048]{2,1,0:T(8,128)(2,1)S(1)}) custom-call(s32[8]{0:T(128)S(1)} %copy-done.7, s32[2]{0:T(128)S(1)} %pad_add_fusion.place_ref, s32[2,512]{1,0:T(2,128)S(1)} %copy-done.4, ...), custom_call_target="tpu_custom_call" | custom-call | tf_op jit(solution)/shard_map/subgrids/pallas_call | solution.py:443
  34.8 0.9 %collective-permute-start.10 = (bf16[8,2048]{1,0:T(8,128)(2,1)S(1)}, bf16[8,2048]{1,0:T(8,128)(2,1)S(1)}, u32[]{:S(2)}, u32[]{:S(2)}) collective-permute-start(bf16[8,2048]{1,0:T(8,128)(2,1)S(1)} %get-tuple-element.28), channel_id=1, source_target_pairs={{0,8},{8,0},{16,24},{24,16},{1,9},{9,1},{17,25},{25,17},{2,10},{10... | collective-permute-start | bytes 98312 | tf_op jit(solution)/shard_map/ppermute | solution.py:722
  35.8 0.0 collective-permute-start.11
  35.8 2.6 %collective-permute-start.12 = (bf16[8,2048]{1,0:T(8,128)(2,1)S(1)}, bf16[8,2048]{1,0:T(8,128)(2,1)S(1)}, u32[]{:S(2)}, u32[]{:S(2)}) collective-permute-start(bf16[8,2048]{1,0:T(8,128)(2,1)S(1)} %get-tuple-element.30), channel_id=1, source_target_pairs={{0,24},{8,16},{16,8},{24,0},{1,25},{9,17},{17,9},{25,1},{2,26},{10... | collective-permute-start | bytes 98312 | tf_op jit(solution)/shard_map/ppermute | solution.py:722
  38.4 0.6 reduce_sum.36
  39.7 0.0 collective-permute-done.10
  39.7 0.0 collective-permute-done.11
  39.7 0.9 %collective-permute-done.12 = bf16[8,2048]{1,0:T(8,128)(2,1)S(1)} collective-permute-done((bf16[8,2048]{1,0:T(8,128)(2,1)S(1)}, bf16[8,2048]{1,0:T(8,128)(2,1)S(1)}, u32[]{:S(2)}, u32[]{:S(2)}) %collective-permute-start.12) | collective-permute-done | bytes 32800 | tf_op jit(solution)/shard_map/ppermute | solution.py:722
  40.6 1.4 %collective-permute-start.13 = (bf16[4,8,2048]{2,1,0:T(8,128)(2,1)S(1)}, bf16[4,8,2048]{2,1,0:T(8,128)(2,1)S(1)}, u32[]{:S(2)}, u32[]{:S(2)}) collective-permute-start(bf16[4,8,2048]{2,1,0:T(8,128)(2,1)S(1)} %pad_maximum_fusion.1.refs_0_), channel_id=1, source_target_pairs={{0,6},{1,7},{2,4},{3,5},{4,2},{5,3},{6,0},{7,1},{8,14},{9,15},{10,... | collective-permute-start | bytes 393224 | tf_op jit(solution)/shard_map/ppermute | solution.py:722
  42.0 0.9 %copy-done.9 = f32[128,256]{1,0:T(8,128)S(1)} copy-done((f32[128,256]{1,0:T(8,128)S(1)}, f32[128,256]{1,0:T(8,128)}, u32[]{:S(2)}) %copy-start.9) | copy-done | bytes 131096
  42.9 0.7 copy-done.10
  43.6 1.7 %mix.1.mix_ref = bf16[2,2,1024,256]{3,2,1,0:T(8,128)(2,1)S(1)} custom-call(s32[1]{0:T(128)} %bitcast.19.base_ref, f32[128,256]{1,0:T(8,128)S(1)} %copy-done.9, f32[8,128]{1,0:T(8,128)S(1)} %copy-done.10), custom_call_target="tpu_custom_call" | custom-call | flops 1073741824 | bytes 4194304 | tf_op jit(solution)/shard_map/mix/pallas_call | solution.py:678
  45.3 1.1 %conditional.1 = (bf16[8,4,8,2048]{3,2,1,0:T(8,128)(2,1)}) conditional(s32[]{:T(128)} %convert_element_type.3, () %tuple.20, bf16[4,8,2048]{2,1,0:T(8,128)(2,1)S(1)} %get-tuple-element.33), branch_computations={%region_4.5_spmd, %region_5.6_spmd} | conditional | flops 720895 | bytes 6685080 | solution.py:781
  45.3 1.1 %broadcast.257 = bf16[8,4,8,2048]{3,2,1,0:T(8,128)(2,1)} broadcast(bf16[]{:T(256)} %constant.95.clone), dimensions={} | broadcast | bytes 1048578 | tf_op jit(solution)/shard_map/broadcast.3
  46.5 0.6 collective-permute-start.17
  47.0 2.5 %collective-permute-start.15 = (bf16[4,8,2048]{2,1,0:T(8,128)(2,1)S(1)}, bf16[4,8,2048]{2,1,0:T(8,128)(2,1)S(1)}, u32[]{:S(2)}, u32[]{:S(2)}) collective-permute-start(bf16[4,8,2048]{2,1,0:T(8,128)(2,1)S(1)} %pad_maximum_fusion.1.refs_0_), channel_id=1, source_target_pairs={{0,2},{1,3},{2,0},{3,1},{4,6},{5,7},{6,4},{7,5},{8,10},{9,11},{10,... | collective-permute-start | bytes 393224 | tf_op jit(solution)/shard_map/ppermute | solution.py:722
  49.5 0.0 collective-permute-start.14
  49.5 0.0 collective-permute-done.13.refs_6_
  49.5 5.0 %collective-permute-done.17.refs_4_ = bf16[4,8,2048]{2,1,0:T(8,128)(2,1)S(1)} collective-permute-done((bf16[4,8,2048]{2,1,0:T(8,128)(2,1)S(1)}, bf16[4,8,2048]{2,1,0:T(8,128)(2,1)S(1)}, u32[]{:S(2)}, u32[]{:S(2)}) %collective-permute-start.17) | collective-permute-done | bytes 131104 | tf_op jit(solution)/shard_map/ppermute | solution.py:722
  54.5 0.0 collective-permute-start.18
  54.5 0.2 collective-permute-done.15.refs_2_
  54.7 0.3 collective-permute-start.16
  55.0 0.2 collective-permute-start.19
  55.2 0.0 collective-permute-done.14.refs_1_
  55.2 0.7 collective-permute-done.18.refs_5_
  55.9 0.2 collective-permute-done.16.refs_3_
  56.1 0.3 collective-permute-done.19.refs_7_
  56.4 0.8 copy-done.2
  57.2 22.9 %image.1 = f32[2,512,4096]{2,1,0:T(8,128)} custom-call(s32[1]{0:T(128)} %bitcast.18.groups_ref, s32[1]{0:T(128)} %bitcast.19.base_ref, s32[4,128]{1,0:T(4,128)S(1)} %bitcast.45, s32[4,128]{1,0:T(4,128)S(1)} %bitcast.44, bf16[2,2,1024,256]{3,2,1,0:T(8,128)(2,1)S(1)} %mix.1.mix_ref, f32[64,128]{1,0:T(8,128)S(1)} %copy-done.2, ...), custom_call_target="tpu_custom_call" | custom-call | tf_op jit(solution)/shard_map/image/pallas_call | solution.py:696
  (12 shorter events, 0.1 us)
Async XLA Ops:
  0.1 0.9 %copy-start = (f32[3,64,256]{2,1,0:T(8,128)S(1)}, f32[3,64,256]{2,1,0:T(8,128)}, u32[]{:S(2)}) copy-start(f32[3,64,256]{2,1,0:T(8,128)} %track_ref.1) | copy-start | bytes 589828
  1.0 0.8 %copy-start.1 = (bf16[2,1,64,256]{3,2,1,0:T(8,128)(2,1)S(1)}, bf16[2,1,64,256]{3,2,1,0:T(8,128)(2,1)}, u32[]{:S(2)}) copy-start(bf16[2,1,64,256]{3,2,1,0:T(8,128)(2,1)} %param.13) | copy-start | bytes 196612
  1.8 0.7 copy-start.6
  2.5 0.7 copy-start.8
  4.7 17.3 %all-to-all-start = ((f32[32,16,128]{2,1,0:T(8,128)}), f32[32,16,128]{2,1,0:T(8,128)S(1)}, u32[]{:S(2)}, u32[]{:S(2)}) async-start(f32[32,16,128]{2,1,0:T(8,128)} %packed.1), calls=%async_computation | async-start | bytes 524288 | tf_op jit(solution)/shard_map/all_to_all | solution.py:749
  22.0 0.8 copy-start.3
  22.8 0.7 copy-start.4
  23.5 0.7 copy-start.5
  24.2 0.7 copy-start.7
  34.8 4.8 %collective-permute-start.10 = (bf16[8,2048]{1,0:T(8,128)(2,1)S(1)}, bf16[8,2048]{1,0:T(8,128)(2,1)S(1)}, u32[]{:S(2)}, u32[]{:S(2)}) collective-permute-start(bf16[8,2048]{1,0:T(8,128)(2,1)S(1)} %get-tuple-element.28), channel_id=1, source_target_pairs={{0,8},{8,0},{16,24},{24,16},{1,9},{9,1},{17,25},{25,17},{2,10},{10... | collective-permute-start | bytes 98312 | tf_op jit(solution)/shard_map/ppermute | solution.py:722
  35.8 3.9 %collective-permute-start.11 = (bf16[8,2048]{1,0:T(8,128)(2,1)S(1)}, bf16[8,2048]{1,0:T(8,128)(2,1)S(1)}, u32[]{:S(2)}, u32[]{:S(2)}) collective-permute-start(bf16[8,2048]{1,0:T(8,128)(2,1)S(1)} %get-tuple-element.29), channel_id=1, source_target_pairs={{0,16},{8,24},{16,0},{24,8},{1,17},{9,25},{17,1},{25,9},{2,18},{10... | collective-permute-start | bytes 98312 | tf_op jit(solution)/shard_map/ppermute | solution.py:722
  35.8 4.8 %collective-permute-start.12 = (bf16[8,2048]{1,0:T(8,128)(2,1)S(1)}, bf16[8,2048]{1,0:T(8,128)(2,1)S(1)}, u32[]{:S(2)}, u32[]{:S(2)}) collective-permute-start(bf16[8,2048]{1,0:T(8,128)(2,1)S(1)} %get-tuple-element.30), channel_id=1, source_target_pairs={{0,24},{8,16},{16,8},{24,0},{1,25},{9,17},{17,9},{25,1},{2,26},{10... | collective-permute-start | bytes 98312 | tf_op jit(solution)/shard_map/ppermute | solution.py:722
  40.6 8.9 %collective-permute-start.13 = (bf16[4,8,2048]{2,1,0:T(8,128)(2,1)S(1)}, bf16[4,8,2048]{2,1,0:T(8,128)(2,1)S(1)}, u32[]{:S(2)}, u32[]{:S(2)}) collective-permute-start(bf16[4,8,2048]{2,1,0:T(8,128)(2,1)S(1)} %pad_maximum_fusion.1.refs_0_), channel_id=1, source_target_pairs={{0,6},{1,7},{2,4},{3,5},{4,2},{5,3},{6,0},{7,1},{8,14},{9,15},{10,... | collective-permute-start | bytes 393224 | tf_op jit(solution)/shard_map/ppermute | solution.py:722
  42.0 0.9 %copy-start.9 = (f32[128,256]{1,0:T(8,128)S(1)}, f32[128,256]{1,0:T(8,128)}, u32[]{:S(2)}) copy-start(f32[128,256]{1,0:T(8,128)} %constant.114.clone.sub_ref) | copy-start | bytes 393220
  42.9 0.7 copy-start.10
  46.5 8.1 %collective-permute-start.17 = (bf16[4,8,2048]{2,1,0:T(8,128)(2,1)S(1)}, bf16[4,8,2048]{2,1,0:T(8,128)(2,1)S(1)}, u32[]{:S(2)}, u32[]{:S(2)}) collective-permute-start(bf16[4,8,2048]{2,1,0:T(8,128)(2,1)S(1)} %pad_maximum_fusion.1.refs_0_), channel_id=1, source_target_pairs={{0,4},{1,5},{2,6},{3,7},{4,0},{5,1},{6,2},{7,3},{8,12},{9,13},{10,... | collective-permute-start | bytes 393224 | tf_op jit(solution)/shard_map/ppermute | solution.py:722
  47.0 7.7 %collective-permute-start.15 = (bf16[4,8,2048]{2,1,0:T(8,128)(2,1)S(1)}, bf16[4,8,2048]{2,1,0:T(8,128)(2,1)S(1)}, u32[]{:S(2)}, u32[]{:S(2)}) collective-permute-start(bf16[4,8,2048]{2,1,0:T(8,128)(2,1)S(1)} %pad_maximum_fusion.1.refs_0_), channel_id=1, source_target_pairs={{0,2},{1,3},{2,0},{3,1},{4,6},{5,7},{6,4},{7,5},{8,10},{9,11},{10,... | collective-permute-start | bytes 393224 | tf_op jit(solution)/shard_map/ppermute | solution.py:722
  49.5 5.7 %collective-permute-start.14 = (bf16[4,8,2048]{2,1,0:T(8,128)(2,1)S(1)}, bf16[4,8,2048]{2,1,0:T(8,128)(2,1)S(1)}, u32[]{:S(2)}, u32[]{:S(2)}) collective-permute-start(bf16[4,8,2048]{2,1,0:T(8,128)(2,1)S(1)} %pad_maximum_fusion.1.refs_0_), channel_id=1, source_target_pairs={{0,1},{1,0},{2,3},{3,2},{4,5},{5,4},{6,7},{7,6},{8,9},{9,8},{10,11... | collective-permute-start | bytes 393224 | tf_op jit(solution)/shard_map/ppermute | solution.py:722
  54.5 1.3 %collective-permute-start.18 = (bf16[4,8,2048]{2,1,0:T(8,128)(2,1)S(1)}, bf16[4,8,2048]{2,1,0:T(8,128)(2,1)S(1)}, u32[]{:S(2)}, u32[]{:S(2)}) collective-permute-start(bf16[4,8,2048]{2,1,0:T(8,128)(2,1)S(1)} %collective-permute-done.17.refs_4_), channel_id=1, source_target_pairs={{0,1},{1,0},{2,3},{3,2},{4,5},{5,4},{6,7},{7,6},{8,9},{9,8},{10,11... | collective-permute-start | bytes 393224 | tf_op jit(solution)/shard_map/ppermute | solution.py:722
  54.7 1.4 %collective-permute-start.16 = (bf16[4,8,2048]{2,1,0:T(8,128)(2,1)S(1)}, bf16[4,8,2048]{2,1,0:T(8,128)(2,1)S(1)}, u32[]{:S(2)}, u32[]{:S(2)}) collective-permute-start(bf16[4,8,2048]{2,1,0:T(8,128)(2,1)S(1)} %collective-permute-done.15.refs_2_), channel_id=1, source_target_pairs={{0,1},{1,0},{2,3},{3,2},{4,5},{5,4},{6,7},{7,6},{8,9},{9,8},{10,11... | collective-permute-start | bytes 393224 | tf_op jit(solution)/shard_map/ppermute | solution.py:722
  55.0 1.3 %collective-permute-start.19 = (bf16[4,8,2048]{2,1,0:T(8,128)(2,1)S(1)}, bf16[4,8,2048]{2,1,0:T(8,128)(2,1)S(1)}, u32[]{:S(2)}, u32[]{:S(2)}) collective-permute-start(bf16[4,8,2048]{2,1,0:T(8,128)(2,1)S(1)} %collective-permute-done.13.refs_6_), channel_id=1, source_target_pairs={{0,1},{1,0},{2,3},{3,2},{4,5},{5,4},{6,7},{7,6},{8,9},{9,8},{10,11... | collective-permute-start | bytes 393224 | tf_op jit(solution)/shard_map/ppermute | solution.py:722
  56.4 0.8 copy-start.2

commit v5 on v3

--- a/solution.py
+++ b/solution.py
@@ -450,12 +450,14 @@
     )(held, place, offsets, slots, jnp.asarray(pixel_rows()), jnp.asarray(row_twiddles()), weight_row)
 
 
-def image_kernel(pol_step, x_block, slabs, groups_ref, base_ref, row_ref, col_ref, mix_ref, twist_ref, *refs):
-    first_refs, more_ref, sky_ref = refs[:slabs], refs[slabs], refs[slabs + 1]
-    bundle_ref, phase_ref, col_phase_ref, *half_refs, moved_ref, sum_ref, stage_ref, out_ref = refs[slabs + 2 : -3]
+def image_kernel(pol_step, x_block, slabs, twice, groups_ref, base_ref, row_ref, col_ref, mix_ref, twist_ref, *refs):
+    first_refs, more_ref = refs[:slabs], refs[slabs]
+    refs = refs[slabs + twice :]
+    sky_ref = refs[0]
+    bundle_ref, phase_ref, col_phase_ref, *half_refs, moved_ref, sum_ref, stage_ref, out_ref = refs[1:-3]
     later_ref, sem_ref, later_sem_ref = refs[-3:]
     x_blocks = sky_ref.shape[1] // x_block
-    groups = groups_ref[0]
+    groups = groups_ref[0] if twice else 1
     lane_index = lax.broadcasted_iota(jnp.int32, (LANES, LANES), 1)
     eighth = SUB // 4
     out_rows = out_ref.shape[2]
@@ -476,7 +478,7 @@
 
         def one_phase(residue, inner):
             carried = low > residue
-            twist = (twist_ref[pl.ds(2 * residue, 1)], twist_ref[pl.ds(2 * residue + 1, 1)])
+            twist = (twist_ref[pl.ds(residue, 1)], twist_ref[pl.ds(SUB + residue, 1)])
             re, im = times((jnp.where(carried, later[0], here[0]), jnp.where(carried, later[1], here[1])), twist)
             re = re.astype(jnp.bfloat16)
             phase_ref[residue, re_rows, :LANES] = re
@@ -532,11 +534,13 @@
         turn_pair(eighth // 2 - 1, halves[(eighth // 2 - 1) % 2])
 
     def load_group(group):
-        @pl.when(group > 0)
-        def _():
-            copy = pltpu.make_async_copy(more_ref, later_ref, later_sem_ref)
-            copy.start()
-            copy.wait()
+        if twice:
+
+            @pl.when(group > 0)
+            def _():
+                copy = pltpu.make_async_copy(more_ref, later_ref, later_sem_ref)
+                copy.start()
+                copy.wait()
 
         for part in range(group_chunks):
             polarized = pl.ds(part * pol_step, pol_step)
@@ -548,9 +552,11 @@
                 def _(part=part, polarized=polarized, peer=peer, rows_at=rows_at):
                     bundle_ref[part, rows_at] = first_refs[peer][polarized].reshape(span, -1)
 
-                @pl.when(group > 0)
-                def _(part=part, polarized=polarized, peer=peer, rows_at=rows_at):
-                    bundle_ref[part, rows_at] = later_ref[peer, polarized].reshape(span, -1)
+                if twice:
+
+                    @pl.when(group > 0)
+                    def _(part=part, polarized=polarized, peer=peer, rows_at=rows_at):
+                        bundle_ref[part, rows_at] = later_ref[peer, polarized].reshape(span, -1)
 
             load_phases(group, part)
 
@@ -633,15 +639,7 @@
         copy_out(x_blocks - 1, step).wait()
 
 
-def twist_table(scale):
-    residue = np.arange(SUB)[:, None]
-    lane = np.arange(LANES)[None, :]
-    angle = 2.0 * np.pi * (residue * lane % G) / G
-    sign = np.where(residue % 2 == 0, scale, -scale)
-    return np.stack([sign * np.cos(angle), sign * np.sin(angle)], axis=1).reshape(2 * SUB, LANES).astype(np.float32)
-
-
-def mix_kernel(base_ref, sub_ref, turn_ref, mix_ref):
+def mix_kernel(scale, base_ref, sub_ref, turn_ref, mix_ref, twist_ref):
     x_block = mix_ref.shape[2] // 4
     highest = lax.Precision.HIGHEST
     cell = lax.broadcasted_iota(jnp.int32, (x_block, LANES), 1)
@@ -662,9 +660,14 @@
         return carry
 
     lax.fori_loop(0, mix_ref.shape[0], one_block, 0)
-
-
-def mix_table(x_base, x_count, x_block):
+    residue = lax.broadcasted_iota(jnp.int32, (SUB, LANES), 0)
+    angle = residue * lax.broadcasted_iota(jnp.int32, (SUB, LANES), 1) + jnp.bitwise_and(residue, 1) * (G // 2)
+    re, im = cos_sin_turns(angle.astype(jnp.float32) * (1.0 / G))
+    twist_ref[:SUB] = re * scale
+    twist_ref[SUB:] = im * scale
+
+
+def mix_table(x_base, x_count, x_block, scale):
     cells, pixels = np.arange(LANES)[:, None], np.arange(LANES)[None, :] % SUB
     angle = -2.0 * np.pi * ((cells - SUB // 2) * (pixels - SUB // 2) % SUB) / SUB
     used = cells < SUB
@@ -674,16 +677,20 @@
     smem = pl.BlockSpec(memory_space=pltpu.SMEM)
     vmem = pl.BlockSpec(memory_space=pltpu.VMEM)
     return pl.pallas_call(
-        mix_kernel,
-        out_shape=jax.ShapeDtypeStruct((x_count // x_block, 2, 4 * x_block, 2 * LANES), jnp.bfloat16),
+        functools.partial(mix_kernel, scale),
+        out_shape=[
+            jax.ShapeDtypeStruct((x_count // x_block, 2, 4 * x_block, 2 * LANES), jnp.bfloat16),
+            jax.ShapeDtypeStruct((2 * SUB, LANES), jnp.float32),
+        ],
         in_specs=[smem, vmem, vmem],
-        out_specs=vmem,
+        out_specs=[vmem, vmem],
         cost_estimate=pl.CostEstimate(flops=1 << 30, bytes_accessed=1 << 22, transcendentals=0),
+        compiler_params=pltpu.CompilerParams(vmem_limit_bytes=16 * 1024 * 1024),
         name="mix",
     )(x_base, jnp.asarray(sub, jnp.float32), jnp.asarray(turns, jnp.float32))
 
 
-def image_of(groups, x_base, first, more, rows, cols, mix, x_count, x_block, scale, pol_step):
+def image_of(groups, x_base, first, more, rows, cols, mix, x_count, x_block, pol_step):
     out_rows = min(x_block, 64)
     parts = 4 // pol_step
     slabs = len(first)
@@ -691,9 +698,9 @@
     vmem = pl.BlockSpec(memory_space=pltpu.VMEM)
     hbm = pl.BlockSpec(memory_space=pl.ANY)
     return pl.pallas_call(
-        functools.partial(image_kernel, pol_step, x_block, slabs),
+        functools.partial(image_kernel, pol_step, x_block, slabs, bool(more)),
         out_shape=jax.ShapeDtypeStruct((2, x_count, G), jnp.float32),
-        in_specs=[smem, smem] + [vmem] * (4 + slabs) + [hbm],
+        in_specs=[smem, smem] + [vmem] * (4 + slabs) + [hbm] * len(more),
         out_specs=hbm,
         scratch_shapes=[
             pltpu.VMEM((parts, LANES, 2 * SUB * SUB), jnp.bfloat16),
@@ -705,13 +712,13 @@
             pltpu.VMEM((SUB, x_block, 2 * LANES), jnp.float32),
             pltpu.VMEM((4, 8, 2, 8, LANES), jnp.float32),
             pltpu.VMEM((x_block // out_rows, 2, out_rows, G), jnp.float32),
-            pltpu.VMEM(more.shape, more.dtype),
+            pltpu.VMEM((slabs if more else 1,) + first[0].shape, first[0].dtype),
             pltpu.SemaphoreType.DMA((x_block // out_rows,)),
             pltpu.SemaphoreType.DMA,
         ],
         compiler_params=pltpu.CompilerParams(vmem_limit_bytes=46 * 1024 * 1024),
         name="image",
-    )(groups, x_base, rows, cols, mix, jnp.asarray(twist_table(scale)), *first, more)
+    )(groups, x_base, rows, cols, *mix, *first, *more)
 
 
 def exchanged(value, axis, distance):
@@ -771,17 +778,20 @@
 
     def mixed(after):
         base, _ = lax.optimization_barrier((x_base, after))
-        return mix_table(base, x_count, x_block)
+        return mix_table(base, x_count, x_block, norm_scale)
 
     first, mix = gathered(pieces, mixed)
     many = total > devices * GROUP
-    more = lax.cond(
-        many,
-        lambda: jnp.stack(gathered([extra[k] for k in range(pols)])[0]),
-        lambda: jnp.zeros((slabs,) + extra.shape, extra.dtype),
-    )
-    groups = jnp.where(many, capacity // GROUP, 1).reshape(1)
-    sky = image_of(groups, x_base, first, more, rows, cols, mix, x_count, x_block, norm_scale, pol_step)
+
+    def image(groups, more):
+        groups = jnp.full((1,), groups, jnp.int32)
+        return image_of(groups, x_base, first, more, rows, cols, mix, x_count, x_block, pol_step)
+
+    def image_of_all():
+        more = jnp.stack(gathered([extra[k] for k in range(pols)])[0])
+        return image(capacity // GROUP, [more])
+
+    sky = lax.cond(many, image_of_all, lambda: image(1, []))
     return sky[:, None]
 
 

time: 77.1 us -> 75.9 us (0.984); the launches traced: 75.6 us -> 75.7 us
  local copies, waits for them, and re-layouts: 6.39 us -> 4.53 us
  waiting for transfers between devices: 11.5 us -> 13 us
    pallas_call x1, Pallas kernels: 7.8 us -> 10.7 us  [subgrids_of(): pl.pallas_call(subgrid_kernel, out_shape=[jax.ShapeDtypeStruct((GROUP, 2...]
    pallas_call x2, Pallas kernels: 26.9 us -> 24 us  [the longest x1 22.3 us: image_of(): pl.pallas_call(functools.partial(image_kernel, pol_step, x_block, slabs,...]
    ppermute x10, waiting for transfers between devices: 5.62 us -> 7.16 us  [exchanged(): return lax.ppermute(value, axis, [(i, i ^ distance) for i in range(peers)])]
    another operation x1 -> x0, local copies, waits for them, and re-layouts: 1.1 us -> none
  transfers between devices with their start and end apart: 11 -> 11, of which waited for: 6 -> 5; matrix products, arithmetic and copies ran while one was open for 9% -> 7% of each run, Pallas kernels for 5% -> 2%
where the time goes in v5:
time: 75.9 us; the launch traced here: 75.7 us
  Pallas kernels  36.7 us (48%)
  starting transfers between devices  15.8 us (21%)
  waiting for transfers between devices  13 us (17%)
  other arithmetic  4.62 us (6%)
  local copies, waits for them, and re-layouts  4.53 us (6%)
  between operations  0.88 us (1%)
    pallas_call x1, Pallas kernels, image_of(): pl.pallas_call(functools.partial(image_kernel, pol_step, x_block, slabs,...  22.3 us
    pallas_call x1, Pallas kernels, subgrids_of(): pl.pallas_call(subgrid_kernel, out_shape=[jax.ShapeDtypeStruct((GROUP, 2...  10.7 us
    ppermute x10, starting transfers between devices, exchanged(): return lax.ppermute(value, axis, [(i, i ^ distance) for i in range(peers)])  8.46 us
    all_to_all x1, starting transfers between devices, in_image_domain(): slots = lax.all_to_all(sent, ('pol', 'slab'), 0, 0, tiled=True)  7.33 us
    ppermute x10, waiting for transfers between devices, exchanged(): return lax.ppermute(value, axis, [(i, i ^ distance) for i in range(peers)])  7.16 us
    all_to_all x1, waiting for transfers between devices, in_image_domain(): slots = lax.all_to_all(sent, ('pol', 'slab'), 0, 0, tiled=True)  5.87 us
    unnamed x6, local copies, waits for them, and re-layouts  2.29 us
    pallas_call x1, Pallas kernels, packed(): pl.pallas_call(pack_kernel, out_shape=jax.ShapeDtypeStruct((devices, 16,...  2 us
  transfers between devices with their start and end apart: 11, of which 5 were waited for; matrix products, arithmetic and copies ran while one was open for 7% of the time, Pallas kernels for 2%

profile of v5, /device:TPU:0, one launch (start us, length us, event | category | flops | bytes accessed | tf_op | source)
XLA Modules:
  0.0 75.7 jit_solution(3116268330308060844)
XLA Ops:
  0.0 0.7 pad_add_fusion.place_ref
  0.7 2.0 %packed.1 = f32[32,16,128]{2,1,0:T(8,128)} custom-call(s32[8]{0:T(128)} %held_counts_ref, s32[2]{0:T(128)} %pad_add_fusion.place_ref, s32[1,64]{1,0:T(1,128)} %bitcast.61, bf16[2,64,256]{2,1,0:T(8,128)(2,1)} %bitcast.50, f32[3,64,256]{2,1,0:T(8,128)} %track_ref.1), custom_call_target="tpu_custom_call" | custom-call | tf_op jit(solution)/shard_map/packed/pallas_call | solution.py:340
  2.7 7.3 %all-to-all-start = ((f32[32,16,128]{2,1,0:T(8,128)}), f32[32,16,128]{2,1,0:T(8,128)S(1)}, u32[]{:S(2)}, u32[]{:S(2)}) async-start(f32[32,16,128]{2,1,0:T(8,128)} %packed.1), calls=%async_computation | async-start | bytes 524288 | tf_op jit(solution)/shard_map/all_to_all | solution.py:753
  10.0 1.4 %reshape.166.weight_ref = f32[1,1024]{1,0:T(1,128)} reshape(f32[32,32]{1,0:T(8,128)} %param.17) | data formatting | bytes 8192 | tf_op jit(solution)/shard_map/reshape | solution.py:773
  11.4 0.8 %select_reduce_fusion.2 = s32[8]{0:T(128)S(1)} fusion(s32[8]{0:T(128)} %held_counts_ref), kind=kLoop, calls=%fused_computation.17 | loop fusion | flops 184 | bytes 64 | tf_op jit(solution)/shard_map/reduce_sum | solution.py:755
  12.2 0.7 add_select_fusion
  12.9 0.1 select_n.98
  13.0 0.8 %fusion.20 = (s32[1,512]{1,0:T(1,128)S(1)}, s32[1,512]{1,0:T(1,128)S(1)}) fusion(s32[2,512]{1,0:T(2,128)} %offsets_ref.1), kind=kLoop, calls=%fused_computation.65 | loop fusion | bytes 8192 | tf_op jit(solution)/shard_map/slice | solution.py:770
  13.8 0.4 select_reduce_fusion
  14.1 5.9 %all-to-all-done.slots_ref = f32[32,16,128]{2,1,0:T(8,128)S(1)} async-done(((f32[32,16,128]{2,1,0:T(8,128)}), f32[32,16,128]{2,1,0:T(8,128)S(1)}, u32[]{:S(2)}, u32[]{:S(2)}) %all-to-all-start) | async-done | bytes 262176 | tf_op jit(solution)/shard_map/all_to_all | solution.py:753
  20.0 0.0 copy-start.2
  20.0 0.7 copy-done.2
  20.7 10.7 %subgrids.1 = (bf16[8,2048]{1,0:T(8,128)(2,1)}, bf16[8,2048]{1,0:T(8,128)(2,1)}, bf16[8,2048]{1,0:T(8,128)(2,1)}, bf16[8,2048]{1,0:T(8,128)(2,1)}, bf16[4,8,2048]{2,1,0:T(8,128)(2,1)S(1)}) custom-call(s32[8]{0:T(128)} %held_counts_ref, s32[2]{0:T(128)} %pad_add_fusion.place_ref, s32[2,512]{1,0:T(2,128)} %offsets_ref.1, f32[32,16,128]{2,1,0:T(8,128)} %copy-done.2, ...), custom_call_target="tpu_custom_call" | custom-call | tf_op jit(solution)/shard_map/subgrids/pallas_call | solution.py:442
  31.4 0.0 collective-permute-start.10
  31.4 0.2 collective-permute-start.11
  31.7 3.2 %collective-permute-start.12 = (bf16[8,2048]{1,0:T(8,128)(2,1)}, bf16[8,2048]{1,0:T(8,128)(2,1)S(1)}, u32[]{:S(2)}, u32[]{:S(2)}) collective-permute-start(bf16[8,2048]{1,0:T(8,128)(2,1)} %get-tuple-element.112), channel_id=1, source_target_pairs={{0,24},{8,16},{16,8},{24,0},{1,25},{9,17},{17,9},{25,1},{2,26},{10... | collective-permute-start | bytes 98312 | tf_op jit(solution)/shard_map/ppermute | solution.py:726
  34.9 0.8 %collective-permute-done.10 = bf16[8,2048]{1,0:T(8,128)(2,1)S(1)} collective-permute-done((bf16[8,2048]{1,0:T(8,128)(2,1)}, bf16[8,2048]{1,0:T(8,128)(2,1)S(1)}, u32[]{:S(2)}, u32[]{:S(2)}) %collective-permute-start.10) | collective-permute-done | bytes 32800 | tf_op jit(solution)/shard_map/ppermute | solution.py:726
  35.7 0.0 collective-permute-done.11
  35.7 1.3 %collective-permute-done.12 = bf16[8,2048]{1,0:T(8,128)(2,1)S(1)} collective-permute-done((bf16[8,2048]{1,0:T(8,128)(2,1)}, bf16[8,2048]{1,0:T(8,128)(2,1)S(1)}, u32[]{:S(2)}, u32[]{:S(2)}) %collective-permute-start.12) | collective-permute-done | bytes 32800 | tf_op jit(solution)/shard_map/ppermute | solution.py:726
  37.0 0.8 %pad_maximum_fusion.1 = bf16[4,8,2048]{2,1,0:T(8,128)(2,1)S(1)} fusion(bf16[1,8,2048]{2,1,0:T(8,128)(2,1)S(1)} %bitcast.54, bf16[1,8,2048]{2,1,0:T(8,128)(2,1)S(1)} %bitcast.53, bf16[1,8,2048]{2,1,0:T(8,128)(2,1)S(1)} %bitcast.52, bf16[1,8,2048]{2,1,0:T(8,128)(2,1)} %bitcast.51), kind=kLoop, calls=%fused_computation.15 | loop fusion | flops 196608 | bytes 262144 | tf_op jit(solution)/shard_map/stack | solution.py:731
  37.8 1.7 %collective-permute-start.13 = (bf16[4,8,2048]{2,1,0:T(8,128)(2,1)S(1)}, bf16[4,8,2048]{2,1,0:T(8,128)(2,1)S(1)}, u32[]{:S(2)}, u32[]{:S(2)}) collective-permute-start(bf16[4,8,2048]{2,1,0:T(8,128)(2,1)S(1)} %pad_maximum_fusion.1), channel_id=1, source_target_pairs={{0,6},{1,7},{2,4},{3,5},{4,2},{5,3},{6,0},{7,1},{8,14},{9,15},{10,... | collective-permute-start | bytes 393224 | tf_op jit(solution)/shard_map/ppermute | solution.py:726
  39.4 0.6 collective-permute-start.17
  40.1 2.2 %collective-permute-start.15 = (bf16[4,8,2048]{2,1,0:T(8,128)(2,1)S(1)}, bf16[4,8,2048]{2,1,0:T(8,128)(2,1)S(1)}, u32[]{:S(2)}, u32[]{:S(2)}) collective-permute-start(bf16[4,8,2048]{2,1,0:T(8,128)(2,1)S(1)} %pad_maximum_fusion.1), channel_id=1, source_target_pairs={{0,2},{1,3},{2,0},{3,1},{4,6},{5,7},{6,4},{7,5},{8,10},{9,11},{10,... | collective-permute-start | bytes 393224 | tf_op jit(solution)/shard_map/ppermute | solution.py:726
  42.2 0.0 collective-permute-start.14
  42.2 0.0 copy-start
  42.2 0.9 %copy-done = f32[128,256]{1,0:T(8,128)S(1)} copy-done((f32[128,256]{1,0:T(8,128)S(1)}, f32[128,256]{1,0:T(8,128)}, u32[]{:S(2)}) %copy-start) | copy-done | bytes 131096
  43.1 0.0 copy-start.1
  43.1 0.7 copy-done.1
  43.8 1.7 %mix.1 = (bf16[2,2,1024,256]{3,2,1,0:T(8,128)(2,1)S(1)}, f32[64,128]{1,0:T(8,128)S(1)}) custom-call(s32[1]{0:T(128)} %bitcast.24.base_ref, f32[128,256]{1,0:T(8,128)S(1)} %copy-done, f32[8,128]{1,0:T(8,128)S(1)} %copy-done.1), custom_call_target="tpu_custom_call" | custom-call | flops 1073741824 | bytes 4194304 | tf_op jit(solution)/shard_map/mix/pallas_call | solution.py:679
  45.6 0.4 collective-permute-done.13
  46.0 4.6 %collective-permute-done.17 = bf16[4,8,2048]{2,1,0:T(8,128)(2,1)S(1)} collective-permute-done((bf16[4,8,2048]{2,1,0:T(8,128)(2,1)S(1)}, bf16[4,8,2048]{2,1,0:T(8,128)(2,1)S(1)}, u32[]{:S(2)}, u32[]{:S(2)}) %collective-permute-start.17) | collective-permute-done | bytes 131104 | tf_op jit(solution)/shard_map/ppermute | solution.py:726
  50.6 0.0 collective-permute-start.18
  50.6 0.0 collective-permute-done.15
  50.6 0.5 collective-permute-start.16
  51.1 0.0 collective-permute-start.19
  51.1 1.3 %reduce_sum.36 = s32[]{:T(128)} reduce(s32[8]{0:T(128)} %held_counts_ref, s32[]{:T(128)} %constant.97.clone.1), dimensions={0}, to_apply=%region_0.1 | reduce | flops 7 | bytes 40 | tf_op jit(solution)/shard_map/reduce_sum | solution.py:756
  53.1 0.0 collective-permute-done.14
  53.1 0.0 collective-permute-done.18
  53.1 0.0 collective-permute-done.16
  53.1 0.0 collective-permute-done.19
  53.1 22.5 %conditional.1 = (f32[2,1,512,4096]{3,2,1,0:T(8,128)}) conditional(s32[]{:T(128)} %convert_element_type.3, (s32[1]{0:T(128)}, s32[4,128]{1,0:T(4,128)S(1)}, s32[4,128]{1,0:T(4,128)S(1)}, bf16[2,2,1024,256]{3,2,1,0:T(8,128)(2,1)S(1)}, f32[64,128]{1,0:T(8,128)S(1)}, /*index=5*/bf16[4,8,2048]{2,1,0:T(8,128)(2,1)S(1)}, bf16[4,8,2048]{2,1,0:T(8,128)(2,1)S(1)}, ...), branch_computations={%region_4.5_spmd, %region_5.6_spmd} | conditional | flops 720895 | bytes 6685080 | solution.py:794
  53.1 22.3 %image.2 = f32[2,512,4096]{2,1,0:T(8,128)} custom-call(s32[1]{0:T(128)} %constant.93.clone.groups_ref, s32[1]{0:T(128)} %get-tuple-element.63.base_ref, s32[4,128]{1,0:T(4,128)S(1)} %get-tuple-element.64.row_ref, s32[4,128]{1,0:T(4,128)S(1)} %get-tuple-element.65.col_ref, bf16[2,2,1024,256]{3,2,1,0:T(8,128)(2,1)S(1)} %get-tuple-element.66.mix_ref, ...), custom_call_target="tpu_custom_call" | custom-call | tf_op jit(solution)/shard_map/cond/branch_0_fun/image/pallas_call | solution.py:700
  (1 shorter events, 0.0 us)
Async XLA Ops:
  2.7 17.3 %all-to-all-start = ((f32[32,16,128]{2,1,0:T(8,128)}), f32[32,16,128]{2,1,0:T(8,128)S(1)}, u32[]{:S(2)}, u32[]{:S(2)}) async-start(f32[32,16,128]{2,1,0:T(8,128)} %packed.1), calls=%async_computation | async-start | bytes 524288 | tf_op jit(solution)/shard_map/all_to_all | solution.py:753
  20.0 0.7 copy-start.2
  31.4 4.2 %collective-permute-start.10 = (bf16[8,2048]{1,0:T(8,128)(2,1)}, bf16[8,2048]{1,0:T(8,128)(2,1)S(1)}, u32[]{:S(2)}, u32[]{:S(2)}) collective-permute-start(bf16[8,2048]{1,0:T(8,128)(2,1)} %get-tuple-element.110), channel_id=1, source_target_pairs={{0,8},{8,0},{16,24},{24,16},{1,9},{9,1},{17,25},{25,17},{2,10},{10... | collective-permute-start | bytes 98312 | tf_op jit(solution)/shard_map/ppermute | solution.py:726
  31.4 4.3 %collective-permute-start.11 = (bf16[8,2048]{1,0:T(8,128)(2,1)}, bf16[8,2048]{1,0:T(8,128)(2,1)S(1)}, u32[]{:S(2)}, u32[]{:S(2)}) collective-permute-start(bf16[8,2048]{1,0:T(8,128)(2,1)} %get-tuple-element.111), channel_id=1, source_target_pairs={{0,16},{8,24},{16,0},{24,8},{1,17},{9,25},{17,1},{25,9},{2,18},{10... | collective-permute-start | bytes 98312 | tf_op jit(solution)/shard_map/ppermute | solution.py:726
  31.7 5.3 %collective-permute-start.12 = (bf16[8,2048]{1,0:T(8,128)(2,1)}, bf16[8,2048]{1,0:T(8,128)(2,1)S(1)}, u32[]{:S(2)}, u32[]{:S(2)}) collective-permute-start(bf16[8,2048]{1,0:T(8,128)(2,1)} %get-tuple-element.112), channel_id=1, source_target_pairs={{0,24},{8,16},{16,8},{24,0},{1,25},{9,17},{17,9},{25,1},{2,26},{10... | collective-permute-start | bytes 98312 | tf_op jit(solution)/shard_map/ppermute | solution.py:726
  37.8 8.2 %collective-permute-start.13 = (bf16[4,8,2048]{2,1,0:T(8,128)(2,1)S(1)}, bf16[4,8,2048]{2,1,0:T(8,128)(2,1)S(1)}, u32[]{:S(2)}, u32[]{:S(2)}) collective-permute-start(bf16[4,8,2048]{2,1,0:T(8,128)(2,1)S(1)} %pad_maximum_fusion.1), channel_id=1, source_target_pairs={{0,6},{1,7},{2,4},{3,5},{4,2},{5,3},{6,0},{7,1},{8,14},{9,15},{10,... | collective-permute-start | bytes 393224 | tf_op jit(solution)/shard_map/ppermute | solution.py:726
  39.4 11.2 %collective-permute-start.17 = (bf16[4,8,2048]{2,1,0:T(8,128)(2,1)S(1)}, bf16[4,8,2048]{2,1,0:T(8,128)(2,1)S(1)}, u32[]{:S(2)}, u32[]{:S(2)}) collective-permute-start(bf16[4,8,2048]{2,1,0:T(8,128)(2,1)S(1)} %pad_maximum_fusion.1), channel_id=1, source_target_pairs={{0,4},{1,5},{2,6},{3,7},{4,0},{5,1},{6,2},{7,3},{8,12},{9,13},{10,... | collective-permute-start | bytes 393224 | tf_op jit(solution)/shard_map/ppermute | solution.py:726
  40.1 10.6 %collective-permute-start.15 = (bf16[4,8,2048]{2,1,0:T(8,128)(2,1)S(1)}, bf16[4,8,2048]{2,1,0:T(8,128)(2,1)S(1)}, u32[]{:S(2)}, u32[]{:S(2)}) collective-permute-start(bf16[4,8,2048]{2,1,0:T(8,128)(2,1)S(1)} %pad_maximum_fusion.1), channel_id=1, source_target_pairs={{0,2},{1,3},{2,0},{3,1},{4,6},{5,7},{6,4},{7,5},{8,10},{9,11},{10,... | collective-permute-start | bytes 393224 | tf_op jit(solution)/shard_map/ppermute | solution.py:726
  42.2 10.8 %collective-permute-start.14 = (bf16[4,8,2048]{2,1,0:T(8,128)(2,1)S(1)}, bf16[4,8,2048]{2,1,0:T(8,128)(2,1)S(1)}, u32[]{:S(2)}, u32[]{:S(2)}) collective-permute-start(bf16[4,8,2048]{2,1,0:T(8,128)(2,1)S(1)} %pad_maximum_fusion.1), channel_id=1, source_target_pairs={{0,1},{1,0},{2,3},{3,2},{4,5},{5,4},{6,7},{7,6},{8,9},{9,8},{10,11... | collective-permute-start | bytes 393224 | tf_op jit(solution)/shard_map/ppermute | solution.py:726
  42.2 0.9 %copy-start = (f32[128,256]{1,0:T(8,128)S(1)}, f32[128,256]{1,0:T(8,128)}, u32[]{:S(2)}) copy-start(f32[128,256]{1,0:T(8,128)} %constant.113.clone.sub_ref) | copy-start | bytes 393220
  43.1 0.7 copy-start.1
  50.6 2.5 %collective-permute-start.18 = (bf16[4,8,2048]{2,1,0:T(8,128)(2,1)S(1)}, bf16[4,8,2048]{2,1,0:T(8,128)(2,1)S(1)}, u32[]{:S(2)}, u32[]{:S(2)}) collective-permute-start(bf16[4,8,2048]{2,1,0:T(8,128)(2,1)S(1)} %collective-permute-done.17), channel_id=1, source_target_pairs={{0,1},{1,0},{2,3},{3,2},{4,5},{5,4},{6,7},{7,6},{8,9},{9,8},{10,11... | collective-permute-start | bytes 393224 | tf_op jit(solution)/shard_map/ppermute | solution.py:726
  50.6 2.5 %collective-permute-start.16 = (bf16[4,8,2048]{2,1,0:T(8,128)(2,1)S(1)}, bf16[4,8,2048]{2,1,0:T(8,128)(2,1)S(1)}, u32[]{:S(2)}, u32[]{:S(2)}) collective-permute-start(bf16[4,8,2048]{2,1,0:T(8,128)(2,1)S(1)} %collective-permute-done.15), channel_id=1, source_target_pairs={{0,1},{1,0},{2,3},{3,2},{4,5},{5,4},{6,7},{7,6},{8,9},{9,8},{10,11... | collective-permute-start | bytes 393224 | tf_op jit(solution)/shard_map/ppermute | solution.py:726
  51.1 2.0 %collective-permute-start.19 = (bf16[4,8,2048]{2,1,0:T(8,128)(2,1)S(1)}, bf16[4,8,2048]{2,1,0:T(8,128)(2,1)S(1)}, u32[]{:S(2)}, u32[]{:S(2)}) collective-permute-start(bf16[4,8,2048]{2,1,0:T(8,128)(2,1)S(1)} %collective-permute-done.13), channel_id=1, source_target_pairs={{0,1},{1,0},{2,3},{3,2},{4,5},{5,4},{6,7},{7,6},{8,9},{9,8},{10,11... | collective-permute-start | bytes 393224 | tf_op jit(solution)/shard_map/ppermute | solution.py:726
